TPU v7x, 32 devices: a whole 2x2x4 slice. The times are simulated.
32 devices in a mesh: dp: 16 (over z, x, core), fsdp: 2 (over y).
Axes of the slice: x: 2, y: 2, z: 4, core: 2. Of those that a mesh axis runs over, the one named last changes fastest.
Arguments:
- waveform: float32 [256, 400], P(('dp', 'fsdp')), may hold values from -6 to 6
- lengths: int32 [256], P(('dp', 'fsdp')), may hold values from 200 to 400, as said below
- owner_of: int32 [256], P(('dp', 'fsdp')), may hold values from 0 to 15, as said below
- targets: float32 [256, 39], P(('dp', 'fsdp')), may hold values from -5 to 5
- first_weight: float32 [10, 512], replicated, may hold values from -2 to 2
- first_gain: float32 [512], replicated, may hold values from 0.1 to 1.9
- first_shift: float32 [512], replicated, may hold values from -3 to 3
- second_weight: bfloat16 [1536, 512], P('fsdp'), may hold values from -0.15625 to 0.15625
- second_gain: float32 [512], replicated, may hold values from 0.1 to 1.9
- second_shift: float32 [512], replicated, may hold values from -3 to 3
Outputs:
- logvar: float32 [256, 39], P(('dp', 'fsdp'))
- loss: float32 [], replicated
- grad_second_weight: float32 [1536, 512], P('fsdp')
- grad_first_weight: float32 [10, 512], replicated
- grad_first_gain: float32 [512], replicated
- grad_first_shift: float32 [512], replicated
- grad_second_gain: float32 [512], replicated
- grad_second_shift: float32 [512], replicated
Inputs may be any that keep to these rules, and one draw needn't show every extreme that they name: `lengths`: every draw has a row of length 400 and one of length 200. `owner_of`: rows read by the devices of one fsdp index go to owners of the same fsdp index. From one reader, each owner receives either no row or exactly 1 row; every owner receives exactly 8 rows.
All inputs are finite; a program needn't handle non-finite values.
Results may differ from a plain program's by a relative error of at most 0.0019.
Values may be sent and summed in bfloat16 or wider, within the bound.
No kernel may reach another device: no remote copies, remote signals or barrier semaphores. Data moves between devices by JAX's collectives and lax.ppermute only.
A program may use at most 64 MiB of HBM per device.

v0:
```python
import jax
import jax.numpy as jnp
from jax import lax
from jax.sharding import PartitionSpec as P

epsilon = 1e-05


def layer_norm(values, norm_gain, norm_shift):
    row_mean = jnp.mean(values, axis=-1, keepdims=True)
    centered = values - row_mean
    row_var = jnp.mean(centered * centered, axis=-1, keepdims=True)
    return centered * lax.rsqrt(row_var + epsilon) * norm_gain + norm_shift


def first_layer(waveform, first_weight, first_gain, first_shift):
    row_total, samples = waveform.shape
    frames = samples // 5 - 1
    blocks = waveform.reshape(row_total, samples // 5, 5)
    windows = jnp.concatenate([blocks[:, :frames], blocks[:, 1 : frames + 1]], axis=2)
    pre_norm = jnp.dot(
        windows.reshape(row_total * frames, 10),
        first_weight,
        precision=lax.Precision.HIGHEST,
        preferred_element_type=jnp.float32,
    )
    return jax.nn.gelu(layer_norm(pre_norm, first_gain, first_shift), approximate=False)


def make_patches(activated, row_total):
    channels = activated.shape[1]
    frames = activated.shape[0] // row_total
    later = (frames - 1) // 2
    shaped = activated.reshape(row_total, frames, channels)
    padded = jnp.concatenate([shaped, jnp.zeros((row_total, 1, channels), activated.dtype)], axis=1)
    paired = padded.reshape(row_total, later + 1, 2, channels)
    even_frames = paired[:, :, 0]
    odd_frames = paired[:, :, 1]
    joined = jnp.concatenate(
        [even_frames[:, :later], odd_frames[:, :later], even_frames[:, 1:]], axis=2
    )
    return joined.reshape(row_total * later, 3 * channels)


def patch_grad(grad_patches, row_total, frames):
    channels = grad_patches.shape[1] // 3
    later = grad_patches.shape[0] // row_total
    shaped = grad_patches.reshape(row_total, later, 3, channels)
    zero_frame = jnp.zeros((row_total, 1, channels), grad_patches.dtype)
    even_frames = jnp.concatenate([shaped[:, :, 0], zero_frame], axis=1) + jnp.concatenate(
        [zero_frame, shaped[:, :, 2]], axis=1
    )
    odd_frames = jnp.concatenate([shaped[:, :, 1], zero_frame], axis=1)
    paired = jnp.stack([even_frames, odd_frames], axis=2).reshape(
        row_total, 2 * later + 2, channels
    )
    return paired[:, :frames].reshape(row_total * frames, channels)


def frame_mask_of(row_lengths, later):
    first_valid = (row_lengths - 10) // 5 + 1
    second_valid = (first_valid - 3) // 2 + 1
    inside = jnp.arange(later, dtype=jnp.int32)[None, :] < second_valid[:, None]
    return inside.astype(jnp.float32).reshape(-1)


def head_loss(second_pre, second_gain, second_shift, target_flat, frame_mask):
    activated = jax.nn.gelu(layer_norm(second_pre, second_gain, second_shift), approximate=False)
    row_mean = jnp.mean(activated, axis=-1, keepdims=True)
    centered = activated - row_mean
    raw_logvar = jnp.log(jnp.mean(centered * centered, axis=-1) + epsilon)
    misfit = raw_logvar - target_flat
    return (jnp.sum(frame_mask * misfit * misfit), raw_logvar)


def per_device(
    waveform,
    lengths,
    owner_of,
    targets,
    first_weight,
    first_gain,
    first_shift,
    second_weight,
    second_gain,
    second_shift,
):
    peer_count = lax.axis_size("dp")
    row_total, samples = waveform.shape
    later = targets.shape[1]
    frames = samples // 5 - 1
    per_owner = max(1, 2 * row_total // peer_count)
    slot_count = peer_count * per_owner
    matches = (owner_of[:, None] == owner_of[None, :]).astype(jnp.int32)
    earlier = jnp.sum(jnp.tril(matches, -1), axis=1)
    slot_index = owner_of * per_owner + earlier
    placing = (slot_index[:, None] == jnp.arange(slot_count, dtype=jnp.int32)[None, :]).astype(
        jnp.float32
    )
    sent_wave = lax.dot_general(
        placing,
        waveform,
        (((0,), (0,)), ((), ())),
        precision=lax.Precision.HIGHEST,
        preferred_element_type=jnp.float32,
    )
    sent_length = jnp.dot(
        lengths.astype(jnp.float32),
        placing,
        precision=lax.Precision.HIGHEST,
        preferred_element_type=jnp.float32,
    )
    got_wave, got_length = (
        lax.all_to_all(
            sent_wave.reshape(peer_count, per_owner, samples),
            "dp",
            split_axis=0,
            concat_axis=0,
            tiled=True,
        ),
        lax.all_to_all(
            sent_length.reshape(peer_count, per_owner),
            "dp",
            split_axis=0,
            concat_axis=0,
            tiled=True,
        ),
    )
    got_wave = got_wave.reshape(slot_count, samples)
    got_length = got_length.reshape(slot_count)
    present = got_length > 0.5
    arrival = jnp.cumsum(present.astype(jnp.int32)) - 1
    picking = (
        present[None, :] & (arrival[None, :] == jnp.arange(row_total, dtype=jnp.int32)[:, None])
    ).astype(jnp.float32)
    owned_wave = jnp.dot(
        picking, got_wave, precision=lax.Precision.HIGHEST, preferred_element_type=jnp.float32
    )
    owned_length = jnp.dot(
        picking, got_length, precision=lax.Precision.HIGHEST, preferred_element_type=jnp.float32
    ).astype(jnp.int32)

    def first_part(weight_first, gain_first, shift_first):
        return first_layer(owned_wave, weight_first, gain_first, shift_first)

    activated, first_pull = jax.vjp(first_part, first_weight, first_gain, first_shift)
    rounded = activated.astype(jnp.bfloat16)
    patches = make_patches(rounded, row_total)
    columns = patches
    second_pre = jnp.dot(
        columns,
        lax.all_gather(second_weight, "fsdp", axis=0, tiled=True),
        preferred_element_type=jnp.float32,
    )
    frame_mask = frame_mask_of(owned_length, later)

    def head_part(pre_norm, gain_second, shift_second):
        return head_loss(pre_norm, gain_second, shift_second, targets.reshape(-1), frame_mask)

    loss_sum, head_pull, raw_logvar = jax.vjp(
        head_part, second_pre, second_gain, second_shift, has_aux=True
    )
    grad_pre, grad_gain_two, grad_shift_two = head_pull(jnp.ones_like(loss_sum))
    grad_pre = grad_pre.astype(jnp.bfloat16)
    columns = patches
    grad_shard = lax.psum_scatter(
        lax.dot_general(
            columns, grad_pre, (((0,), (0,)), ((), ())), preferred_element_type=jnp.float32
        ).astype(jnp.bfloat16),
        "fsdp",
        scatter_dimension=0,
        tiled=True,
    ).astype(jnp.float32)
    grad_weight_two = lax.psum(grad_shard, "dp")
    grad_patches = lax.dot_general(
        grad_pre,
        lax.all_gather(second_weight, "fsdp", axis=0, tiled=True),
        (((1,), (1,)), ((), ())),
        preferred_element_type=jnp.float32,
    )
    grad_act = patch_grad(grad_patches, row_total, frames)
    grad_weight_one, grad_gain_one, grad_shift_one = first_pull(grad_act)
    summed = lax.psum(
        (
            grad_weight_one,
            grad_gain_one,
            grad_shift_one,
            grad_gain_two,
            grad_shift_two,
            loss_sum,
            jnp.sum(frame_mask),
        ),
        ("dp", "fsdp"),
    )
    logvar = (raw_logvar * frame_mask).reshape(row_total, later)
    loss = summed[5] / summed[6]
    return (logvar, loss, grad_weight_two, summed[0], summed[1], summed[2], summed[3], summed[4])


def solution(mesh):
    placed = (
        P(("dp", "fsdp"), None),
        P(("dp", "fsdp")),
        P(("dp", "fsdp")),
        P(("dp", "fsdp"), None),
        P(),
        P(),
        P(),
        P("fsdp", None),
        P(),
        P(),
    )
    return jax.shard_map(
        per_device,
        mesh=mesh,
        in_specs=placed,
        out_specs=(P(("dp", "fsdp"), None), P(), P("fsdp", None), P(), P(), P(), P(), P()),
        check_vma=False,
    )
```

profile of v0, /device:TPU:0, one launch (start us, length us, event | category | flops | bytes accessed | tf_op | source)
XLA Modules:
  0.0 200.0 jit_solution(7417395136879654368)
XLA Ops:
  7.2 0.9 select_reduce_fusion
  8.1 0.7 add.108
  8.8 1.5 fusion.21
  10.3 7.4 %all-to-all-start = ((f32[16,1,1]{2,1,0:T(1,128)}), f32[16,1,1]{2,1,0:T(1,128)S(1)}, u32[]{:S(2)}, u32[]{:S(2)}) async-start(f32[16,1,1]{2,1,0:T(1,128)} %bitcast.21), calls=%async_computation | async-start | bytes 16384 | tf_op jit(solution)/shard_map/all_to_all | solution.py:121
  17.7 0.7 all-gather.2.cloned.1.call-update
  18.4 1.0 convolution_bitcast_fusion
  19.4 0.7 copy.79
  20.0 0.8 reshape.196
  20.8 3.2 %all-to-all-done = f32[16,1,1]{2,1,0:T(1,128)S(1)} async-done(((f32[16,1,1]{2,1,0:T(1,128)}), f32[16,1,1]{2,1,0:T(1,128)S(1)}, u32[]{:S(2)}, u32[]{:S(2)}) %all-to-all-start) | async-done | bytes 96 | tf_op jit(solution)/shard_map/all_to_all | solution.py:121
  24.0 3.5 %all-to-all-start.1 = ((f32[16,1,400]{2,1,0:T(1,128)}), f32[16,1,400]{2,1,0:T(1,128)S(1)}, u32[]{:S(2)}, u32[]{:S(2)}) async-start(f32[16,1,400]{2,1,0:T(1,128)} %copy.79), calls=%async_computation.1 | async-start | bytes 65536 | tf_op jit(solution)/shard_map/all_to_all | solution.py:114
  28.3 5.8 %all-to-all-done.1 = f32[16,1,400]{2,1,0:T(1,128)S(1)} async-done(((f32[16,1,400]{2,1,0:T(1,128)}), f32[16,1,400]{2,1,0:T(1,128)S(1)}, u32[]{:S(2)}, u32[]{:S(2)}) %all-to-all-start.1) | async-done | bytes 25632 | tf_op jit(solution)/shard_map/all_to_all | solution.py:114
  34.9 1.3 fusion.55
  36.5 4.4 %multiply_convert_fusion = (bf16[632,512]{1,0:T(8,128)(2,1)S(1)}, f32[632,512]{1,0:T(8,128)}) fusion(f32[632,512]{1,0:T(8,128)S(1)} %get-tuple-element.47, f32[512]{0:T(512)S(1)} %copy-done.6, f32[512]{0:T(512)S(1)} %copy-done.2, f32[632]{0:T(1024)S(1)} %fusion.26, f32[632]{0:T(1024)S(1)} %broadcast_multiply_fusion), kind=kLoop, calls=%fused_computation.10 | loop fusion | flops 22327296 | bytes 3244992 | tf_op jit(solution)/shard_map/convert_element_type | solution.py:147
  41.4 1.2 fusion.52
  43.3 5.4 %all-gather.2.cloned.1.call-done = bf16[1536,512]{1,0:T(8,128)(2,1)} async-done(((bf16[768,512]{1,0:T(8,128)(2,1)}), bf16[1536,512]{1,0:T(8,128)(2,1)}) %all-gather.2.cloned.1.call-update) | async-done | bytes 1572880 | tf_op jit(solution)/shard_map/all_gather | solution.py:152
  48.6 2.2 %fusion.56 = (f32[312]{0:T(512)S(1)}, f32[312,512]{1,0:T(8,128)S(1)}) fusion(bf16[312,1536]{1,0:T(8,128)(2,1)S(1)} %reshape.195, bf16[1536,512]{1,0:T(8,128)(2,1)} %all-gather.2.cloned.1.call-done), kind=kOutput, calls=%fused_computation.124 | convolution fusion | flops 490892992 | bytes 3171552 | tf_op jit(solution)/shard_map/dot_general | solution.py:150
  51.1 1.7 fusion.48
  53.3 0.8 multiply_reduce_fusion.3
  54.1 0.3 fusion.47
  54.4 0.8 copy-done.1
  55.3 2.2 %convolution_convert_fusion = bf16[1536,512]{1,0:T(8,128)(2,1)} fusion(bf16[312,1536]{1,0:T(8,128)(2,1)S(1)} %reshape.195, f32[312,512]{1,0:T(8,128)S(1)} %get-tuple-element.27, f32[312]{0:T(512)S(1)} %negate_multiply_fusion.3), kind=kOutput, calls=%fused_computation | convolution fusion | flops 491839488 | bytes 3171552 | tf_op jit(solution)/shard_map/dot_general | solution.py:167
  57.5 2.3 %fusion.45 = f32[312,1536]{1,0:T(8,128)S(1)} fusion(bf16[1536,512]{1,0:T(8,128)(2,1)} %all-gather.2.cloned.1.call-done, f32[312,512]{1,0:T(8,128)} %copy-done.1, f32[312]{0:T(512)S(1)} %negate_multiply_fusion.3), kind=kOutput, calls=%fused_computation.115 | convolution fusion | flops 491053056 | bytes 4130016 | tf_op jit(solution)/shard_map/dot_general | solution.py:175
  59.8 2.7 %reshape.197 = f32[8,39,3,512]{3,2,1,0:T(4,128)} reshape(f32[312,1536]{1,0:T(8,128)S(1)} %fusion.45) | data formatting | bytes 3833856 | tf_op jit(solution)/shard_map/reshape | solution.py:48
  62.6 5.6 %fusion.51 = (f32[8,39,1,512]{3,2,1,0:T(1,128)S(1)}, f32[8,39,1,512]{3,2,1,0:T(1,128)S(1)}, f32[8,39,1,512]{3,2,1,0:T(1,128)S(1)}) fusion(f32[8,39,3,512]{3,2,1,0:T(4,128)} %reshape.197), kind=kLoop, calls=%fused_computation.119 | loop fusion | bytes 3833856 | tf_op jit(solution)/shard_map/slice | solution.py:50
  68.8 0.8 copy.88
  69.6 1.2 reshape.199
  70.9 2.9 %multiply_reduce_fusion = (f32[512]{0:T(512)S(1)}, f32[632]{0:T(1024)S(1)}, f32[512]{0:T(512)S(1)}, f32[632,512]{1,0:T(8,128)S(1)}) fusion(f32[632,512]{1,0:T(8,128)S(1)} %get-tuple-element.47, f32[632]{0:T(1024)S(1)} %fusion.26, f32[632]{0:T(1024)S(1)} %broadcast_multiply_fusion, f32[512]{0:T(512)S(1)} %copy-done.2, f32[632,512]{1,0:T(8,128)} %reshape.199, ...), kind=kLoop, calls=%fused_computation.5 | loop fusion | flops 7440776 | bytes 5193120 | tf_op jit(solution)/shard_map/transpose(jvp())/reduce_sum | solution.py:13
  73.8 0.5 fusion.46
  74.5 1.3 convert_reduce_fusion
  75.8 0.8 fusion.1
  76.7 40.4 %all-reduce.4 = (f32[]{:T(128)}, f32[]{:T(128)}, f32[10,512]{1,0:T(8,128)}, f32[512]{0:T(512)}, f32[512]{0:T(512)}, /*index=5*/f32[512]{0:T(512)}, f32[512]{0:T(512)}) all-reduce(f32[]{:T(128)} %get-tuple-element.15, f32[]{:T(128)} %get-tuple-element.14, f32[10,512]{1,0:T(8,128)S(1)} %fusion.1, ...), channel_id=1, replica_groups=mesh['dp'=16,'fsdp'=2] {'dp','fsdp'}, use_global_device_ids=true, to_apply=%region_9.10 | all-reduce | flops 7170 | bytes 57360 | tf_op jit(solution)/shard_map/psum | solution.py:183
  118.4 73.7 %all-reduce.6 = f32[768,512]{1,0:T(8,128)} all-reduce(bf16[768,512]{1,0:T(8,128)(2,1)} %reduce-scatter.2.cloned.1.call-done), channel_id=1, replica_groups=mesh['dp'=16,'fsdp'=2] {'dp'}, use_global_device_ids=true, to_apply=%region_16.17 | all-reduce | flops 393216 | bytes 2359296 | tf_op jit(solution)/shard_map/psum | solution.py:174
  (63 shorter events, 4.6 us)
Async XLA Ops:
  7.2 27.7 %copy-start = (f32[10,512]{1,0:T(8,128)S(1)}, f32[10,512]{1,0:T(8,128)}, u32[]{:S(2)}) copy-start(f32[10,512]{1,0:T(8,128)} %param.14) | copy-start | bytes 61444
  10.3 13.8 %all-to-all-start = ((f32[16,1,1]{2,1,0:T(1,128)}), f32[16,1,1]{2,1,0:T(1,128)S(1)}, u32[]{:S(2)}, u32[]{:S(2)}) async-start(f32[16,1,1]{2,1,0:T(1,128)} %bitcast.21), calls=%async_computation | async-start | bytes 16384 | tf_op jit(solution)/shard_map/all_to_all | solution.py:121
  17.7 31.0 %all-gather.2.cloned.1.call-start = ((), (), s32[]{:S(2)}) async-start(), calls=%async_computation.3 | async-start | bytes 2359296 | tf_op jit(solution)/shard_map/all_gather | solution.py:152
  24.0 10.1 %all-to-all-start.1 = ((f32[16,1,400]{2,1,0:T(1,128)}), f32[16,1,400]{2,1,0:T(1,128)S(1)}, u32[]{:S(2)}, u32[]{:S(2)}) async-start(f32[16,1,400]{2,1,0:T(1,128)} %copy.79), calls=%async_computation.1 | async-start | bytes 65536 | tf_op jit(solution)/shard_map/all_to_all | solution.py:114
  27.5 90.8 %reduce-scatter.2.cloned.1.call-start = ((), (), s32[]{:S(2)}) async-start(), calls=%async_computation.4 | async-start | bytes 2359296 | tf_op jit(solution)/shard_map/reduce_scatter | solution.py:166
  34.8 1.6 copy-start.2
  34.8 1.6 copy-start.6
  43.3 7.8 %copy-start.3 = (f32[512]{0:T(512)S(1)}, f32[512]{0:T(512)}, u32[]{:S(2)}) copy-start(f32[512]{0:T(512)} %param.18) | copy-start | bytes 6148
  43.3 7.8 %copy-start.5 = (f32[512]{0:T(512)S(1)}, f32[512]{0:T(512)}, u32[]{:S(2)}) copy-start(f32[512]{0:T(512)} %param.19) | copy-start | bytes 6148
  54.4 0.9 copy-start.1
  73.8 0.7 copy-start.4
Sparse Core Ops, SparseCore 0:
  20.0 28.5 all-gather.1
  57.6 26.1 reduce-scatter.1
where the time goes:
time: 201 us; the launch traced here: 200 us
  blocking collectives  114 us (57%)
  between operations  16.8 us (8%)
  local copies, waits for them, and re-layouts  15.8 us (8%)
  other arithmetic  15.4 us (8%)
  waiting for transfers between devices  15.2 us (8%)
  matrix products  11.8 us (6%)
  starting transfers between devices  11 us (5%)
    psum x1, blocking collectives, per_device(): grad_weight_two = lax.psum(grad_shard, 'dp')  73.7 us
    psum x1, blocking collectives, per_device(): lax.psum((grad_weight_one, grad_gain_one, grad_shift_one, grad_gain_two,...  40.4 us
    all_to_all x1, starting transfers between devices, per_device(): lax.all_to_all(sent_length.reshape(peer_count, per_owner), 'dp', split_ax...  7.39 us
    all_to_all x1, waiting for transfers between devices, per_device(): lax.all_to_all(sent_wave.reshape(peer_count, per_owner, samples), 'dp', s...  5.85 us
    slice x2, local copies, waits for them, and re-layouts, patch_grad(): shaped[:, :, 0]  5.62 us
    all_gather x1, waiting for transfers between devices, per_device(): lax.all_gather(second_weight, 'fsdp', axis=0, tiled=True)  5.37 us
    convert_element_type x1, other arithmetic, per_device(): rounded = activated.astype(jnp.bfloat16)  4.39 us
  transfers between devices with their start and end apart: 4, of which 3 were waited for; matrix products, arithmetic and copies ran while one was open for 15% of the time, Pallas kernels for 0%

commit v1 on v0

v1 whole, which is shorter than its diff:
```python
import jax
import jax.numpy as jnp
from jax import lax
from jax.sharding import PartitionSpec as P

epsilon = 1e-05
HIGHEST = lax.Precision.HIGHEST


def power_of_two(value):
    return value & (value - 1) == 0


def digits_of(size):
    digits = []
    stride, left = 1, size
    if left > 1:
        digits.append((stride, 2))
        stride, left = 2, left // 2
    while left > 1:
        radix = 2 if left in (2, 8, 32, 128) else 4
        digits.append((stride, radix))
        stride, left = stride * radix, left // radix
    return digits


def swap(values, axis_name, mask):
    size = lax.axis_size(axis_name)
    return lax.ppermute(values, axis_name, [(i, i ^ mask) for i in range(size)])


def gather_relative(values, axis_name):
    size = lax.axis_size(axis_name)
    step = 1
    while step < size:
        values = jnp.concatenate([values, swap(values, axis_name, step)], axis=0)
        step *= 2
    return values


def sum_everywhere(values, axis_sizes):
    for axis_name, size in axis_sizes:
        step = 1
        while step < size:
            values = values + swap(values, axis_name, step)
            step *= 2
    return values


def part_of(values, index, count):
    size = values.shape[0] // count
    return lax.dynamic_slice_in_dim(values, index * size, size, axis=0)


def scatter_sum(values, axis_name, stride, radix, link_type):
    digit = lax.axis_index(axis_name) // stride % radix
    total = part_of(values, digit, radix).astype(jnp.float32)
    for other in range(1, radix):
        sent = part_of(values, digit ^ other, radix).astype(link_type)
        total = total + swap(sent, axis_name, other * stride).astype(jnp.float32)
    return total


def gather_parts(values, axis_name, stride, radix):
    digit = lax.axis_index(axis_name) // stride % radix
    parts = [values] + [swap(values, axis_name, other * stride) for other in range(1, radix)]
    size = values.shape[0]
    whole = jnp.zeros((radix * size,) + values.shape[1:], values.dtype)
    for other in range(radix):
        whole = lax.dynamic_update_slice_in_dim(whole, parts[other], (digit ^ other) * size, axis=0)
    return whole


def gather_weight(weight, cores):
    if lax.axis_size("fsdp") != 2 or not cores:
        return lax.all_gather(weight, "fsdp", axis=0, tiled=True)
    core = lax.axis_index("dp") % 2
    fetched = swap(part_of(weight, core, 2), "fsdp", 1)
    others = swap(fetched, "dp", 1)
    missing = jnp.where(
        core == 0,
        jnp.concatenate([fetched, others], axis=0),
        jnp.concatenate([others, fetched], axis=0),
    )
    return jnp.where(
        lax.axis_index("fsdp") == 0,
        jnp.concatenate([weight, missing], axis=0),
        jnp.concatenate([missing, weight], axis=0),
    )


def normalized(values):
    row_mean = jnp.mean(values, axis=-1, keepdims=True)
    centered = values - row_mean
    row_var = jnp.mean(centered * centered, axis=-1, keepdims=True)
    scale = lax.rsqrt(row_var + epsilon)
    return centered * scale, scale


def gelu_parts(values):
    share = 0.5 * lax.erfc(values * (-(0.5**0.5)))
    density = jnp.exp(-0.5 * values * values) * 0.3989422804014327
    return values * share, share + values * density


def norm_pull(grad_out, unit, scale, gain):
    grad_unit = grad_out * gain
    first = jnp.mean(grad_unit, axis=-1, keepdims=True)
    second = jnp.mean(grad_unit * unit, axis=-1, keepdims=True)
    grad_raw = scale * (grad_unit - first - unit * second)
    return grad_raw, jnp.sum(grad_out * unit, axis=0), jnp.sum(grad_out, axis=0)


def per_device(
    waveform,
    lengths,
    owner_of,
    targets,
    first_weight,
    first_gain,
    first_shift,
    second_weight,
    second_gain,
    second_shift,
):
    peers, groups = lax.axis_size("dp"), lax.axis_size("fsdp")
    rows, samples = waveform.shape
    later = targets.shape[1]
    frames = samples // 5 - 1
    channels = first_weight.shape[1]
    doubling = power_of_two(peers) and power_of_two(groups)
    me = lax.axis_index("dp")

    weight = gather_weight(second_weight, doubling and peers > 1)

    noted = jnp.concatenate([targets, owner_of.astype(jnp.float32)[:, None]], axis=1)
    if doubling:
        known = gather_relative(noted, "dp")
        reader = me ^ (jnp.arange(peers * rows, dtype=jnp.int32) // rows)
    else:
        known = lax.all_gather(noted, "dp", axis=0, tiled=True)
        reader = jnp.arange(peers * rows, dtype=jnp.int32) // rows
    known_owner = known[:, later].astype(jnp.int32)
    known_targets = known[:, :later]
    same_owner = owner_of[:, None] == known_owner[None, :]
    slot = jnp.sum((same_owner & (reader < me)[None, :]).astype(jnp.int32), axis=1)
    held = jnp.arange(peers * rows, dtype=jnp.int32) % rows
    wanted = (reader[None, :] == owner_of[:, None]) & (held[None, :] == slot[:, None])
    row_targets = lax.dot_general(
        known_targets,
        wanted.astype(jnp.float32),
        (((0,), (1,)), ((), ())),
        precision=HIGHEST,
        preferred_element_type=jnp.float32,
    ).reshape(later * rows, 1)
    mine = known_owner == me
    arrival = jnp.sum((mine[None, :] & (reader[None, :] < reader[:, None])).astype(jnp.int32), axis=1)
    picking = (
        mine[None, :] & (arrival[None, :] == jnp.arange(rows, dtype=jnp.int32)[:, None])
    ).astype(jnp.float32)

    blocks = waveform.reshape(rows, samples // 5, 5).transpose(1, 0, 2)
    windows = jnp.concatenate([blocks[:frames], blocks[1 : frames + 1]], axis=2)
    windows = windows.reshape(frames * rows, 10)
    first_pre = jnp.dot(
        windows, first_weight, precision=HIGHEST, preferred_element_type=jnp.float32
    )
    first_unit, first_scale = normalized(first_pre)
    activated, first_slope = gelu_parts(first_unit * first_gain + first_shift)
    rounded = activated.astype(jnp.bfloat16).reshape(frames, rows, channels)
    even, odd = rounded[0::2], rounded[1::2]
    patches = jnp.concatenate([even[:later], odd, even[1:]], axis=2)
    patches = patches.reshape(later * rows, 3 * channels)

    second_pre = jnp.dot(patches, weight, preferred_element_type=jnp.float32)
    second_unit, second_scale = normalized(second_pre)
    second_act, second_slope = gelu_parts(second_unit * second_gain + second_shift)
    act_mean = jnp.mean(second_act, axis=-1, keepdims=True)
    act_centered = second_act - act_mean
    act_var = jnp.mean(act_centered * act_centered, axis=-1, keepdims=True) + epsilon
    raw_logvar = jnp.log(act_var)
    first_valid = (lengths - 10) // 5 + 1
    second_valid = (first_valid - 3) // 2 + 1
    frame_mask = (
        jnp.arange(later, dtype=jnp.int32)[:, None] < second_valid[None, :]
    ).astype(jnp.float32)
    frame_mask = frame_mask.reshape(later * rows, 1)
    misfit = raw_logvar - row_targets
    loss_sum = jnp.sum(frame_mask * misfit * misfit)
    frame_count = jnp.sum(frame_mask)
    pull = frame_mask * misfit / act_var * (4.0 / channels)
    grad_pre, grad_gain_two, grad_shift_two = norm_pull(
        pull * act_centered * second_slope, second_unit, second_scale, second_gain
    )
    grad_pre = grad_pre.astype(jnp.bfloat16)

    def weight_gradient(columns):
        return lax.dot_general(
            patches, columns, (((0,), (0,)), ((), ())), preferred_element_type=jnp.float32
        )

    if doubling and peers > 1:
        half = channels // 2
        core = me % 2
        sent = weight_gradient(lax.dynamic_slice_in_dim(grad_pre, (1 - core) * half, half, 1))
        kept = weight_gradient(lax.dynamic_slice_in_dim(grad_pre, core * half, half, 1))
        total = kept + swap(sent, "dp", 1)
        stride = groups
        while stride > 1:
            stride //= 2
            total = scatter_sum(total, "fsdp", stride, 2, jnp.bfloat16)
        digits = digits_of(peers)[1:]
        for position, (stride, radix) in enumerate(digits):
            kind = jnp.bfloat16 if position == 0 and len(digits) > 1 else jnp.float32
            total = scatter_sum(total, "dp", stride, radix, kind)
        for stride, radix in digits[::-1]:
            total = gather_parts(total, "dp", stride, radix)
        other_half = swap(total, "dp", 1)
        grad_weight_two = jnp.where(
            core == 0,
            jnp.concatenate([total, other_half], axis=1),
            jnp.concatenate([other_half, total], axis=1),
        )
    else:
        grad_weight_two = lax.psum(
            lax.psum_scatter(
                weight_gradient(grad_pre), "fsdp", scatter_dimension=0, tiled=True
            ),
            "dp",
        )

    grad_patches = lax.dot_general(
        grad_pre, weight, (((1,), (1,)), ((), ())), preferred_element_type=jnp.float32
    ).reshape(later, rows, 3 * channels)
    zero_frame = jnp.zeros((1, rows, channels), jnp.float32)
    grad_even = jnp.concatenate([grad_patches[:, :, :channels], zero_frame], axis=0)
    grad_even = grad_even + jnp.concatenate([zero_frame, grad_patches[:, :, 2 * channels :]], axis=0)
    grad_odd = jnp.concatenate([grad_patches[:, :, channels : 2 * channels], zero_frame], axis=0)
    grad_act = jnp.stack([grad_even, grad_odd], axis=1).reshape(2 * later + 2, rows, channels)
    grad_act = grad_act[:frames].reshape(frames * rows, channels)
    grad_first, grad_gain_one, grad_shift_one = norm_pull(
        grad_act * first_slope, first_unit, first_scale, first_gain
    )
    grad_weight_one = lax.dot_general(
        windows,
        grad_first,
        (((0,), (0,)), ((), ())),
        precision=HIGHEST,
        preferred_element_type=jnp.float32,
    )
    scalars = jnp.concatenate(
        [loss_sum.reshape(1), frame_count.reshape(1), jnp.zeros((channels - 2,), jnp.float32)]
    )
    small = jnp.concatenate(
        [
            grad_weight_one,
            jnp.stack([grad_gain_one, grad_shift_one, grad_gain_two, grad_shift_two, scalars]),
            jnp.zeros((1, channels), jnp.float32),
        ],
        axis=0,
    )
    own_logvar = (raw_logvar * frame_mask).reshape(later, rows).T
    if doubling:
        small = sum_everywhere(small, (("dp", peers), ("fsdp", groups)))
        all_logvar = gather_relative(own_logvar, "dp")
    else:
        small = lax.psum(small, ("dp", "fsdp"))
        all_logvar = lax.all_gather(own_logvar, "dp", axis=0, tiled=True)
    logvar = jnp.dot(
        picking, all_logvar, precision=HIGHEST, preferred_element_type=jnp.float32
    )
    loss = small[14, 0] / small[14, 1]
    return (logvar, loss, grad_weight_two, small[:10], small[10], small[11], small[12], small[13])


def solution(mesh):
    placed = (
        P(("dp", "fsdp"), None),
        P(("dp", "fsdp")),
        P(("dp", "fsdp")),
        P(("dp", "fsdp"), None),
        P(),
        P(),
        P(),
        P("fsdp", None),
        P(),
        P(),
    )
    return jax.shard_map(
        per_device,
        mesh=mesh,
        in_specs=placed,
        out_specs=(P(("dp", "fsdp"), None), P(), P("fsdp", None), P(), P(), P(), P(), P()),
        check_vma=False,
    )
```

time: 201 us -> 111 us (0.55)
  blocking collectives: 114 us -> 0 us
  waiting for transfers between devices: 15.2 us -> 43 us
  starting transfers between devices: 11 us -> 30.1 us
  between operations: 16.8 us -> 3.83 us
  local copies, waits for them, and re-layouts: 15.8 us -> 9.55 us
  matrix products: 11.8 us -> 7.82 us
    psum x2 -> x0, blocking collectives: 114 us -> none  [the longest x1 73.7 us: per_device(): grad_weight_two = lax.psum(grad_shard, 'dp')]
    ppermute x0 -> x26, waiting for transfers between devices: none -> 43 us  [swap(): return lax.ppermute(values, axis_name, [(i, i ^ mask) for i in range(size)])]
    ppermute x0 -> x26, starting transfers between devices: none -> 30.1 us  [swap(): return lax.ppermute(values, axis_name, [(i, i ^ mask) for i in range(size)])]
    all_to_all x2 -> x0, starting transfers between devices: 10.9 us -> none  [the longest x1 7.39 us: per_device(): lax.all_to_all(sent_length.reshape(peer_count, per_owner), 'dp', split_ax...]
    all_to_all x2 -> x0, waiting for transfers between devices: 9.07 us -> none  [the longest x1 5.85 us: per_device(): lax.all_to_all(sent_wave.reshape(peer_count, per_owner, samples), 'dp', s...]
    slice x9 -> x7, local copies, waits for them, and re-layouts: 7.89 us -> 1.47 us  [the longest x1 0.6 us: per_device(): small[13]]
    all_gather x1 -> x0, waiting for transfers between devices: 5.37 us -> none  [per_device(): lax.all_gather(second_weight, 'fsdp', axis=0, tiled=True)]
    reshape x8 -> x3, local copies, waits for them, and re-layouts: 6.2 us -> 1.2 us  [the longest x1 0.87 us: per_device(): blocks = waveform.reshape(rows, samples // 5, 5).transpose(1, 0, 2)]
  transfers between devices with their start and end apart: 4 -> 26, of which waited for: 3 -> 14; matrix products, arithmetic and copies ran while one was open for 15% -> 19% of each run, Pallas kernels for 0% -> 0%
where the time goes in v1:
time: 111 us
  waiting for transfers between devices  43 us (39%)
  starting transfers between devices  30.1 us (27%)
  other arithmetic  16.6 us (15%)
  local copies, waits for them, and re-layouts  9.55 us (9%)
  matrix products  7.82 us (7%)
  between operations  3.83 us (3%)
    ppermute x26, waiting for transfers between devices, swap(): return lax.ppermute(values, axis_name, [(i, i ^ mask) for i in range(size)])  43 us
    ppermute x26, starting transfers between devices, swap(): return lax.ppermute(values, axis_name, [(i, i ^ mask) for i in range(size)])  30.1 us
    reshape x1, other arithmetic, per_device(): rounded = activated.astype(jnp.bfloat16).reshape(frames, rows, channels)  4.38 us
    unnamed x30, local copies, waits for them, and re-layouts  2.54 us
    dot_general x1, matrix products, per_device(): second_pre = jnp.dot(patches, weight, preferred_element_type=jnp.float32)  2.51 us
  transfers between devices with their start and end apart: 26, of which 14 were waited for; matrix products, arithmetic and copies ran while one was open for 19% of the time, Pallas kernels for 0%

profile of v1, /device:TPU:0, one launch (start us, length us, event | category | flops | bytes accessed | tf_op | source)
XLA Modules:
  0.0 110.9 jit_solution(15588179414196812089)
XLA Ops:
  2.6 1.8 %constant_dynamic-slice_fusion.3 = bf16[384,512]{1,0:T(8,128)(2,1)} fusion(bf16[768,512]{1,0:T(8,128)(2,1)} %param.17, s32[]{:T(128)S(6)} %select_n.136), kind=kLoop, calls=%fused_computation.113 | loop fusion | bytes 786436 | tf_op jit(solution)/shard_map/dynamic_slice | solution.py:52
  4.4 2.5 %collective-permute-start.4 = (bf16[384,512]{1,0:T(8,128)(2,1)}, bf16[384,512]{1,0:T(8,128)(2,1)}, u32[]{:S(2)}, u32[]{:S(2)}) collective-permute-start(bf16[384,512]{1,0:T(8,128)(2,1)} %constant_dynamic-slice_fusion.3), channel_id=1, source_target_pairs={{0,1},{1,0},{2,3},{3,2},{4,5},{5,4},{6,7},{7,6},{8,9},{9,8},{10,11... | collective-permute-start | bytes 1179656 | tf_op jit(solution)/shard_map/ppermute | solution.py:29
  8.8 1.3 %fusion.76 = (f32[632]{0:T(1024)S(1)}, f32[632,512]{1,0:T(8,128)S(1)}) fusion(f32[632,10]{0,1:T(8,128)S(1)} %reshape.214, f32[10,512]{1,0:T(8,128)S(1)} %copy-done), kind=kOutput, calls=%fused_computation.170 | convolution fusion | flops 39153032 | bytes 1342624 | tf_op jit(solution)/shard_map/dot_general | solution.py:165
  10.5 4.4 %fusion.19 = (bf16[79,8,512]{2,1,0:T(8,128)(2,1)S(1)}, f32[632,512]{1,0:T(8,128)}) fusion(f32[512]{0:T(512)S(1)} %copy-done.12, f32[512]{0:T(512)S(1)} %copy-done.10, f32[632]{0:T(1024)S(1)} %add_rsqrt_fusion, f32[632,512]{1,0:T(8,128)S(1)} %get-tuple-element.46, f32[632]{0:T(1024)S(1)} %broadcast_multiply_fusion.2), kind=kLoop, calls=%fused_computation.49 | loop fusion | flops 22003712 | bytes 3244992 | tf_op jit(solution)/shard_map/reshape | solution.py:170
  15.6 1.5 %collective-permute-start.1 = (f32[16,40]{1,0:T(8,128)S(1)}, f32[16,40]{1,0:T(8,128)S(1)}, u32[]{:S(2)}, u32[]{:S(2)}) collective-permute-start(f32[16,40]{1,0:T(8,128)S(1)} %pad_maximum_fusion.6), channel_id=1, source_target_pairs={{0,4},{2,6},{4,0},{6,2},{8,12},{10,14},{12,8},{14,10},{16,20},{18,... | collective-permute-start | bytes 7688 | tf_op jit(solution)/shard_map/ppermute | solution.py:29
  17.2 2.1 %collective-permute-done.1 = f32[16,40]{1,0:T(8,128)S(1)} collective-permute-done((f32[16,40]{1,0:T(8,128)S(1)}, f32[16,40]{1,0:T(8,128)S(1)}, u32[]{:S(2)}, u32[]{:S(2)}) %collective-permute-start.1) | collective-permute-done | bytes 2592 | tf_op jit(solution)/shard_map/ppermute | solution.py:29
  19.4 1.6 %collective-permute-start.2 = (f32[32,40]{1,0:T(8,128)S(1)}, f32[32,40]{1,0:T(8,128)S(1)}, u32[]{:S(2)}, u32[]{:S(2)}) collective-permute-start(f32[32,40]{1,0:T(8,128)S(1)} %pad_maximum_fusion.4), channel_id=1, source_target_pairs={{0,8},{2,10},{4,12},{6,14},{8,0},{10,2},{12,4},{14,6},{16,24},{18,... | collective-permute-start | bytes 15368 | tf_op jit(solution)/shard_map/ppermute | solution.py:29
  20.9 2.2 %collective-permute-done.2 = f32[32,40]{1,0:T(8,128)S(1)} collective-permute-done((f32[32,40]{1,0:T(8,128)S(1)}, f32[32,40]{1,0:T(8,128)S(1)}, u32[]{:S(2)}, u32[]{:S(2)}) %collective-permute-start.2) | collective-permute-done | bytes 5152 | tf_op jit(solution)/shard_map/ppermute | solution.py:29
  23.2 2.6 %collective-permute-start.3 = (f32[64,40]{1,0:T(8,128)S(1)}, f32[64,40]{1,0:T(8,128)S(1)}, u32[]{:S(2)}, u32[]{:S(2)}) collective-permute-start(f32[64,40]{1,0:T(8,128)S(1)} %pad_maximum_fusion.2), channel_id=1, source_target_pairs={{0,16},{2,18},{4,20},{6,22},{8,24},{10,26},{12,28},{14,30},{16,0},... | collective-permute-start | bytes 30728 | tf_op jit(solution)/shard_map/ppermute | solution.py:29
  26.5 1.5 %collective-permute-done.3 = f32[64,40]{1,0:T(8,128)S(1)} collective-permute-done((f32[64,40]{1,0:T(8,128)S(1)}, f32[64,40]{1,0:T(8,128)S(1)}, u32[]{:S(2)}, u32[]{:S(2)}) %collective-permute-start.3) | collective-permute-done | bytes 10272 | tf_op jit(solution)/shard_map/ppermute | solution.py:29
  28.8 1.3 %collective-permute-done.5 = bf16[384,512]{1,0:T(8,128)(2,1)S(1)} collective-permute-done((bf16[384,512]{1,0:T(8,128)(2,1)}, bf16[384,512]{1,0:T(8,128)(2,1)S(1)}, u32[]{:S(2)}, u32[]{:S(2)}) %collective-permute-start.5) | collective-permute-done | bytes 393248 | tf_op jit(solution)/shard_map/ppermute | solution.py:29
  30.2 1.4 %maximum_select_fusion.2 = bf16[768,512]{1,0:T(8,128)(2,1)S(1)} fusion(bf16[384,512]{1,0:T(8,128)(2,1)S(1)} %collective-permute-done.5, bf16[384,512]{1,0:T(8,128)(2,1)} %collective-permute-done.4, pred[]{:T(512)S(6)} %eq.83), kind=kLoop, calls=%fused_computation.44 | loop fusion | flops 3538944 | bytes 1572865 | tf_op jit(solution)/shard_map/jit(_where)/select_n | solution.py:80
  31.6 2.5 %fusion.77 = (f32[312]{0:T(512)S(1)}, f32[312,512]{1,0:T(8,128)S(1)}) fusion(bf16[768,512]{1,0:T(8,128)(2,1)S(1)} %maximum_select_fusion.2, bf16[768,512]{1,0:T(8,128)(2,1)} %param.17, pred[]{:T(512)S(6)} %eq.82, bf16[39,8,512]{2,1,0:T(8,128)(2,1)S(1)} %get-tuple-element.33, bf16[39,8,512]{2,1,0:T(8,128)(2,1)S(1)} %slice.62, ...), kind=kOutput, calls=%fused_computation.171 | convolution fusion | flops 500846272 | bytes 3171553 | tf_op jit(solution)/shard_map/dot_general | solution.py:175
  34.4 1.7 %fusion.38 = (f32[312]{0:T(512)S(1)}, f32[312,512]{1,0:T(8,128)S(1)}) fusion(f32[512]{0:T(512)S(1)} %copy-done.11, f32[512]{0:T(512)S(1)} %copy-done.9, f32[312]{0:T(512)S(1)} %add_rsqrt_fusion.1, f32[312,512]{1,0:T(8,128)S(1)} %get-tuple-element.48, f32[312]{0:T(512)S(1)} %broadcast_multiply_fusion.6), kind=kLoop, calls=%fused_computation.83 | loop fusion | flops 10862280 | bytes 1285792 | tf_op jit(solution)/shard_map/reduce_sum | solution.py:178
  44.9 11.0 %collective-permute-done.16 = bf16[768,256]{1,0:T(8,128)(2,1)S(1)} collective-permute-done((bf16[768,256]{1,0:T(8,128)(2,1)S(1)}, bf16[768,256]{1,0:T(8,128)(2,1)S(1)}, u32[]{:S(2)}, u32[]{:S(2)}) %collective-permute-start.16) | collective-permute-done | bytes 393248 | tf_op jit(solution)/shard_map/ppermute | solution.py:29
  55.9 1.6 %collective-permute-start.17 = (bf16[384,256]{1,0:T(8,128)(2,1)S(1)}, bf16[384,256]{1,0:T(8,128)(2,1)S(1)}, u32[]{:S(2)}, u32[]{:S(2)}) collective-permute-start(bf16[384,256]{1,0:T(8,128)(2,1)S(1)} %dynamic-slice_convert_fusion.1), channel_id=1, source_target_pairs={{0,4},{2,6},{4,0},{6,2},{8,12},{10,14},{12,8},{14,10},{16,20},{18,... | collective-permute-start | bytes 589832 | tf_op jit(solution)/shard_map/ppermute | solution.py:29
  58.6 3.5 %collective-permute-done.17 = bf16[384,256]{1,0:T(8,128)(2,1)S(1)} collective-permute-done((bf16[384,256]{1,0:T(8,128)(2,1)S(1)}, bf16[384,256]{1,0:T(8,128)(2,1)S(1)}, u32[]{:S(2)}, u32[]{:S(2)}) %collective-permute-start.17) | collective-permute-done | bytes 196640 | tf_op jit(solution)/shard_map/ppermute | solution.py:29
  62.2 3.9 %collective-permute-start.20 = (f32[96,256]{1,0:T(8,128)S(1)}, f32[96,256]{1,0:T(8,128)S(1)}, u32[]{:S(2)}, u32[]{:S(2)}) collective-permute-start(f32[96,256]{1,0:T(8,128)S(1)} %get-tuple-element.30), channel_id=1, source_target_pairs={{0,24},{2,26},{4,28},{6,30},{8,16},{10,18},{12,20},{14,22},{16,8},... | collective-permute-start | bytes 294920 | tf_op jit(solution)/shard_map/ppermute | solution.py:29
  66.7 1.4 %pad_maximum_fusion.9 = f32[512]{0:T(512)S(1)} fusion(f32[510]{0:T(512)S(1)} %broadcast_in_dim.11, f32[1]{0:T(128)} %bitcast.16, f32[1]{0:T(128)} %bitcast.15), kind=kLoop, calls=%fused_computation.127 | loop fusion | flops 1024 | bytes 4096 | tf_op jit(solution)/shard_map/concatenate | solution.py:251
  68.9 4.0 %collective-permute-done.19 = f32[96,256]{1,0:T(8,128)S(1)} collective-permute-done((f32[96,256]{1,0:T(8,128)S(1)}, f32[96,256]{1,0:T(8,128)S(1)}, u32[]{:S(2)}, u32[]{:S(2)}) %collective-permute-start.19) | collective-permute-done | bytes 98336 | tf_op jit(solution)/shard_map/ppermute | solution.py:29
  73.6 1.5 %collective-permute-start.7 = (f32[16,39]{1,0:T(8,128)S(1)}, f32[16,39]{1,0:T(8,128)S(1)}, u32[]{:S(2)}, u32[]{:S(2)}) collective-permute-start(f32[16,39]{1,0:T(8,128)S(1)} %pad_maximum_fusion.7), channel_id=1, source_target_pairs={{0,4},{2,6},{4,0},{6,2},{8,12},{10,14},{12,8},{14,10},{16,20},{18,... | collective-permute-start | bytes 7496 | tf_op jit(solution)/shard_map/ppermute | solution.py:29
  75.1 2.6 %collective-permute-start.22 = (f32[96,256]{1,0:T(8,128)S(1)}, f32[96,256]{1,0:T(8,128)S(1)}, u32[]{:S(2)}, u32[]{:S(2)}) collective-permute-start(f32[96,256]{1,0:T(8,128)S(1)} %get-tuple-element.19), channel_id=1, source_target_pairs={{0,16},{2,18},{4,20},{6,22},{8,24},{10,26},{12,28},{14,30},{16,0},... | collective-permute-start | bytes 294920 | tf_op jit(solution)/shard_map/ppermute | solution.py:29
  78.9 5.5 %collective-permute-done.22 = f32[96,256]{1,0:T(8,128)S(1)} collective-permute-done((f32[96,256]{1,0:T(8,128)S(1)}, f32[96,256]{1,0:T(8,128)S(1)}, u32[]{:S(2)}, u32[]{:S(2)}) %collective-permute-start.22) | collective-permute-done | bytes 98336 | tf_op jit(solution)/shard_map/ppermute | solution.py:29
  85.0 1.6 %collective-permute-start.11 = (f32[16,512]{1,0:T(8,128)S(1)}, f32[16,512]{1,0:T(8,128)S(1)}, u32[]{:S(2)}, u32[]{:S(2)}) collective-permute-start(f32[16,512]{1,0:T(8,128)S(1)} %add.201), channel_id=1, source_target_pairs={{0,4},{2,6},{4,0},{6,2},{8,12},{10,14},{12,8},{14,10},{16,20},{18,... | collective-permute-start | bytes 98312 | tf_op jit(solution)/shard_map/ppermute | solution.py:29
  86.6 1.6 %collective-permute-start.8 = (f32[32,39]{1,0:T(8,128)S(1)}, f32[32,39]{1,0:T(8,128)S(1)}, u32[]{:S(2)}, u32[]{:S(2)}) collective-permute-start(f32[32,39]{1,0:T(8,128)S(1)} %pad_maximum_fusion.5), channel_id=1, source_target_pairs={{0,8},{2,10},{4,12},{6,14},{8,0},{10,2},{12,4},{14,6},{16,24},{18,... | collective-permute-start | bytes 14984 | tf_op jit(solution)/shard_map/ppermute | solution.py:29
  88.3 4.3 %collective-permute-done.11 = f32[16,512]{1,0:T(8,128)S(1)} collective-permute-done((f32[16,512]{1,0:T(8,128)S(1)}, f32[16,512]{1,0:T(8,128)S(1)}, u32[]{:S(2)}, u32[]{:S(2)}) %collective-permute-start.11) | collective-permute-done | bytes 32800 | tf_op jit(solution)/shard_map/ppermute | solution.py:29
  92.6 2.6 %collective-permute-start.12 = (f32[16,512]{1,0:T(8,128)S(1)}, f32[16,512]{1,0:T(8,128)S(1)}, u32[]{:S(2)}, u32[]{:S(2)}) collective-permute-start(f32[16,512]{1,0:T(8,128)S(1)} %add.202), channel_id=1, source_target_pairs={{0,8},{2,10},{4,12},{6,14},{8,0},{10,2},{12,4},{14,6},{16,24},{18,... | collective-permute-start | bytes 98312 | tf_op jit(solution)/shard_map/ppermute | solution.py:29
  95.6 1.6 %collective-permute-done.12 = f32[16,512]{1,0:T(8,128)S(1)} collective-permute-done((f32[16,512]{1,0:T(8,128)S(1)}, f32[16,512]{1,0:T(8,128)S(1)}, u32[]{:S(2)}, u32[]{:S(2)}) %collective-permute-start.12) | collective-permute-done | bytes 32800 | tf_op jit(solution)/shard_map/ppermute | solution.py:29
  97.1 1.4 %collective-permute-start.13 = (f32[16,512]{1,0:T(8,128)S(1)}, f32[16,512]{1,0:T(8,128)S(1)}, u32[]{:S(2)}, u32[]{:S(2)}) collective-permute-start(f32[16,512]{1,0:T(8,128)S(1)} %add.203), channel_id=1, source_target_pairs={{0,16},{2,18},{4,20},{6,22},{8,24},{10,26},{12,28},{14,30},{16,0},... | collective-permute-start | bytes 98312 | tf_op jit(solution)/shard_map/ppermute | solution.py:29
  99.1 2.0 %collective-permute-done.9 = f32[64,39]{1,0:T(8,128)S(1)} collective-permute-done((f32[64,39]{1,0:T(8,128)S(1)}, f32[64,39]{1,0:T(8,128)S(1)}, u32[]{:S(2)}, u32[]{:S(2)}) %collective-permute-start.9) | collective-permute-done | bytes 10016 | tf_op jit(solution)/shard_map/ppermute | solution.py:29
  103.2 2.7 %collective-permute-done.14 = f32[16,512]{1,0:T(8,128)S(1)} collective-permute-done((f32[16,512]{1,0:T(8,128)S(1)}, f32[16,512]{1,0:T(8,128)S(1)}, u32[]{:S(2)}, u32[]{:S(2)}) %collective-permute-start.14) | collective-permute-done | bytes 32800 | tf_op jit(solution)/shard_map/ppermute | solution.py:29
  108.4 1.4 %maximum_select_fusion.1 = f32[768,512]{1,0:T(8,128)} fusion(f32[768,256]{1,0:T(8,128)S(1)} %collective-permute-done.25, f32[768,256]{1,0:T(8,128)S(1)} %constant_dynamic-update-slice_fusion, pred[]{:T(512)S(6)} %eq.83), kind=kLoop, calls=%fused_computation.5 | loop fusion | flops 1179648 | bytes 3145729 | tf_op jit(solution)/shard_map/jit(_where)/select_n | solution.py:219
  (152 shorter events, 24.8 us)
Async XLA Ops:
  0.6 8.2 %copy-start = (f32[10,512]{1,0:T(8,128)S(1)}, f32[10,512]{1,0:T(8,128)}, u32[]{:S(2)}) copy-start(f32[10,512]{1,0:T(8,128)} %param.14) | copy-start | bytes 61444
  2.2 13.4 %collective-permute-start = (f32[8,40]{1,0:T(8,128)S(1)}, f32[8,40]{1,0:T(8,128)S(1)}, u32[]{:S(2)}, u32[]{:S(2)}) collective-permute-start(f32[8,40]{1,0:T(8,128)S(1)} %pad_maximum_fusion.8), channel_id=1, source_target_pairs={{0,2},{2,0},{4,6},{6,4},{8,10},{10,8},{12,14},{14,12},{16,18},{18,... | collective-permute-start | bytes 3848 | tf_op jit(solution)/shard_map/ppermute | solution.py:29
  4.4 23.7 %collective-permute-start.4 = (bf16[384,512]{1,0:T(8,128)(2,1)}, bf16[384,512]{1,0:T(8,128)(2,1)}, u32[]{:S(2)}, u32[]{:S(2)}) collective-permute-start(bf16[384,512]{1,0:T(8,128)(2,1)} %constant_dynamic-slice_fusion.3), channel_id=1, source_target_pairs={{0,1},{1,0},{2,3},{3,2},{4,5},{5,4},{6,7},{7,6},{8,9},{9,8},{10,11... | collective-permute-start | bytes 1179656 | tf_op jit(solution)/shard_map/ppermute | solution.py:29
  14.9 13.4 %copy-start.13 = (s32[8]{0:T(128)S(1)}, s32[8]{0:T(128)}, u32[]{:S(2)}) copy-start(s32[8]{0:T(128)} %param.12) | copy-start | bytes 100
  15.6 3.7 %collective-permute-start.1 = (f32[16,40]{1,0:T(8,128)S(1)}, f32[16,40]{1,0:T(8,128)S(1)}, u32[]{:S(2)}, u32[]{:S(2)}) collective-permute-start(f32[16,40]{1,0:T(8,128)S(1)} %pad_maximum_fusion.6), channel_id=1, source_target_pairs={{0,4},{2,6},{4,0},{6,2},{8,12},{10,14},{12,8},{14,10},{16,20},{18,... | collective-permute-start | bytes 7688 | tf_op jit(solution)/shard_map/ppermute | solution.py:29
  19.4 3.7 %collective-permute-start.2 = (f32[32,40]{1,0:T(8,128)S(1)}, f32[32,40]{1,0:T(8,128)S(1)}, u32[]{:S(2)}, u32[]{:S(2)}) collective-permute-start(f32[32,40]{1,0:T(8,128)S(1)} %pad_maximum_fusion.4), channel_id=1, source_target_pairs={{0,8},{2,10},{4,12},{6,14},{8,0},{10,2},{12,4},{14,6},{16,24},{18,... | collective-permute-start | bytes 15368 | tf_op jit(solution)/shard_map/ppermute | solution.py:29
  23.2 4.8 %collective-permute-start.3 = (f32[64,40]{1,0:T(8,128)S(1)}, f32[64,40]{1,0:T(8,128)S(1)}, u32[]{:S(2)}, u32[]{:S(2)}) collective-permute-start(f32[64,40]{1,0:T(8,128)S(1)} %pad_maximum_fusion.2), channel_id=1, source_target_pairs={{0,16},{2,18},{4,20},{6,22},{8,24},{10,26},{12,28},{14,30},{16,0},... | collective-permute-start | bytes 30728 | tf_op jit(solution)/shard_map/ppermute | solution.py:29
  25.9 8.2 %copy-start.2 = (bf16[39,8,512]{2,1,0:T(8,128)(2,1)}, bf16[39,8,512]{2,1,0:T(8,128)(2,1)S(1)}, u32[]{:S(2)}) copy-start(bf16[39,8,512]{2,1,0:T(8,128)(2,1)S(1)} %slice.62) | copy-start | bytes 958468
  28.2 2.0 %collective-permute-start.5 = (bf16[384,512]{1,0:T(8,128)(2,1)}, bf16[384,512]{1,0:T(8,128)(2,1)S(1)}, u32[]{:S(2)}, u32[]{:S(2)}) collective-permute-start(bf16[384,512]{1,0:T(8,128)(2,1)} %collective-permute-done.4), channel_id=1, source_target_pairs={{0,2},{2,0},{4,6},{6,4},{8,10},{10,8},{12,14},{14,12},{16,18},{18,... | collective-permute-start | bytes 1179656 | tf_op jit(solution)/shard_map/ppermute | solution.py:29
  31.5 2.8 %copy-start.9 = (f32[512]{0:T(512)S(1)}, f32[512]{0:T(512)}, u32[]{:S(2)}) copy-start(f32[512]{0:T(512)} %param.18) | copy-start | bytes 6148
  31.6 2.8 %copy-start.11 = (f32[512]{0:T(512)S(1)}, f32[512]{0:T(512)}, u32[]{:S(2)}) copy-start(f32[512]{0:T(512)} %param.19) | copy-start | bytes 6148
  38.9 5.0 %collective-permute-start.15 = (f32[1536,256]{1,0:T(8,128)S(1)}, f32[1536,256]{1,0:T(8,128)S(1)}, u32[]{:S(2)}, u32[]{:S(2)}) collective-permute-start(f32[1536,256]{1,0:T(8,128)S(1)} %fusion.40), channel_id=1, source_target_pairs={{0,2},{2,0},{4,6},{6,4},{8,10},{10,8},{12,14},{14,12},{16,18},{18,... | collective-permute-start | bytes 4718600 | tf_op jit(solution)/shard_map/ppermute | solution.py:29
  39.8 33.8 %collective-permute-start.6 = (f32[8,39]{1,0:T(8,128)S(1)}, f32[8,39]{1,0:T(8,128)S(1)}, u32[]{:S(2)}, u32[]{:S(2)}) collective-permute-start(f32[8,39]{1,0:T(8,128)S(1)} %get-tuple-element.42), channel_id=1, source_target_pairs={{0,2},{2,0},{4,6},{6,4},{8,10},{10,8},{12,14},{14,12},{16,18},{18,... | collective-permute-start | bytes 3752 | tf_op jit(solution)/shard_map/ppermute | solution.py:29
  44.6 11.2 %collective-permute-start.16 = (bf16[768,256]{1,0:T(8,128)(2,1)S(1)}, bf16[768,256]{1,0:T(8,128)(2,1)S(1)}, u32[]{:S(2)}, u32[]{:S(2)}) collective-permute-start(bf16[768,256]{1,0:T(8,128)(2,1)S(1)} %dynamic-slice_convert_fusion), channel_id=1, source_target_pairs={{0,1},{1,0},{2,3},{3,2},{4,5},{5,4},{6,7},{7,6},{8,9},{9,8},{10,11... | collective-permute-start | bytes 1179656 | tf_op jit(solution)/shard_map/ppermute | solution.py:29
  55.9 6.2 %collective-permute-start.17 = (bf16[384,256]{1,0:T(8,128)(2,1)S(1)}, bf16[384,256]{1,0:T(8,128)(2,1)S(1)}, u32[]{:S(2)}, u32[]{:S(2)}) collective-permute-start(bf16[384,256]{1,0:T(8,128)(2,1)S(1)} %dynamic-slice_convert_fusion.1), channel_id=1, source_target_pairs={{0,4},{2,6},{4,0},{6,2},{8,12},{10,14},{12,8},{14,10},{16,20},{18,... | collective-permute-start | bytes 589832 | tf_op jit(solution)/shard_map/ppermute | solution.py:29
  62.2 6.7 %collective-permute-start.20 = (f32[96,256]{1,0:T(8,128)S(1)}, f32[96,256]{1,0:T(8,128)S(1)}, u32[]{:S(2)}, u32[]{:S(2)}) collective-permute-start(f32[96,256]{1,0:T(8,128)S(1)} %get-tuple-element.30), channel_id=1, source_target_pairs={{0,24},{2,26},{4,28},{6,30},{8,16},{10,18},{12,20},{14,22},{16,8},... | collective-permute-start | bytes 294920 | tf_op jit(solution)/shard_map/ppermute | solution.py:29
  66.1 6.8 %collective-permute-start.19 = (f32[96,256]{1,0:T(8,128)S(1)}, f32[96,256]{1,0:T(8,128)S(1)}, u32[]{:S(2)}, u32[]{:S(2)}) collective-permute-start(f32[96,256]{1,0:T(8,128)S(1)} %get-tuple-element.31), channel_id=1, source_target_pairs={{0,16},{2,18},{4,20},{6,22},{8,24},{10,26},{12,28},{14,30},{16,0},... | collective-permute-start | bytes 294920 | tf_op jit(solution)/shard_map/ppermute | solution.py:29
  66.1 6.8 %collective-permute-start.18 = (f32[96,256]{1,0:T(8,128)S(1)}, f32[96,256]{1,0:T(8,128)S(1)}, u32[]{:S(2)}, u32[]{:S(2)}) collective-permute-start(f32[96,256]{1,0:T(8,128)S(1)} %get-tuple-element.29), channel_id=1, source_target_pairs={{0,8},{2,10},{4,12},{6,14},{8,0},{10,2},{12,4},{14,6},{16,24},{18,... | collective-permute-start | bytes 294920 | tf_op jit(solution)/shard_map/ppermute | solution.py:29
  68.1 16.8 %collective-permute-start.10 = (f32[16,512]{1,0:T(8,128)S(1)}, f32[16,512]{1,0:T(8,128)S(1)}, u32[]{:S(2)}, u32[]{:S(2)}) collective-permute-start(f32[16,512]{1,0:T(8,128)S(1)} %concatenate.91), channel_id=1, source_target_pairs={{0,2},{2,0},{4,6},{6,4},{8,10},{10,8},{12,14},{14,12},{16,18},{18,... | collective-permute-start | bytes 98312 | tf_op jit(solution)/shard_map/ppermute | solution.py:29
  72.9 6.0 %collective-permute-start.21 = (f32[96,256]{1,0:T(8,128)S(1)}, f32[96,256]{1,0:T(8,128)S(1)}, u32[]{:S(2)}, u32[]{:S(2)}) collective-permute-start(f32[96,256]{1,0:T(8,128)S(1)} %get-tuple-element.19), channel_id=1, source_target_pairs={{0,8},{2,10},{4,12},{6,14},{8,0},{10,2},{12,4},{14,6},{16,24},{18,... | collective-permute-start | bytes 294920 | tf_op jit(solution)/shard_map/ppermute | solution.py:29
  73.6 13.0 %collective-permute-start.7 = (f32[16,39]{1,0:T(8,128)S(1)}, f32[16,39]{1,0:T(8,128)S(1)}, u32[]{:S(2)}, u32[]{:S(2)}) collective-permute-start(f32[16,39]{1,0:T(8,128)S(1)} %pad_maximum_fusion.7), channel_id=1, source_target_pairs={{0,4},{2,6},{4,0},{6,2},{8,12},{10,14},{12,8},{14,10},{16,20},{18,... | collective-permute-start | bytes 7496 | tf_op jit(solution)/shard_map/ppermute | solution.py:29
  75.1 9.3 %collective-permute-start.22 = (f32[96,256]{1,0:T(8,128)S(1)}, f32[96,256]{1,0:T(8,128)S(1)}, u32[]{:S(2)}, u32[]{:S(2)}) collective-permute-start(f32[96,256]{1,0:T(8,128)S(1)} %get-tuple-element.19), channel_id=1, source_target_pairs={{0,16},{2,18},{4,20},{6,22},{8,24},{10,26},{12,28},{14,30},{16,0},... | collective-permute-start | bytes 294920 | tf_op jit(solution)/shard_map/ppermute | solution.py:29
  77.7 6.7 %collective-permute-start.23 = (f32[96,256]{1,0:T(8,128)S(1)}, f32[96,256]{1,0:T(8,128)S(1)}, u32[]{:S(2)}, u32[]{:S(2)}) collective-permute-start(f32[96,256]{1,0:T(8,128)S(1)} %get-tuple-element.19), channel_id=1, source_target_pairs={{0,24},{2,26},{4,28},{6,30},{8,16},{10,18},{12,20},{14,22},{16,8},... | collective-permute-start | bytes 294920 | tf_op jit(solution)/shard_map/ppermute | solution.py:29
  84.4 10.9 %collective-permute-start.24 = (f32[384,256]{1,0:T(8,128)S(1)}, f32[384,256]{1,0:T(8,128)S(1)}, u32[]{:S(2)}, u32[]{:S(2)}) collective-permute-start(f32[384,256]{1,0:T(8,128)S(1)} %constant_dynamic-update-slice_fusion.2), channel_id=1, source_target_pairs={{0,4},{2,6},{4,0},{6,2},{8,12},{10,14},{12,8},{14,10},{16,20},{18,... | collective-permute-start | bytes 1179656 | tf_op jit(solution)/shard_map/ppermute | solution.py:29
  85.0 7.6 %collective-permute-start.11 = (f32[16,512]{1,0:T(8,128)S(1)}, f32[16,512]{1,0:T(8,128)S(1)}, u32[]{:S(2)}, u32[]{:S(2)}) collective-permute-start(f32[16,512]{1,0:T(8,128)S(1)} %add.201), channel_id=1, source_target_pairs={{0,4},{2,6},{4,0},{6,2},{8,12},{10,14},{12,8},{14,10},{16,20},{18,... | collective-permute-start | bytes 98312 | tf_op jit(solution)/shard_map/ppermute | solution.py:29
  86.6 8.9 %collective-permute-start.8 = (f32[32,39]{1,0:T(8,128)S(1)}, f32[32,39]{1,0:T(8,128)S(1)}, u32[]{:S(2)}, u32[]{:S(2)}) collective-permute-start(f32[32,39]{1,0:T(8,128)S(1)} %pad_maximum_fusion.5), channel_id=1, source_target_pairs={{0,8},{2,10},{4,12},{6,14},{8,0},{10,2},{12,4},{14,6},{16,24},{18,... | collective-permute-start | bytes 14984 | tf_op jit(solution)/shard_map/ppermute | solution.py:29
  92.6 4.5 %collective-permute-start.12 = (f32[16,512]{1,0:T(8,128)S(1)}, f32[16,512]{1,0:T(8,128)S(1)}, u32[]{:S(2)}, u32[]{:S(2)}) collective-permute-start(f32[16,512]{1,0:T(8,128)S(1)} %add.202), channel_id=1, source_target_pairs={{0,8},{2,10},{4,12},{6,14},{8,0},{10,2},{12,4},{14,6},{16,24},{18,... | collective-permute-start | bytes 98312 | tf_op jit(solution)/shard_map/ppermute | solution.py:29
  95.4 13.0 %collective-permute-start.25 = (f32[768,256]{1,0:T(8,128)S(1)}, f32[768,256]{1,0:T(8,128)S(1)}, u32[]{:S(2)}, u32[]{:S(2)}) collective-permute-start(f32[768,256]{1,0:T(8,128)S(1)} %constant_dynamic-update-slice_fusion), channel_id=1, source_target_pairs={{0,2},{2,0},{4,6},{6,4},{8,10},{10,8},{12,14},{14,12},{16,18},{18,... | collective-permute-start | bytes 2359304 | tf_op jit(solution)/shard_map/ppermute | solution.py:29
  95.5 5.6 %collective-permute-start.9 = (f32[64,39]{1,0:T(8,128)S(1)}, f32[64,39]{1,0:T(8,128)S(1)}, u32[]{:S(2)}, u32[]{:S(2)}) collective-permute-start(f32[64,39]{1,0:T(8,128)S(1)} %pad_maximum_fusion.3), channel_id=1, source_target_pairs={{0,16},{2,18},{4,20},{6,22},{8,24},{10,26},{12,28},{14,30},{16,0},... | collective-permute-start | bytes 29960 | tf_op jit(solution)/shard_map/ppermute | solution.py:29
  97.1 4.8 %collective-permute-start.13 = (f32[16,512]{1,0:T(8,128)S(1)}, f32[16,512]{1,0:T(8,128)S(1)}, u32[]{:S(2)}, u32[]{:S(2)}) collective-permute-start(f32[16,512]{1,0:T(8,128)S(1)} %add.203), channel_id=1, source_target_pairs={{0,16},{2,18},{4,20},{6,22},{8,24},{10,26},{12,28},{14,30},{16,0},... | collective-permute-start | bytes 98312 | tf_op jit(solution)/shard_map/ppermute | solution.py:29
  102.0 3.9 %collective-permute-start.14 = (f32[16,512]{1,0:T(8,128)S(1)}, f32[16,512]{1,0:T(8,128)S(1)}, u32[]{:S(2)}, u32[]{:S(2)}) collective-permute-start(f32[16,512]{1,0:T(8,128)S(1)} %add.204), channel_id=1, source_target_pairs={{0,1},{1,0},{2,3},{3,2},{4,5},{5,4},{6,7},{7,6},{8,9},{9,8},{10,11... | collective-permute-start | bytes 98312 | tf_op jit(solution)/shard_map/ppermute | solution.py:29
  105.9 3.9 %copy-start.8 = (f32[16,512]{1,0:T(8,128)}, f32[16,512]{1,0:T(8,128)S(1)}, u32[]{:S(2)}) copy-start(f32[16,512]{1,0:T(8,128)S(1)} %add.205) | copy-start | bytes 98308
  (9 other events, 13.3 us)

commit v2 on v1

v2 whole, which is shorter than its diff:
```python
import jax
import jax.numpy as jnp
from jax import lax
from jax.sharding import PartitionSpec as P

epsilon = 1e-05
HIGHEST = lax.Precision.HIGHEST


def tie(*values):
    return lax.optimization_barrier(values)


def power_of_two(value):
    return value & (value - 1) == 0


def swap(values, axis_name, mask):
    size = lax.axis_size(axis_name)
    return lax.ppermute(values, axis_name, [(i, i ^ mask) for i in range(size)])


def part_of(values, index, count):
    size = values.shape[0] // count
    return lax.dynamic_slice_in_dim(values, index * size, size, axis=0)


def packed(values, exponent):
    (scale,) = tie(jnp.exp2(14.0 - exponent))
    note = jnp.broadcast_to(exponent, (8, values.shape[1]))
    return jnp.concatenate([values * scale, note], axis=0).astype(jnp.float16)


def added(total, exponent, message):
    received = message[-8:].astype(jnp.float32)[:1]
    scale, larger = tie(jnp.exp2(received - 14.0), jnp.maximum(received, exponent) + 1.0)
    return total + message[:-8].astype(jnp.float32) * scale, larger


def scatter_message(total, exponent, axis_name, mask):
    bit = jnp.minimum(lax.axis_index(axis_name) & mask, 1)
    return packed(part_of(total, 1 - bit, 2), exponent)


def scatter_sum(total, exponent, message, axis_name, mask):
    bit = jnp.minimum(lax.axis_index(axis_name) & mask, 1)
    return added(part_of(total, bit, 2), exponent, swap(message, axis_name, mask))


def gather_pair(values, axis_name, mask):
    bit = jnp.minimum(lax.axis_index(axis_name) & mask, 1)
    size = values.shape[0]
    whole = jnp.zeros((2 * size,) + values.shape[1:], values.dtype)
    whole = lax.dynamic_update_slice_in_dim(whole, values, bit * size, axis=0)
    other = swap(values, axis_name, mask)
    return lax.dynamic_update_slice_in_dim(whole, other, (1 - bit) * size, axis=0)


def normalized(values):
    row_mean = jnp.mean(values, axis=-1, keepdims=True)
    centered = values - row_mean
    row_var = jnp.mean(centered * centered, axis=-1, keepdims=True)
    scale = lax.rsqrt(row_var + epsilon)
    return centered * scale, scale


def gelu_share(values):
    return 0.5 * lax.erf(values * 0.5**0.5) + 0.5


def gelu_slope(values):
    return gelu_share(values) + values * jnp.exp(-0.5 * values * values) * 0.3989422804014327


def norm_pull(grad_out, unit, scale, gain):
    grad_unit = grad_out * gain
    first = jnp.mean(grad_unit, axis=-1, keepdims=True)
    second = jnp.mean(grad_unit * unit, axis=-1, keepdims=True)
    grad_raw = scale * (grad_unit - first - unit * second)
    return grad_raw, jnp.sum(grad_out * unit, axis=0), jnp.sum(grad_out, axis=0)


def per_device(
    waveform,
    lengths,
    owner_of,
    targets,
    first_weight,
    first_gain,
    first_shift,
    second_weight,
    second_gain,
    second_shift,
):
    peers, groups = lax.axis_size("dp"), lax.axis_size("fsdp")
    rows, samples = waveform.shape
    later = targets.shape[1]
    frames = samples // 5 - 1
    channels = first_weight.shape[1]
    staged = power_of_two(peers) and power_of_two(groups) and peers >= 4 and groups > 1
    core, side = lax.axis_index("dp") % 2, lax.axis_index("dp") // 2 % 2

    fetched = None
    if staged and groups == 2:
        fetched = swap(part_of(second_weight, core, 2), "fsdp", 1)

    width = samples + 1
    noted = jnp.concatenate([waveform, lengths.astype(jnp.float32)[:, None]], axis=1)
    per_owner = max(1, 2 * rows // peers)
    matches = (owner_of[:, None] == owner_of[None, :]).astype(jnp.int32)
    slots = owner_of * per_owner + jnp.sum(jnp.tril(matches, -1), axis=1)
    placing = slots[:, None] == jnp.arange(peers * per_owner, dtype=jnp.int32)[None, :]
    sent = lax.dot_general(
        placing.astype(jnp.float32),
        noted,
        (((0,), (0,)), ((), ())),
        precision=HIGHEST,
        preferred_element_type=jnp.float32,
    )
    got = lax.all_to_all(sent, "dp", split_axis=0, concat_axis=0, tiled=True)
    present = got[:, samples] > 0.5
    arrival = jnp.cumsum(present.astype(jnp.int32)) - 1
    picking = present[None, :] & (
        arrival[None, :] == jnp.arange(rows, dtype=jnp.int32)[:, None]
    )
    owned = jnp.dot(
        picking.astype(jnp.float32), got, precision=HIGHEST, preferred_element_type=jnp.float32
    )
    waveform, lengths = owned[:, :samples], owned[:, samples].astype(jnp.int32)

    blocks = waveform.reshape(rows, samples // 5, 5).transpose(1, 0, 2)
    windows = jnp.concatenate([blocks[:frames], blocks[1 : frames + 1]], axis=2)
    windows = windows.reshape(frames * rows, 10)
    if fetched is None:
        weight = lax.all_gather(second_weight, "fsdp", axis=0, tiled=True)
    else:
        windows, fetched = tie(windows, fetched)
        fetched_others = swap(fetched, "dp", 1)
        missing = jnp.where(
            core == 0,
            jnp.concatenate([fetched, fetched_others], axis=0),
            jnp.concatenate([fetched_others, fetched], axis=0),
        )
        weight = jnp.where(
            lax.axis_index("fsdp") == 0,
            jnp.concatenate([second_weight, missing], axis=0),
            jnp.concatenate([missing, second_weight], axis=0),
        )
    first_pre = jnp.dot(
        windows, first_weight, precision=HIGHEST, preferred_element_type=jnp.float32
    )
    first_unit, first_scale = normalized(first_pre)
    first_normed = first_unit * first_gain + first_shift
    activated = first_normed * gelu_share(first_normed)
    rounded = activated.astype(jnp.bfloat16).reshape(frames, rows, channels)
    even, odd = rounded[0::2], rounded[1::2]
    patches = jnp.concatenate([even[:later], odd, even[1:]], axis=2)
    patches = patches.reshape(later * rows, 3 * channels)

    second_pre = jnp.dot(patches, weight, preferred_element_type=jnp.float32)
    second_unit, second_scale = normalized(second_pre)
    second_normed = second_unit * second_gain + second_shift
    second_share = gelu_share(second_normed)
    second_act = second_normed * second_share
    second_slope = second_share + second_normed * (
        jnp.exp(-0.5 * second_normed * second_normed) * 0.3989422804014327
    )
    act_mean = jnp.mean(second_act, axis=-1, keepdims=True)
    act_centered = second_act - act_mean
    act_var = jnp.mean(act_centered * act_centered, axis=-1, keepdims=True) + epsilon
    raw_logvar = jnp.log(act_var)
    first_valid = (lengths - 10) // 5 + 1
    second_valid = (first_valid - 3) // 2 + 1
    frame_mask = (
        jnp.arange(later, dtype=jnp.int32)[:, None] < second_valid[None, :]
    ).astype(jnp.float32)
    frame_mask = frame_mask.reshape(later * rows, 1)
    misfit = raw_logvar - targets.T.reshape(later * rows, 1)
    pull = frame_mask * misfit / act_var * (4.0 / channels)
    grad_pre, grad_gain_two, grad_shift_two = norm_pull(
        pull * act_centered * second_slope, second_unit, second_scale, second_gain
    )
    grad_pre = grad_pre.astype(jnp.bfloat16)

    def product(columns):
        return lax.dot_general(
            columns, grad_pre, (((0,), (0,)), ((), ())), preferred_element_type=jnp.float32
        )

    def backward(grad_pre, misfit, windows, first_unit, grad_gain_two, grad_shift_two):
        first_normed = first_unit * first_gain + first_shift
        grad_patches = lax.dot_general(
            grad_pre, weight, (((1,), (1,)), ((), ())), preferred_element_type=jnp.float32
        ).reshape(later, rows, 3 * channels)
        zero_frame = jnp.zeros((1, rows, channels), jnp.float32)
        grad_even = jnp.concatenate([grad_patches[:, :, :channels], zero_frame], axis=0)
        grad_even = grad_even + jnp.concatenate(
            [zero_frame, grad_patches[:, :, 2 * channels :]], axis=0
        )
        grad_odd = jnp.concatenate([grad_patches[:, :, channels : 2 * channels], zero_frame], axis=0)
        grad_act = jnp.stack([grad_even, grad_odd], axis=1).reshape(2 * later + 2, rows, channels)
        grad_act = grad_act[:frames].reshape(frames * rows, channels)
        grad_first, grad_gain_one, grad_shift_one = norm_pull(
            grad_act * gelu_slope(first_normed), first_unit, first_scale, first_gain
        )
        grad_weight_one = lax.dot_general(
            windows,
            grad_first,
            (((0,), (0,)), ((), ())),
            precision=HIGHEST,
            preferred_element_type=jnp.float32,
        )
        loss_sum = jnp.sum(frame_mask * misfit * misfit, axis=0, keepdims=True)
        frame_count = jnp.sum(frame_mask, axis=0, keepdims=True)
        return jnp.concatenate(
            [
                grad_weight_one,
                jnp.stack([grad_gain_one, grad_shift_one, grad_gain_two, grad_shift_two]),
                jnp.broadcast_to(loss_sum, (1, channels)),
                jnp.broadcast_to(frame_count, (1, channels)),
            ],
            axis=0,
        )

    saved = (misfit, windows, first_unit, grad_gain_two, grad_shift_two)
    if staged:
        half = 3 * channels // groups // 2
        middle = channels // 2
        strides = [1 << bit for bit in range(2, peers.bit_length() - 1)]
        group_strides = [1 << bit for bit in range(groups.bit_length() - 2, -1, -1)]
        patch_bound = channels**0.5 * jnp.max(jnp.abs(first_gain)) + jnp.max(jnp.abs(first_shift))
        bound = jnp.max(jnp.abs(grad_pre.astype(jnp.float32)), axis=0, keepdims=True)
        bound = bound * (later * rows * patch_bound)
        exponent = jnp.ceil(jnp.log2(jnp.maximum(bound, 1e-30)))
        (exponent,) = tie(exponent)

        total = product(patches).reshape(groups, 2, half, channels)
        sent = lax.dynamic_index_in_dim(total, 1 - core, 1, keepdims=False)
        kept = lax.dynamic_index_in_dim(total, core, 1, keepdims=False)
        message = packed(sent.reshape(-1, channels), exponent)
        total, exponent = added(kept.reshape(-1, channels), exponent, swap(message, "dp", 1))

        near, far = total[:, :middle], total[:, middle:]
        near_exponent, far_exponent = exponent[:, :middle], exponent[:, middle:]
        near_message = scatter_message(near, near_exponent, "fsdp", group_strides[0])
        sides = far.reshape(groups, 2, half // 2, middle)
        kept = lax.dynamic_index_in_dim(sides, side, 1, keepdims=False).reshape(-1, middle)
        sent = lax.dynamic_index_in_dim(sides, 1 - side, 1, keepdims=False).reshape(-1, middle)
        far_message = packed(sent, far_exponent)
        grad_pre, near_message, far_message = tie(grad_pre, near_message, far_message)
        small = backward(grad_pre, *saved)
        far, far_exponent = added(kept, far_exponent, swap(far_message, "dp", 2))
        for mask in group_strides:
            if mask != group_strides[0]:
                near_message = scatter_message(near, near_exponent, "fsdp", mask)
            near, near_exponent = scatter_sum(near, near_exponent, near_message, "fsdp", mask)
        near_message = scatter_message(near, near_exponent, "dp", 2)
        far_message = scatter_message(far, far_exponent, "fsdp", group_strides[0])
        small, near_message, far_message = tie(small, near_message, far_message)
        small = small + swap(small, "dp", 1)
        near, near_exponent = scatter_sum(near, near_exponent, near_message, "dp", 2)
        for mask in group_strides:
            if mask != group_strides[0]:
                far_message = scatter_message(far, far_exponent, "fsdp", mask)
            far, far_exponent = scatter_sum(far, far_exponent, far_message, "fsdp", mask)
        total = jnp.concatenate([near, far], axis=1)
        exponent = jnp.concatenate([near_exponent, far_exponent], axis=1)

        steps = [("fsdp", mask) for mask in group_strides] + [("dp", 2)]
        steps += [("dp", mask) for mask in strides]
        for mask in strides:
            message = scatter_message(total, exponent, "dp", mask)
            message, small = tie(message, small)
            axis_name, small_mask = steps.pop(0)
            small = small + swap(small, axis_name, small_mask)
            total, exponent = scatter_sum(total, exponent, message, "dp", mask)
        piece = total.shape[0]
        message = packed(total, exponent)
        for mask in strides[::-1] + [2]:
            message, small = tie(message, small)
            if steps:
                axis_name, small_mask = steps.pop(0)
                small = small + swap(small, axis_name, small_mask)
            message = gather_pair(message, "dp", mask)
        while steps:
            axis_name, small_mask = steps.pop(0)
            small = small + swap(small, axis_name, small_mask)
        other_message = swap(message, "dp", 1)

        def opened(blocks):
            blocks = blocks.reshape(-1, piece + 8, channels)
            (scale,) = tie(jnp.exp2(blocks[:, piece:, :].astype(jnp.float32)[:, :1] - 14.0))
            return (blocks[:, :piece].astype(jnp.float32) * scale).reshape(half, channels)

        gradient = jnp.zeros((2 * half, channels), jnp.float32)
        gradient = lax.dynamic_update_slice_in_dim(gradient, opened(message), core * half, axis=0)
        grad_weight_two = lax.dynamic_update_slice_in_dim(
            gradient, opened(other_message), (1 - core) * half, axis=0
        )
    else:
        partial = lax.psum_scatter(product(patches), "fsdp", scatter_dimension=0, tiled=True)
        grad_weight_two = lax.psum(partial, "dp")
        small = lax.psum(backward(grad_pre, *saved), ("dp", "fsdp"))

    logvar = (raw_logvar * frame_mask).reshape(later, rows).T
    loss = small[14, 0] / small[15, 0]
    return (logvar, loss, grad_weight_two, small[:10], small[10], small[11], small[12], small[13])


def solution(mesh):
    placed = (
        P(("dp", "fsdp"), None),
        P(("dp", "fsdp")),
        P(("dp", "fsdp")),
        P(("dp", "fsdp"), None),
        P(),
        P(),
        P(),
        P("fsdp", None),
        P(),
        P(),
    )
    return jax.shard_map(
        per_device,
        mesh=mesh,
        in_specs=placed,
        out_specs=(P(("dp", "fsdp"), None), P(), P("fsdp", None), P(), P(), P(), P(), P()),
        check_vma=False,
    )
```

time: 111 us -> 94.2 us (0.85)
  waiting for transfers between devices: 43 us -> 26.3 us
  starting transfers between devices: 30.1 us -> 24.1 us
  other arithmetic: 16.6 us -> 19.3 us
  between operations: 3.83 us -> 5.31 us
  local copies, waits for them, and re-layouts: 9.55 us -> 10.7 us
    ppermute x26 -> x18, waiting for transfers between devices: 43 us -> 24.4 us  [swap(): return lax.ppermute(values, axis_name, [(i, i ^ mask) for i in range(size)])]
    ppermute x26 -> x18, starting transfers between devices: 30.1 us -> 18.1 us  [swap(): return lax.ppermute(values, axis_name, [(i, i ^ mask) for i in range(size)])]
    all_to_all x0 -> x1, starting transfers between devices: none -> 5.91 us  [per_device(): got = lax.all_to_all(sent, 'dp', split_axis=0, concat_axis=0, tiled=True)]
    add x7 -> x19, other arithmetic: 0.15 us -> 4.76 us  [the longest x6 2.63 us: added(): return (total + message[:-8].astype(jnp.float32) * scale, larger)]
    reshape x1, other arithmetic: 4.38 us -> 0.49 us  [per_device(): rounded = activated.astype(jnp.bfloat16).reshape(frames, rows, channels)]
    reduce_max x0 -> x3, other arithmetic: none -> 2.85 us  [the longest x1 1.29 us: per_device(): jnp.max(jnp.abs(first_gain))]
    all_to_all x0 -> x1, waiting for transfers between devices: none -> 1.88 us  [per_device(): got = lax.all_to_all(sent, 'dp', split_axis=0, concat_axis=0, tiled=True)]
    broadcast_in_dim x5 -> x15, local copies, waits for them, and re-layouts: 0.17 us -> 1.7 us  [the longest x1 0.65 us: backward(): jnp.broadcast_to(loss_sum, (1, channels))]
  transfers between devices with their start and end apart: 26 -> 19, of which waited for: 14 -> 17; matrix products, arithmetic and copies ran while one was open for 19% -> 19% of each run, Pallas kernels for 0% -> 0%
where the time goes in v2:
time: 94.2 us; the launch traced here: 93.6 us
  waiting for transfers between devices  26.3 us (28%)
  starting transfers between devices  24.1 us (26%)
  other arithmetic  19.3 us (20%)
  local copies, waits for them, and re-layouts  10.7 us (11%)
  matrix products  7.94 us (8%)
  between operations  5.31 us (6%)
    ppermute x18, waiting for transfers between devices, swap(): return lax.ppermute(values, axis_name, [(i, i ^ mask) for i in range(size)])  24.4 us
    ppermute x18, starting transfers between devices, swap(): return lax.ppermute(values, axis_name, [(i, i ^ mask) for i in range(size)])  18.1 us
    all_to_all x1, starting transfers between devices, per_device(): got = lax.all_to_all(sent, 'dp', split_axis=0, concat_axis=0, tiled=True)  5.91 us
    unnamed x36, local copies, waits for them, and re-layouts  3.46 us
    add x6, other arithmetic, added(): return (total + message[:-8].astype(jnp.float32) * scale, larger)  2.63 us
    dot_general x1, matrix products, per_device(): second_pre = jnp.dot(patches, weight, preferred_element_type=jnp.float32)  2.47 us
    reduce_sum x2, other arithmetic, norm_pull(): jnp.sum(grad_out * unit, axis=0)  2.07 us
    concatenate x8, other arithmetic, packed(): return jnp.concatenate([values * scale, note], axis=0).astype(jnp.float16)  1.97 us
  transfers between devices with their start and end apart: 19, of which 17 were waited for; matrix products, arithmetic and copies ran while one was open for 19% of the time, Pallas kernels for 0%

profile of v2, /device:TPU:0, one launch (start us, length us, event | category | flops | bytes accessed | tf_op | source)
XLA Modules:
  0.0 93.6 jit_solution(1083097987646898349)
XLA Ops:
  1.7 3.1 %collective-permute-start = (bf16[384,512]{1,0:T(8,128)(2,1)S(1)}, bf16[384,512]{1,0:T(8,128)(2,1)}, u32[]{:S(2)}, u32[]{:S(2)}) collective-permute-start(bf16[384,512]{1,0:T(8,128)(2,1)S(1)} %constant_dynamic-slice_fusion.4), channel_id=1, source_target_pairs={{0,1},{1,0},{2,3},{3,2},{4,5},{5,4},{6,7},{7,6},{8,9},{9,8},{10,11... | collective-permute-start | bytes 1179656 | tf_op jit(solution)/shard_map/ppermute | solution.py:20
  8.7 5.9 %all-to-all-start = ((f32[16,1,401]{2,1,0:T(1,128)}), f32[16,1,401]{2,1,0:T(1,128)S(1)}, u32[]{:S(2)}, u32[]{:S(2)}) async-start(f32[16,1,401]{2,1,0:T(1,128)} %copy.60), calls=%async_computation | async-start | bytes 65536 | tf_op jit(solution)/shard_map/all_to_all | solution.py:120
  14.6 1.3 %abs_reduce_fusion.2 = f32[]{:T(128)} fusion(f32[512]{0:T(512)} %param.15), kind=kLoop, calls=%fused_computation.153 | loop fusion | flops 1023 | bytes 2052 | tf_op jit(solution)/shard_map/reduce_max | solution.py:231
  15.9 1.3 %abs_reduce_fusion.1 = f32[]{:T(128)} fusion(f32[512]{0:T(512)} %param.16), kind=kLoop, calls=%fused_computation.152 | loop fusion | flops 1023 | bytes 2052 | tf_op jit(solution)/shard_map/reduce_max | solution.py:231
  19.4 1.9 %all-to-all-done = f32[16,1,401]{2,1,0:T(1,128)S(1)} async-done(((f32[16,1,401]{2,1,0:T(1,128)}), f32[16,1,401]{2,1,0:T(1,128)S(1)}, u32[]{:S(2)}, u32[]{:S(2)}) %all-to-all-start) | async-done | bytes 25696 | tf_op jit(solution)/shard_map/all_to_all | solution.py:120
  23.5 1.3 %fusion.65 = (f32[632]{0:T(1024)S(1)}, f32[632,512]{1,0:T(8,128)S(1)}) fusion(f32[632,10]{0,1:T(8,128)S(1)} %reshape.341, f32[10,512]{1,0:T(8,128)S(1)} %copy-done), kind=kOutput, calls=%fused_computation.208 | convolution fusion | flops 39153032 | bytes 1342624 | tf_op jit(solution)/shard_map/dot_general | solution.py:149
  27.8 1.6 %maximum_select_fusion.1 = bf16[768,512]{1,0:T(8,128)(2,1)S(1)} fusion(bf16[384,512]{1,0:T(8,128)(2,1)} %collective-permute-done.1, bf16[384,512]{1,0:T(8,128)(2,1)} %collective-permute-done, pred[]{:T(512)S(6)} %eq.58), kind=kLoop, calls=%fused_computation.35 | loop fusion | flops 3538944 | bytes 1572865 | tf_op jit(solution)/shard_map/jit(_where)/select_n | solution.py:139
  29.5 2.5 %fusion.66 = (f32[312]{0:T(512)S(1)}, f32[312,512]{1,0:T(8,128)S(1)}) fusion(bf16[768,512]{1,0:T(8,128)(2,1)S(1)} %maximum_select_fusion.1, bf16[768,512]{1,0:T(8,128)(2,1)} %param.17, pred[]{:T(512)S(6)} %eq.57, bf16[39,8,512]{2,1,0:T(8,128)(2,1)S(1)} %copy-done.5, bf16[39,8,512]{2,1,0:T(8,128)(2,1)S(1)} %copy-done.7, bf16[39,8,512]{2,1,0:T(8,128)(2,1)S(1)} %copy-done.3), kind=kOutput, calls=%fused_computation.209 | convolution fusion | flops 500846272 | bytes 3171553 | tf_op jit(solution)/shard_map/dot_general | solution.py:160
  34.0 1.0 %fusion.14 = f32[2,2,384,512]{3,2,1,0:T(8,128)S(1)} fusion(bf16[2,2,384,312]{2,1,0,3:T(2,128)(2,1)S(1)} %dot_general.30, bf16[312,512]{1,0:T(8,128)(2,1)S(1)} %get-tuple-element.46), kind=kOutput, calls=%fused_computation.32 | convolution fusion | flops 490733568 | bytes 4423680 | tf_op jit(solution)/shard_map/dot_general | solution.py:186
  35.6 1.1 %pad_maximum_fusion.2 = f16[776,512]{1,0:T(8,128)(2,1)} fusion(f16[8,512]{1,0:T(8,128)(2,1)S(1)} %broadcast_in_dim.55, f16[768,512]{1,0:T(8,128)(2,1)S(1)} %fusion), kind=kLoop, calls=%fused_computation.34 | loop fusion | flops 397312 | bytes 1589248 | tf_op jit(solution)/shard_map/concatenate | solution.py:31
  37.5 1.8 %collective-permute-done.2 = f16[776,512]{1,0:T(8,128)(2,1)} collective-permute-done((f16[776,512]{1,0:T(8,128)(2,1)}, f16[776,512]{1,0:T(8,128)(2,1)}, u32[]{:S(2)}, u32[]{:S(2)}) %collective-permute-start.2) | collective-permute-done | bytes 794656 | tf_op jit(solution)/shard_map/ppermute | solution.py:20
  40.1 1.5 %bitcast_add_fusion = f32[768,512]{1,0:T(8,128)S(1)} fusion(f32[2,1,384,512]{3,2,1,0:T(8,128)S(1)} %get-tuple-element.132, f16[776,512]{1,0:T(8,128)(2,1)} %collective-permute-done.2, f32[512]{0:T(512)S(1)} %bitcast.116), kind=kLoop, calls=%fused_computation.5 | loop fusion | flops 1179648 | bytes 3934208 | tf_op jit(solution)/shard_map/add | solution.py:37
  44.9 1.4 %multiply_reduce_fusion = (f32[512]{0:T(512)S(1)}, f32[632]{0:T(1024)S(1)}, f32[632]{0:T(1024)S(1)}, f32[512]{0:T(512)S(1)}, f32[632,512]{1,0:T(8,128)S(1)}) fusion(f32[632]{0:T(1024)S(1)} %add_rsqrt_fusion, f32[632,512]{1,0:T(8,128)S(1)} %get-tuple-element.173, f32[632]{0:T(1024)S(1)} %broadcast_multiply_fusion.2, f32[512]{0:T(512)S(1)} %copy-done.13, ...), kind=kLoop, calls=%fused_computation.13 | loop fusion | flops 6469392 | bytes 3901312 | tf_op jit(solution)/shard_map/reduce_sum | solution.py:80
  46.3 1.3 %fusion.6 = f32[10,512]{1,0:T(8,128)S(1)} fusion(f32[632,10]{0,1:T(8,128)S(1)} %reshape.341, f32[632,512]{1,0:T(8,128)S(1)} %get-tuple-element.124, f32[632]{0:T(1024)S(1)} %broadcast_multiply_fusion, f32[632]{0:T(1024)S(1)} %broadcast_multiply_fusion.1, f32[512]{0:T(512)S(1)} %copy-done.13, f32[632]{0:T(1024)S(1)} %add_rsqrt_fusion, ...), kind=kOutput, calls=%fused_computation.14 | convolution fusion | flops 41095168 | bytes 2646592 | tf_op jit(solution)/shard_map/dot_general | solution.py:206
  48.9 1.1 %collective-permute-done.3 = f16[392,256]{1,0:T(8,128)(2,1)S(1)} collective-permute-done((f16[392,256]{1,0:T(8,128)(2,1)}, f16[392,256]{1,0:T(8,128)(2,1)S(1)}, u32[]{:S(2)}, u32[]{:S(2)}) %collective-permute-start.3) | collective-permute-done | bytes 200736 | tf_op jit(solution)/shard_map/ppermute | solution.py:20
  52.1 1.6 %collective-permute-start.6 = (f16[200,256]{1,0:T(8,128)(2,1)S(1)}, f16[200,256]{1,0:T(8,128)(2,1)S(1)}, u32[]{:S(2)}, u32[]{:S(2)}) collective-permute-start(f16[200,256]{1,0:T(8,128)(2,1)S(1)} %pad_maximum_fusion.9), channel_id=1, source_target_pairs={{0,1},{1,0},{2,3},{3,2},{4,5},{5,4},{6,7},{7,6},{8,9},{9,8},{10,11... | collective-permute-start | bytes 307208 | tf_op jit(solution)/shard_map/ppermute | solution.py:20
  54.9 1.9 %collective-permute-done.6 = f16[200,256]{1,0:T(8,128)(2,1)S(1)} collective-permute-done((f16[200,256]{1,0:T(8,128)(2,1)S(1)}, f16[200,256]{1,0:T(8,128)(2,1)S(1)}, u32[]{:S(2)}, u32[]{:S(2)}) %collective-permute-start.6) | collective-permute-done | bytes 102432 | tf_op jit(solution)/shard_map/ppermute | solution.py:20
  56.8 2.1 %collective-permute-done.5 = f16[200,256]{1,0:T(8,128)(2,1)S(1)} collective-permute-done((f16[200,256]{1,0:T(8,128)(2,1)S(1)}, f16[200,256]{1,0:T(8,128)(2,1)S(1)}, u32[]{:S(2)}, u32[]{:S(2)}) %collective-permute-start.5) | collective-permute-done | bytes 102432 | tf_op jit(solution)/shard_map/ppermute | solution.py:20
  60.1 3.4 %collective-permute-done.9 = f32[16,512]{1,0:T(8,128)S(1)} collective-permute-done((f32[16,512]{1,0:T(8,128)S(1)}, f32[16,512]{1,0:T(8,128)S(1)}, u32[]{:S(2)}, u32[]{:S(2)}) %collective-permute-start.9) | collective-permute-done | bytes 32800 | tf_op jit(solution)/shard_map/ppermute | solution.py:20
  64.1 1.7 %collective-permute-start.10 = (f16[56,512]{1,0:T(8,128)(2,1)S(1)}, f16[56,512]{1,0:T(8,128)(2,1)S(1)}, u32[]{:S(2)}, u32[]{:S(2)}) collective-permute-start(f16[56,512]{1,0:T(8,128)(2,1)S(1)} %pad_maximum_fusion.10), channel_id=1, source_target_pairs={{0,16},{2,18},{4,20},{6,22},{8,24},{10,26},{12,28},{14,30},{16,0},... | collective-permute-start | bytes 172040 | tf_op jit(solution)/shard_map/ppermute | solution.py:20
  65.8 1.5 %collective-permute-start.11 = (f32[16,512]{1,0:T(8,128)S(1)}, f32[16,512]{1,0:T(8,128)S(1)}, u32[]{:S(2)}, u32[]{:S(2)}) collective-permute-start(f32[16,512]{1,0:T(8,128)S(1)} %add.320), channel_id=1, source_target_pairs={{0,4},{2,6},{4,0},{6,2},{8,12},{10,14},{12,8},{14,10},{16,20},{18,... | collective-permute-start | bytes 98312 | tf_op jit(solution)/shard_map/ppermute | solution.py:20
  68.0 1.8 %collective-permute-done.11 = f32[16,512]{1,0:T(8,128)S(1)} collective-permute-done((f32[16,512]{1,0:T(8,128)S(1)}, f32[16,512]{1,0:T(8,128)S(1)}, u32[]{:S(2)}, u32[]{:S(2)}) %collective-permute-start.11) | collective-permute-done | bytes 32800 | tf_op jit(solution)/shard_map/ppermute | solution.py:20
  70.7 1.8 %collective-permute-start.12 = (f16[56,512]{1,0:T(8,128)(2,1)S(1)}, f16[56,512]{1,0:T(8,128)(2,1)S(1)}, u32[]{:S(2)}, u32[]{:S(2)}) collective-permute-start(f16[56,512]{1,0:T(8,128)(2,1)S(1)} %pad_maximum_fusion.11), channel_id=1, source_target_pairs={{0,16},{2,18},{4,20},{6,22},{8,24},{10,26},{12,28},{14,30},{16,0},... | collective-permute-start | bytes 172040 | tf_op jit(solution)/shard_map/ppermute | solution.py:20
  72.5 1.3 %collective-permute-done.13 = f32[16,512]{1,0:T(8,128)S(1)} collective-permute-done((f32[16,512]{1,0:T(8,128)S(1)}, f32[16,512]{1,0:T(8,128)S(1)}, u32[]{:S(2)}, u32[]{:S(2)}) %collective-permute-start.13) | collective-permute-done | bytes 32800 | tf_op jit(solution)/shard_map/ppermute | solution.py:20
  73.9 1.9 %collective-permute-done.12 = f16[56,512]{1,0:T(8,128)(2,1)S(1)} collective-permute-done((f16[56,512]{1,0:T(8,128)(2,1)S(1)}, f16[56,512]{1,0:T(8,128)(2,1)S(1)}, u32[]{:S(2)}, u32[]{:S(2)}) %collective-permute-start.12) | collective-permute-done | bytes 57376 | tf_op jit(solution)/shard_map/ppermute | solution.py:20
  75.8 2.4 %collective-permute-start.15 = (f32[16,512]{1,0:T(8,128)S(1)}, f32[16,512]{1,0:T(8,128)S(1)}, u32[]{:S(2)}, u32[]{:S(2)}) collective-permute-start(f32[16,512]{1,0:T(8,128)S(1)} %add.326), channel_id=1, source_target_pairs={{0,16},{2,18},{4,20},{6,22},{8,24},{10,26},{12,28},{14,30},{16,0},... | collective-permute-start | bytes 98312 | tf_op jit(solution)/shard_map/ppermute | solution.py:20
  78.3 1.5 %collective-permute-start.14 = (f16[112,512]{1,0:T(8,128)(2,1)S(1)}, f16[112,512]{1,0:T(8,128)(2,1)S(1)}, u32[]{:S(2)}, u32[]{:S(2)}) collective-permute-start(f16[112,512]{1,0:T(8,128)(2,1)S(1)} %constant_dynamic-update-slice_fusion.6), channel_id=1, source_target_pairs={{0,8},{2,10},{4,12},{6,14},{8,0},{10,2},{12,4},{14,6},{16,24},{18,... | collective-permute-start | bytes 344072 | tf_op jit(solution)/shard_map/ppermute | solution.py:20
  80.7 2.3 %collective-permute-done.14 = f16[112,512]{1,0:T(8,128)(2,1)S(1)} collective-permute-done((f16[112,512]{1,0:T(8,128)(2,1)S(1)}, f16[112,512]{1,0:T(8,128)(2,1)S(1)}, u32[]{:S(2)}, u32[]{:S(2)}) %collective-permute-start.14) | collective-permute-done | bytes 114720 | tf_op jit(solution)/shard_map/ppermute | solution.py:20
  83.1 1.3 %collective-permute-start.16 = (f16[224,512]{1,0:T(8,128)(2,1)S(1)}, f16[224,512]{1,0:T(8,128)(2,1)S(1)}, u32[]{:S(2)}, u32[]{:S(2)}) collective-permute-start(f16[224,512]{1,0:T(8,128)(2,1)S(1)} %constant_dynamic-update-slice_fusion.4), channel_id=1, source_target_pairs={{0,4},{2,6},{4,0},{6,2},{8,12},{10,14},{12,8},{14,10},{16,20},{18,... | collective-permute-start | bytes 688136 | tf_op jit(solution)/shard_map/ppermute | solution.py:20
  86.9 2.3 %collective-permute-done.16 = f16[224,512]{1,0:T(8,128)(2,1)S(1)} collective-permute-done((f16[224,512]{1,0:T(8,128)(2,1)S(1)}, f16[224,512]{1,0:T(8,128)(2,1)S(1)}, u32[]{:S(2)}, u32[]{:S(2)}) %collective-permute-start.16) | collective-permute-done | bytes 229408 | tf_op jit(solution)/shard_map/ppermute | solution.py:20
  89.7 1.4 %collective-permute-done.17 = f16[448,512]{1,0:T(8,128)(2,1)S(1)} collective-permute-done((f16[448,512]{1,0:T(8,128)(2,1)S(1)}, f16[448,512]{1,0:T(8,128)(2,1)S(1)}, u32[]{:S(2)}, u32[]{:S(2)}) %collective-permute-start.17) | collective-permute-done | bytes 458784 | tf_op jit(solution)/shard_map/ppermute | solution.py:20
  91.3 1.1 %copy-done.1 = f32[768,512]{1,0:T(8,128)} copy-done((f32[768,512]{1,0:T(8,128)}, f32[768,512]{1,0:T(8,128)S(1)}, u32[]{:S(2)}) %copy-start.1) | copy-done | bytes 1572888
  (186 shorter events, 29.0 us)
Async XLA Ops:
  0.6 22.8 %copy-start = (f32[10,512]{1,0:T(8,128)S(1)}, f32[10,512]{1,0:T(8,128)}, u32[]{:S(2)}) copy-start(f32[10,512]{1,0:T(8,128)} %param.14) | copy-start | bytes 61444
  1.7 21.8 %collective-permute-start = (bf16[384,512]{1,0:T(8,128)(2,1)S(1)}, bf16[384,512]{1,0:T(8,128)(2,1)}, u32[]{:S(2)}, u32[]{:S(2)}) collective-permute-start(bf16[384,512]{1,0:T(8,128)(2,1)S(1)} %constant_dynamic-slice_fusion.4), channel_id=1, source_target_pairs={{0,1},{1,0},{2,3},{3,2},{4,5},{5,4},{6,7},{7,6},{8,9},{9,8},{10,11... | collective-permute-start | bytes 1179656 | tf_op jit(solution)/shard_map/ppermute | solution.py:20
  8.7 12.6 %all-to-all-start = ((f32[16,1,401]{2,1,0:T(1,128)}), f32[16,1,401]{2,1,0:T(1,128)S(1)}, u32[]{:S(2)}, u32[]{:S(2)}) async-start(f32[16,1,401]{2,1,0:T(1,128)} %copy.60), calls=%async_computation | async-start | bytes 65536 | tf_op jit(solution)/shard_map/all_to_all | solution.py:120
  23.4 1.7 %copy-start.13 = (f32[512]{0:T(512)S(1)}, f32[512]{0:T(512)}, u32[]{:S(2)}) copy-start(f32[512]{0:T(512)} %param.15) | copy-start | bytes 6148
  23.5 1.7 %copy-start.15 = (f32[512]{0:T(512)S(1)}, f32[512]{0:T(512)}, u32[]{:S(2)}) copy-start(f32[512]{0:T(512)} %param.16) | copy-start | bytes 6148
  25.7 2.1 %collective-permute-start.1 = (bf16[384,512]{1,0:T(8,128)(2,1)}, bf16[384,512]{1,0:T(8,128)(2,1)}, u32[]{:S(2)}, u32[]{:S(2)}) collective-permute-start(bf16[384,512]{1,0:T(8,128)(2,1)} %collective-permute-done), channel_id=1, source_target_pairs={{0,2},{2,0},{4,6},{6,4},{8,10},{10,8},{12,14},{14,12},{16,18},{18,... | collective-permute-start | bytes 1179656 | tf_op jit(solution)/shard_map/ppermute | solution.py:20
  26.9 2.5 %copy-start.3 = (bf16[39,8,512]{2,1,0:T(8,128)(2,1)S(1)}, bf16[39,8,512]{2,1,0:T(8,128)(2,1)}, u32[]{:S(2)}) copy-start(bf16[39,8,512]{2,1,0:T(8,128)(2,1)} %copy-done.2) | copy-start | bytes 958468
  26.9 2.5 %copy-start.5 = (bf16[39,8,512]{2,1,0:T(8,128)(2,1)S(1)}, bf16[39,8,512]{2,1,0:T(8,128)(2,1)}, u32[]{:S(2)}) copy-start(bf16[39,8,512]{2,1,0:T(8,128)(2,1)} %copy-done.4) | copy-start | bytes 958468
  27.0 2.5 %copy-start.7 = (bf16[39,8,512]{2,1,0:T(8,128)(2,1)S(1)}, bf16[39,8,512]{2,1,0:T(8,128)(2,1)}, u32[]{:S(2)}) copy-start(bf16[39,8,512]{2,1,0:T(8,128)(2,1)} %copy-done.6) | copy-start | bytes 958468
  29.4 2.5 %copy-start.8 = (bf16[768,512]{1,0:T(8,128)(2,1)}, bf16[768,512]{1,0:T(8,128)(2,1)S(1)}, u32[]{:S(2)}) copy-start(bf16[768,512]{1,0:T(8,128)(2,1)S(1)} %maximum_select_fusion.1) | copy-start | bytes 2359300
  29.4 2.8 %copy-start.12 = (f32[512]{0:T(512)S(1)}, f32[512]{0:T(512)}, u32[]{:S(2)}) copy-start(f32[512]{0:T(512)} %param.18) | copy-start | bytes 6148
  29.5 2.8 %copy-start.14 = (f32[512]{0:T(512)S(1)}, f32[512]{0:T(512)}, u32[]{:S(2)}) copy-start(f32[512]{0:T(512)} %param.19) | copy-start | bytes 6148
  36.7 2.6 %collective-permute-start.2 = (f16[776,512]{1,0:T(8,128)(2,1)}, f16[776,512]{1,0:T(8,128)(2,1)}, u32[]{:S(2)}, u32[]{:S(2)}) collective-permute-start(f16[776,512]{1,0:T(8,128)(2,1)} %pad_maximum_fusion.2), channel_id=1, source_target_pairs={{0,2},{2,0},{4,6},{6,4},{8,10},{10,8},{12,14},{14,12},{16,18},{18,... | collective-permute-start | bytes 2383880 | tf_op jit(solution)/shard_map/ppermute | solution.py:20
  41.8 1.8 %copy-start.9 = (bf16[768,512]{1,0:T(8,128)(2,1)S(1)}, bf16[768,512]{1,0:T(8,128)(2,1)}, u32[]{:S(2)}) copy-start(bf16[768,512]{1,0:T(8,128)(2,1)} %copy-done.8) | copy-start | bytes 2359300
  41.8 1.8 %copy-start.10 = (bf16[768,512]{1,0:T(8,128)(2,1)S(1)}, bf16[768,512]{1,0:T(8,128)(2,1)}, u32[]{:S(2)}) copy-start(bf16[768,512]{1,0:T(8,128)(2,1)} %param.17) | copy-start | bytes 2359300
  42.7 7.2 %collective-permute-start.3 = (f16[392,256]{1,0:T(8,128)(2,1)}, f16[392,256]{1,0:T(8,128)(2,1)S(1)}, u32[]{:S(2)}, u32[]{:S(2)}) collective-permute-start(f16[392,256]{1,0:T(8,128)(2,1)} %pad_maximum_fusion.5), channel_id=1, source_target_pairs={{0,1},{1,0},{2,3},{3,2},{4,5},{5,4},{6,7},{7,6},{8,9},{9,8},{10,11... | collective-permute-start | bytes 602120 | tf_op jit(solution)/shard_map/ppermute | solution.py:20
  43.2 6.9 %collective-permute-start.4 = (f16[392,256]{1,0:T(8,128)(2,1)S(1)}, f16[392,256]{1,0:T(8,128)(2,1)}, u32[]{:S(2)}, u32[]{:S(2)}) collective-permute-start(f16[392,256]{1,0:T(8,128)(2,1)S(1)} %pad_maximum_fusion.6), channel_id=1, source_target_pairs={{0,4},{2,6},{4,0},{6,2},{8,12},{10,14},{12,8},{14,10},{16,20},{18,... | collective-permute-start | bytes 602120 | tf_op jit(solution)/shard_map/ppermute | solution.py:20
  52.1 4.7 %collective-permute-start.6 = (f16[200,256]{1,0:T(8,128)(2,1)S(1)}, f16[200,256]{1,0:T(8,128)(2,1)S(1)}, u32[]{:S(2)}, u32[]{:S(2)}) collective-permute-start(f16[200,256]{1,0:T(8,128)(2,1)S(1)} %pad_maximum_fusion.9), channel_id=1, source_target_pairs={{0,1},{1,0},{2,3},{3,2},{4,5},{5,4},{6,7},{7,6},{8,9},{9,8},{10,11... | collective-permute-start | bytes 307208 | tf_op jit(solution)/shard_map/ppermute | solution.py:20
  53.7 1.2 %collective-permute-start.7 = (f32[16,512]{1,0:T(8,128)S(1)}, f32[16,512]{1,0:T(8,128)S(1)}, u32[]{:S(2)}, u32[]{:S(2)}) collective-permute-start(f32[16,512]{1,0:T(8,128)S(1)} %concatenate.92), channel_id=1, source_target_pairs={{0,2},{2,0},{4,6},{6,4},{8,10},{10,8},{12,14},{14,12},{16,18},{18,... | collective-permute-start | bytes 98312 | tf_op jit(solution)/shard_map/ppermute | solution.py:20
  53.7 5.3 %collective-permute-start.5 = (f16[200,256]{1,0:T(8,128)(2,1)S(1)}, f16[200,256]{1,0:T(8,128)(2,1)S(1)}, u32[]{:S(2)}, u32[]{:S(2)}) collective-permute-start(f16[200,256]{1,0:T(8,128)(2,1)S(1)} %pad_maximum_fusion.8), channel_id=1, source_target_pairs={{0,4},{2,6},{4,0},{6,2},{8,12},{10,14},{12,8},{14,10},{16,20},{18,... | collective-permute-start | bytes 307208 | tf_op jit(solution)/shard_map/ppermute | solution.py:20
  59.2 4.8 %collective-permute-start.8 = (f16[104,512]{1,0:T(8,128)(2,1)S(1)}, f16[104,512]{1,0:T(8,128)(2,1)S(1)}, u32[]{:S(2)}, u32[]{:S(2)}) collective-permute-start(f16[104,512]{1,0:T(8,128)(2,1)S(1)} %pad_maximum_fusion.7), channel_id=1, source_target_pairs={{0,8},{2,10},{4,12},{6,14},{8,0},{10,2},{12,4},{14,6},{16,24},{18,... | collective-permute-start | bytes 319496 | tf_op jit(solution)/shard_map/ppermute | solution.py:20
  59.6 3.9 %collective-permute-start.9 = (f32[16,512]{1,0:T(8,128)S(1)}, f32[16,512]{1,0:T(8,128)S(1)}, u32[]{:S(2)}, u32[]{:S(2)}) collective-permute-start(f32[16,512]{1,0:T(8,128)S(1)} %add.315), channel_id=1, source_target_pairs={{0,1},{1,0},{2,3},{3,2},{4,5},{5,4},{6,7},{7,6},{8,9},{9,8},{10,11... | collective-permute-start | bytes 98312 | tf_op jit(solution)/shard_map/ppermute | solution.py:20
  64.1 5.6 %collective-permute-start.10 = (f16[56,512]{1,0:T(8,128)(2,1)S(1)}, f16[56,512]{1,0:T(8,128)(2,1)S(1)}, u32[]{:S(2)}, u32[]{:S(2)}) collective-permute-start(f16[56,512]{1,0:T(8,128)(2,1)S(1)} %pad_maximum_fusion.10), channel_id=1, source_target_pairs={{0,16},{2,18},{4,20},{6,22},{8,24},{10,26},{12,28},{14,30},{16,0},... | collective-permute-start | bytes 172040 | tf_op jit(solution)/shard_map/ppermute | solution.py:20
  65.8 3.9 %collective-permute-start.11 = (f32[16,512]{1,0:T(8,128)S(1)}, f32[16,512]{1,0:T(8,128)S(1)}, u32[]{:S(2)}, u32[]{:S(2)}) collective-permute-start(f32[16,512]{1,0:T(8,128)S(1)} %add.320), channel_id=1, source_target_pairs={{0,4},{2,6},{4,0},{6,2},{8,12},{10,14},{12,8},{14,10},{16,20},{18,... | collective-permute-start | bytes 98312 | tf_op jit(solution)/shard_map/ppermute | solution.py:20
  69.9 4.0 %collective-permute-start.13 = (f32[16,512]{1,0:T(8,128)S(1)}, f32[16,512]{1,0:T(8,128)S(1)}, u32[]{:S(2)}, u32[]{:S(2)}) collective-permute-start(f32[16,512]{1,0:T(8,128)S(1)} %add.323), channel_id=1, source_target_pairs={{0,8},{2,10},{4,12},{6,14},{8,0},{10,2},{12,4},{14,6},{16,24},{18,... | collective-permute-start | bytes 98312 | tf_op jit(solution)/shard_map/ppermute | solution.py:20
  70.7 5.1 %collective-permute-start.12 = (f16[56,512]{1,0:T(8,128)(2,1)S(1)}, f16[56,512]{1,0:T(8,128)(2,1)S(1)}, u32[]{:S(2)}, u32[]{:S(2)}) collective-permute-start(f16[56,512]{1,0:T(8,128)(2,1)S(1)} %pad_maximum_fusion.11), channel_id=1, source_target_pairs={{0,16},{2,18},{4,20},{6,22},{8,24},{10,26},{12,28},{14,30},{16,0},... | collective-permute-start | bytes 172040 | tf_op jit(solution)/shard_map/ppermute | solution.py:20
  75.8 4.9 %collective-permute-start.15 = (f32[16,512]{1,0:T(8,128)S(1)}, f32[16,512]{1,0:T(8,128)S(1)}, u32[]{:S(2)}, u32[]{:S(2)}) collective-permute-start(f32[16,512]{1,0:T(8,128)S(1)} %add.326), channel_id=1, source_target_pairs={{0,16},{2,18},{4,20},{6,22},{8,24},{10,26},{12,28},{14,30},{16,0},... | collective-permute-start | bytes 98312 | tf_op jit(solution)/shard_map/ppermute | solution.py:20
  78.3 4.8 %collective-permute-start.14 = (f16[112,512]{1,0:T(8,128)(2,1)S(1)}, f16[112,512]{1,0:T(8,128)(2,1)S(1)}, u32[]{:S(2)}, u32[]{:S(2)}) collective-permute-start(f16[112,512]{1,0:T(8,128)(2,1)S(1)} %constant_dynamic-update-slice_fusion.6), channel_id=1, source_target_pairs={{0,8},{2,10},{4,12},{6,14},{8,0},{10,2},{12,4},{14,6},{16,24},{18,... | collective-permute-start | bytes 344072 | tf_op jit(solution)/shard_map/ppermute | solution.py:20
  80.7 8.7 %copy-start.11 = (f32[16,512]{1,0:T(8,128)}, f32[16,512]{1,0:T(8,128)S(1)}, u32[]{:S(2)}) copy-start(f32[16,512]{1,0:T(8,128)S(1)} %add.329) | copy-start | bytes 98308
  83.1 6.1 %collective-permute-start.16 = (f16[224,512]{1,0:T(8,128)(2,1)S(1)}, f16[224,512]{1,0:T(8,128)(2,1)S(1)}, u32[]{:S(2)}, u32[]{:S(2)}) collective-permute-start(f16[224,512]{1,0:T(8,128)(2,1)S(1)} %constant_dynamic-update-slice_fusion.4), channel_id=1, source_target_pairs={{0,4},{2,6},{4,0},{6,2},{8,12},{10,14},{12,8},{14,10},{16,20},{18,... | collective-permute-start | bytes 688136 | tf_op jit(solution)/shard_map/ppermute | solution.py:20
  89.2 1.9 %collective-permute-start.17 = (f16[448,512]{1,0:T(8,128)(2,1)S(1)}, f16[448,512]{1,0:T(8,128)(2,1)S(1)}, u32[]{:S(2)}, u32[]{:S(2)}) collective-permute-start(f16[448,512]{1,0:T(8,128)(2,1)S(1)} %constant_dynamic-update-slice_fusion.2), channel_id=1, source_target_pairs={{0,2},{2,0},{4,6},{6,4},{8,10},{10,8},{12,14},{14,12},{16,18},{18,... | collective-permute-start | bytes 1376264 | tf_op jit(solution)/shard_map/ppermute | solution.py:20
  91.3 1.1 %copy-start.1 = (f32[768,512]{1,0:T(8,128)}, f32[768,512]{1,0:T(8,128)S(1)}, u32[]{:S(2)}) copy-start(f32[768,512]{1,0:T(8,128)S(1)} %constant_dynamic-update-slice_fusion) | copy-start | bytes 4718596
  (3 other events, 2.2 us)

commit v3 on v2

v3 whole, which is shorter than its diff:
```python
import functools

import jax
import jax.numpy as jnp
from jax import lax
from jax.experimental import pallas as pl
from jax.experimental.pallas import tpu as pltpu
from jax.sharding import PartitionSpec as P

epsilon = 1e-05
HIGHEST = lax.Precision.HIGHEST


def tie(*values):
    return lax.optimization_barrier(values)


def power_of_two(value):
    return value & (value - 1) == 0


def swap(values, axis_name, mask):
    size = lax.axis_size(axis_name)
    return lax.ppermute(values, axis_name, [(i, i ^ mask) for i in range(size)])


def part_of(values, index, count):
    size = values.shape[0] // count
    return lax.dynamic_slice_in_dim(values, index * size, size, axis=0)


def scaled_rows(values):
    bound = jnp.max(jnp.abs(values), axis=0, keepdims=True)
    exponent = jnp.ceil(jnp.log2(jnp.maximum(bound, 1e-30)))
    values = values * jnp.exp2(14.0 - exponent)
    upper = lax.reduce_precision(values, 5, 10)
    return jnp.concatenate([upper, (values - upper) * 2048.0], axis=0), exponent


def packed(values, exponent, small=None):
    note = jnp.broadcast_to(exponent, (8, values.shape[1]))
    (scale,) = tie(jnp.exp2(14.0 - exponent))
    parts = [values * scale, note]
    if small is not None:
        rows, small_exponent = scaled_rows(small)
        parts[1] = jnp.where(jnp.arange(8)[:, None] == 0, note, small_exponent)
        parts.append(rows)
    return jnp.concatenate(parts, axis=0).astype(jnp.float16)


def opened_small(message, rows):
    exponent = message[rows : rows + 8].astype(jnp.float32)[1:2]
    parts = message[rows + 8 :].astype(jnp.float32)
    count = parts.shape[0] // 2
    return (parts[:count] + parts[count:] * 2.0**-11) * jnp.exp2(exponent - 14.0)


def exchanged_small(sent, received, rows):
    return opened_small(sent, rows) + opened_small(received, rows)


def opened(message, rows):
    exponent = message[rows : rows + 8].astype(jnp.float32)[:1]
    (scale,) = tie(jnp.exp2(exponent - 14.0))
    return message[:rows].astype(jnp.float32) * scale, exponent


def added(total, exponent, message):
    rows = total.shape[0]
    received = message[rows : rows + 8].astype(jnp.float32)[:1]
    scale, larger = tie(jnp.exp2(received - 14.0), jnp.maximum(received, exponent) + 1.0)
    return total + message[:rows].astype(jnp.float32) * scale, larger


def half_of(total, axis_name, mask, other=False):
    bit = jnp.minimum(lax.axis_index(axis_name) & mask, 1)
    return part_of(total, 1 - bit if other else bit, 2)


def gather_pair(values, received, axis_name, mask):
    bit = jnp.minimum(lax.axis_index(axis_name) & mask, 1)
    size = values.shape[0]
    whole = jnp.zeros((2 * size,) + values.shape[1:], values.dtype)
    whole = lax.dynamic_update_slice_in_dim(whole, values, bit * size, axis=0)
    return lax.dynamic_update_slice_in_dim(whole, received, (1 - bit) * size, axis=0)


def gelu_share(values):
    return 0.5 * lax.erf(values * 0.5**0.5) + 0.5


def gelu_slope(values):
    return gelu_share(values) + values * jnp.exp(-0.5 * values * values) * 0.3989422804014327


def row_mean(values):
    return jnp.sum(values, axis=-1, keepdims=True) * (1.0 / values.shape[-1])


def first_raw(windows, weight):
    return jnp.dot(
        windows[...],
        weight[...],
        precision=HIGHEST,
        preferred_element_type=jnp.float32,
    )


def unit_of(raw):
    centered = raw - row_mean(raw)
    scale = lax.rsqrt(row_mean(centered * centered) + epsilon)
    return centered * scale, scale


def blocks_of(total, size):
    return [slice(start, min(start + size, total)) for start in range(0, total, size)]


def folded(values):
    return jnp.sum(values.reshape(-1, 8, values.shape[-1]), axis=0)


def first_kernel(windows, weight, vectors, act, raw):
    raw[...] = first_raw(windows, weight)
    gains, shifts = vectors[0:1, :], vectors[1:2, :]
    for rows in blocks_of(raw.shape[0], 80):
        normed = unit_of(raw[rows, :])[0] * gains + shifts
        act[rows, :] = (normed * gelu_share(normed)).astype(jnp.bfloat16)


def first_layer(windows, weight, vectors):
    shape = (windows.shape[0], weight.shape[1])
    return pl.pallas_call(
        first_kernel,
        out_shape=jax.ShapeDtypeStruct(shape, jnp.bfloat16),
        scratch_shapes=[pltpu.VMEM(shape, jnp.float32)],
        compiler_params=pltpu.CompilerParams(vmem_limit_bytes=4 << 20),
    )(windows, weight, vectors)


def back_kernel(
    windows, windows_across, first_weight, vectors, weight, padded, sums, small, raw, grad
):
    later_rows = raw.shape[0] - padded.shape[0]
    even_rows, channels = padded.shape
    step = even_rows - later_rows
    raw[...] = first_raw(windows, first_weight)

    def pulled(values, tap):
        return lax.dot_general(
            values,
            weight[tap * channels : (tap + 1) * channels, :],
            (((1,), (1,)), ((), ())),
            preferred_element_type=jnp.float32,
        )

    values = padded[...]
    latest = pulled(values, 2)
    grad[:even_rows, :] = pulled(values, 0)
    grad[step:even_rows, :] += latest[:later_rows]
    grad[even_rows:, :] = pulled(values, 1)[:later_rows]
    gains, shifts = vectors[0:1, :], vectors[1:2, :]
    gain_sum = jnp.zeros((8, channels), jnp.float32)
    shift_sum = jnp.zeros((8, channels), jnp.float32)
    for rows in blocks_of(raw.shape[0], 40):
        unit, scale = unit_of(raw[rows, :])
        grad_out = grad[rows, :] * gelu_slope(unit * gains + shifts)
        grad_unit = grad_out * gains
        grad[rows, :] = scale * (
            grad_unit - row_mean(grad_unit) - unit * row_mean(grad_unit * unit)
        )
        gain_sum += folded(grad_out * unit)
        shift_sum += folded(grad_out)
    taps = windows_across.shape[0]
    small[:taps, :] = jnp.dot(
        windows_across[...], grad[...], precision=HIGHEST, preferred_element_type=jnp.float32
    )
    small[taps : taps + 1, :] = jnp.sum(gain_sum, axis=0, keepdims=True)
    small[taps + 1 : taps + 2, :] = jnp.sum(shift_sum, axis=0, keepdims=True)
    small[taps + 2 :, :] = sums[:4, :]


def backward(windows, windows_across, first_weight, vectors, weight, padded, sums):
    frames, channels = windows.shape[0], vectors.shape[1]
    return pl.pallas_call(
        back_kernel,
        out_shape=jax.ShapeDtypeStruct((windows.shape[1] + 6, channels), jnp.float32),
        scratch_shapes=[pltpu.VMEM((frames, channels), jnp.float32)] * 2,
        compiler_params=pltpu.CompilerParams(vmem_limit_bytes=8 << 20),
    )(windows, windows_across, first_weight, vectors, weight, padded, sums)


def head_kernel(groups, place, act, *refs):
    *weights, target, valid, vectors = refs[:-8]
    weight_out, padded, logvar, sums, message, weight, grad, semaphore = refs[-8:]
    later_rows, channels = target.shape[0], vectors.shape[1]
    even_rows = padded.shape[0]
    step = even_rows - later_rows
    depth = weight.shape[0]
    half = depth // groups // 2
    group, core = place[0], place[1]
    if len(weights) == 1:
        places = [slice(None)]
    else:
        base = (1 - group) * 2 * half
        places = [
            pl.ds(pl.multiple_of(group * 2 * half, half), 2 * half),
            pl.ds(pl.multiple_of(base + core * half, half), half),
            pl.ds(pl.multiple_of(base + (1 - core) * half, half), half),
        ]
    copies = [
        pltpu.make_async_copy(source, weight.at[rows, :], semaphore.at[index])
        for index, (source, rows) in enumerate(zip(weights, places))
    ]
    for copy in copies:
        copy.start()
    for copy in copies:
        copy.wait()
    copy = pltpu.make_async_copy(weight, weight_out, semaphore.at[3])
    copy.start()

    def matmul(left, right):
        return jnp.dot(left, right, preferred_element_type=jnp.float32)

    even, odd = act[:even_rows, :], act[even_rows:, :]
    latest = matmul(even, weight[2 * channels :, :])
    grad[:later_rows, :] = (
        matmul(even, weight[:channels, :])[:later_rows]
        + matmul(odd, weight[channels : 2 * channels, :])
        + latest[step:]
    )
    gains, shifts = vectors[2:3, :], vectors[3:4, :]
    block = 3 * step if later_rows % (3 * step) == 0 else step
    last = jnp.concatenate([valid[...]] * (block // step), axis=0)
    times = lax.broadcasted_iota(jnp.int32, (block, 1), 0)
    gain_sum = jnp.zeros((8, channels), jnp.float32)
    shift_sum = jnp.zeros((8, channels), jnp.float32)
    largest = jnp.zeros((8, channels), jnp.float32)
    loss_sum = jnp.zeros((block, 1), jnp.float32)
    count = jnp.zeros((block, 1), jnp.float32)
    for rows in blocks_of(later_rows, block):
        unit, scale = unit_of(grad[rows, :])
        normed = unit * gains + shifts
        share = gelu_share(normed)
        slope = share + normed * (jnp.exp(-0.5 * normed * normed) * 0.3989422804014327)
        active = normed * share
        active = active - row_mean(active)
        variance = row_mean(active * active) + epsilon
        raw_logvar = jnp.log(variance)
        frame_mask = jnp.where(times + rows.start < last, 1.0, 0.0)
        logvar[rows, :] = raw_logvar * frame_mask
        misfit = raw_logvar - target[rows, :]
        weighted = frame_mask * misfit
        loss_sum += weighted * misfit
        count += frame_mask
        grad_out = weighted / variance * (4.0 / channels) * active * slope
        grad_unit = grad_out * gains
        result = scale * (grad_unit - row_mean(grad_unit) - unit * row_mean(grad_unit * unit))
        gain_sum += folded(grad_out * unit)
        shift_sum += folded(grad_out)
        largest = jnp.maximum(
            largest, jnp.max(jnp.abs(result).reshape(-1, 8, channels), axis=0)
        )
        grad[rows, :] = result
    sums[0:1, :] = jnp.sum(gain_sum, axis=0, keepdims=True)
    sums[1:2, :] = jnp.sum(shift_sum, axis=0, keepdims=True)
    sums[2:3, :] = jnp.broadcast_to(jnp.sum(loss_sum, axis=0, keepdims=True), (1, channels))
    sums[3:4, :] = jnp.broadcast_to(jnp.sum(count, axis=0, keepdims=True), (1, channels))
    sums[4:8, :] = jnp.zeros((4, channels), jnp.float32)
    patch_bound = channels**0.5 * jnp.max(
        jnp.abs(vectors[0:1, :]), axis=1, keepdims=True
    ) + jnp.max(jnp.abs(vectors[1:2, :]), axis=1, keepdims=True)
    grad[later_rows:, :] = jnp.zeros((step, channels), jnp.float32)
    padded[...] = grad[...].astype(jnp.bfloat16)
    bound = jnp.max(largest, axis=0, keepdims=True) * 1.01 * (later_rows * patch_bound)
    exponent = jnp.ceil(jnp.log2(jnp.maximum(bound, 1e-30)))
    sums[8:, :] = jnp.broadcast_to(exponent, (8, channels))
    middle = channels // 2
    away = pl.ds(pl.multiple_of((1 - core) * middle, middle), middle)
    message[:even_rows, :] = grad[:, away].astype(jnp.bfloat16)
    message[even_rows:, :] = sums[8:, away].astype(jnp.bfloat16)
    copy.wait()


def head(groups, place, act, weights, target, valid, vectors):
    channels = act.shape[1]
    depth = 3 * channels
    later_rows = target.shape[0]
    even_rows = act.shape[0] - later_rows
    shapes = [
        pltpu.HBM((depth, channels), jnp.bfloat16),
        pltpu.VMEM((even_rows, channels), jnp.bfloat16),
        pltpu.HBM((later_rows, 1), jnp.float32),
        pltpu.VMEM((16, channels), jnp.float32),
        pltpu.VMEM((even_rows + 8, channels // 2), jnp.bfloat16),
    ]
    weights = [pltpu.with_memory_space_constraint(part, pltpu.HBM) for part in weights]
    arrays = [act, *weights, target, valid, vectors]
    return pl.pallas_call(
        functools.partial(head_kernel, groups),
        out_shape=shapes,
        in_specs=[
            pl.BlockSpec(memory_space=pltpu.SMEM),
            pl.BlockSpec(memory_space=pltpu.VMEM),
        ]
        + [pl.BlockSpec(memory_space=pl.ANY)] * len(weights)
        + [pl.BlockSpec(memory_space=pltpu.VMEM)] * 3,
        out_specs=[pl.BlockSpec(memory_space=pltpu.HBM)]
        + [pl.BlockSpec(memory_space=pltpu.VMEM)] * (len(shapes) - 1),
        scratch_shapes=[
            pltpu.VMEM((depth, channels), jnp.bfloat16),
            pltpu.VMEM((even_rows, channels), jnp.float32),
            pltpu.SemaphoreType.DMA((4,)),
        ],
        compiler_params=pltpu.CompilerParams(vmem_limit_bytes=8 << 20),
    )(place, *arrays)


def split_kernel(
    groups,
    place,
    own_act,
    other_act,
    own_grad,
    received,
    own_note,
    near_message,
    near_kept,
    far_message,
    far_kept,
    note,
    product,
):
    depth, middle = product.shape
    even_rows = own_grad.shape[0]
    later_rows = own_act.shape[0] - even_rows
    step, channels = even_rows - later_rows, own_act.shape[1]
    quarter = middle // 2
    core, bit, side = place[0], place[1], place[2]
    columns = pl.ds(pl.multiple_of(core * middle, middle), middle)

    def outer(left, right):
        return lax.dot_general(
            left, right, (((0,), (0,)), ((), ())), preferred_element_type=jnp.float32
        )

    def shifted(values):
        values = values[:later_rows].astype(jnp.float32)
        zeros = jnp.zeros((step, middle), jnp.float32)
        return jnp.concatenate([zeros, values], axis=0).astype(jnp.bfloat16)

    own, other = own_grad[:, columns], received[:even_rows, :]
    own_even, own_odd = own_act[:even_rows, :], own_act[even_rows:, :]
    other_even, other_odd = other_act[:even_rows, :], other_act[even_rows:, :]
    product[:channels, :] = outer(own_even, own) + outer(other_even, other)
    product[channels : 2 * channels, :] = outer(own_odd, own[:later_rows]) + outer(
        other_odd, other[:later_rows]
    )
    product[2 * channels :, :] = outer(own_even, shifted(own)) + outer(other_even, shifted(other))

    larger = jnp.maximum(own_note[8:, columns], received[even_rows:, :].astype(jnp.float32)) + 1.0
    note[...] = larger
    near, far = slice(0, quarter), slice(quarter, middle)
    stay, size = depth // 2, depth // groups
    cut = size // 2
    near_message[:stay, :] = product[
        pl.ds(pl.multiple_of((1 - bit) * stay, 16), stay), near
    ].astype(jnp.bfloat16)
    near_message[stay:, :] = larger[:, near].astype(jnp.bfloat16)
    far_message[stay:, :] = larger[:, far].astype(jnp.bfloat16)
    for index in range(groups):
        rows = slice(index * cut, (index + 1) * cut)
        away = pl.ds(pl.multiple_of(index * size + (1 - side) * cut, 16), cut)
        far_message[rows, :] = product[away, far].astype(jnp.bfloat16)
        far_kept[rows, :] = product[pl.ds(pl.multiple_of(index * size + side * cut, 16), cut), far]
    near_kept[...] = product[pl.ds(pl.multiple_of(bit * stay, 16), stay), near]


def split(groups, place, own_act, other_act, own_grad, received, note):
    channels = own_act.shape[1]
    depth, quarter = 3 * channels, channels // 4
    message = jax.ShapeDtypeStruct((depth // 2 + 8, quarter), jnp.bfloat16)
    part = jax.ShapeDtypeStruct((depth // 2, quarter), jnp.float32)
    shapes = [message, part, message, part, jax.ShapeDtypeStruct((8, 2 * quarter), jnp.float32)]
    return pl.pallas_call(
        functools.partial(split_kernel, groups),
        out_shape=shapes,
        in_specs=[pl.BlockSpec(memory_space=pltpu.SMEM)]
        + [pl.BlockSpec(memory_space=pltpu.VMEM)] * 5,
        out_specs=[pl.BlockSpec(memory_space=pltpu.VMEM)] * len(shapes),
        scratch_shapes=[pltpu.VMEM((depth, 2 * quarter), jnp.float32)],
        compiler_params=pltpu.CompilerParams(vmem_limit_bytes=8 << 20),
    )(place, own_act, other_act, own_grad, received, note)


def added_plain(total, exponent, message):
    rows = total.shape[0]
    received = message[rows : rows + 8].astype(jnp.float32)[:1]
    (larger,) = tie(jnp.maximum(received, exponent) + 1.0)
    return total + message[:rows].astype(jnp.float32), larger


def per_device(
    waveform,
    lengths,
    owner_of,
    targets,
    first_weight,
    first_gain,
    first_shift,
    second_weight,
    second_gain,
    second_shift,
):
    peers, groups = lax.axis_size("dp"), lax.axis_size("fsdp")
    rows, samples = waveform.shape
    later = targets.shape[1]
    frames = samples // 5 - 1
    channels = first_weight.shape[1]
    staged = power_of_two(peers) and power_of_two(groups) and peers >= 4 and groups > 1
    core, side = lax.axis_index("dp") % 2, lax.axis_index("dp") // 2 % 2

    vectors = jnp.stack([first_gain, first_shift, second_gain, second_shift] * 2)

    fetched = None
    if staged and groups == 2:
        fetched = swap(part_of(second_weight, core, 2), "fsdp", 1)

    width = samples + 1
    noted = jnp.concatenate([waveform, lengths.astype(jnp.float32)[:, None]], axis=1)
    per_owner = max(1, 2 * rows // peers)
    matches = (owner_of[:, None] == owner_of[None, :]).astype(jnp.int32)
    slots = owner_of * per_owner + jnp.sum(jnp.tril(matches, -1), axis=1)
    placing = slots[:, None] == jnp.arange(peers * per_owner, dtype=jnp.int32)[None, :]
    sent = lax.dot_general(
        placing.astype(jnp.float32),
        noted,
        (((0,), (0,)), ((), ())),
        precision=HIGHEST,
        preferred_element_type=jnp.float32,
    )
    got = lax.all_to_all(sent, "dp", split_axis=0, concat_axis=0, tiled=True)
    if fetched is not None:
        got, fetched, vectors = tie(got, fetched, vectors)
        fetched_others = swap(fetched, "dp", 1)
    present = got[:, samples] > 0.5
    arrival = jnp.cumsum(present.astype(jnp.int32)) - 1
    picking = present[None, :] & (
        arrival[None, :] == jnp.arange(rows, dtype=jnp.int32)[:, None]
    )
    owned = jnp.dot(
        picking.astype(jnp.float32), got, precision=HIGHEST, preferred_element_type=jnp.float32
    )
    waveform, lengths = owned[:, :samples], owned[:, samples].astype(jnp.int32)

    blocks = waveform.reshape(rows, later + 1, 2, 5).transpose(1, 2, 0, 3)
    earlier_block, later_block = blocks[:, 0], blocks[:, 1]
    windows = jnp.concatenate(
        [
            jnp.concatenate([earlier_block, later_block], axis=2),
            jnp.concatenate([later_block[:later], earlier_block[1:]], axis=2),
        ],
        axis=0,
    ).reshape(frames * rows, 10)
    if fetched is None:
        weights = [lax.all_gather(second_weight, "fsdp", axis=0, tiled=True)]
    else:
        weights = [second_weight, fetched, fetched_others]
    first = (first_weight, vectors)
    windows_across = windows.T
    act = first_layer(windows, *first)
    if staged:
        act_other = swap(act, "dp", 1)

    first_valid = (lengths - 10) // 5 + 1
    second_valid = ((first_valid - 3) // 2 + 1) * rows
    weight, padded, flat_logvar, sums, message = head(
        groups,
        jnp.stack([lax.axis_index("fsdp"), core]),
        act,
        weights,
        targets.T.reshape(later * rows, 1),
        second_valid[:, None],
        vectors,
    )

    if staged:
        group_rows = 3 * channels // groups
        middle, quarter = channels // 2, channels // 4
        strides = [1 << bit for bit in range(2, peers.bit_length() - 1)]
        group_strides = [1 << bit for bit in range(groups.bit_length() - 2, -1, -1)]
        top = group_strides[0]
        received = swap(message, "dp", 1)
        bit = jnp.minimum(lax.axis_index("fsdp") & top, 1)
        near_message, near, far_message, far, note = split(
            groups, jnp.stack([core, bit, side]), act, act_other, padded, received, sums
        )
        near_exponent, far_exponent = note[:1, :quarter], note[:1, quarter:]
        padded, near_message, far_message = tie(padded, near_message, far_message)
        small = backward(windows, windows_across, *first, weight, padded, sums)
        far, far_exponent = added_plain(far, far_exponent, swap(far_message, "dp", 2))
        received = swap(near_message, "fsdp", top)
        near, near_exponent = added_plain(near, near_exponent, received)
        for mask in group_strides[1:]:
            near_message = packed(half_of(near, "fsdp", mask, True), near_exponent)
            received = swap(near_message, "fsdp", mask)
            near, near_exponent = added(half_of(near, "fsdp", mask), near_exponent, received)
        near_message = packed(half_of(near, "dp", 2, True), near_exponent)
        small = jnp.concatenate(
            [small[:, start : start + quarter] for start in range(0, channels, quarter)], axis=0
        )
        for mask in group_strides:
            sent = half_of(far, "fsdp", mask, True)
            far_message = packed(sent, far_exponent, small)
            near_message, far_message = tie(near_message, far_message)
            received = swap(far_message, "fsdp", mask)
            small = exchanged_small(far_message, received, sent.shape[0])
            far, far_exponent = added(half_of(far, "fsdp", mask), far_exponent, received)
        received = swap(near_message, "dp", 2)
        near, near_exponent = added(half_of(near, "dp", 2), near_exponent, received)
        total = jnp.concatenate([near, far], axis=1)
        exponent = jnp.concatenate([near_exponent, far_exponent], axis=1)
        count = small.shape[0] // 2
        small = jnp.concatenate([small[:count], small[count:]], axis=1)

        for mask in strides[:-1]:
            sent = half_of(total, "dp", mask, True)
            message = packed(sent, exponent, small)
            received = swap(message, "dp", mask)
            small = exchanged_small(message, received, sent.shape[0])
            total, exponent = added(half_of(total, "dp", mask), exponent, received)
        piece = total.shape[0]
        for mask in strides[-1:]:
            message = packed(total, exponent, small)
            received = swap(message, "dp", mask)
            small = exchanged_small(message, received, piece)
            total, exponent = opened(message, piece)
            total, exponent = added(total, exponent, received)
        message = packed(total, exponent)
        small = small + swap(small, "dp", 1)
        for mask in strides[-2::-1]:
            message = gather_pair(message, swap(message, "dp", mask), "dp", mask)

        rows_sent = message.shape[0]
        extra, small_exponent = scaled_rows(small)
        small_exponent = jnp.broadcast_to(small_exponent, (8, middle))
        extra = jnp.concatenate([small_exponent, extra], axis=0)
        sent = jnp.concatenate([message, extra.astype(jnp.float16)], axis=0)
        received = swap(sent, "dp", 2)
        small = exchanged_small(sent, received, rows_sent)
        message = gather_pair(message, received[:rows_sent], "dp", 2)
        other_message = swap(message, "dp", 1)
        count = small.shape[0] // 2
        small = jnp.concatenate(
            [
                small[start : start + count, place : place + quarter]
                for place in (0, quarter)
                for start in (0, count)
            ],
            axis=1,
        )

        def opened_blocks(blocks):
            blocks = blocks.reshape(-1, piece + 8, middle)
            (scale,) = tie(jnp.exp2(blocks[:, piece:, :].astype(jnp.float32)[:, :1] - 14.0))
            return (blocks[:, :piece].astype(jnp.float32) * scale).reshape(group_rows, middle)

        gradient = jnp.zeros((group_rows, channels), jnp.float32)
        gradient = lax.dynamic_update_slice_in_dim(
            gradient, opened_blocks(message), core * middle, axis=1
        )
        grad_weight_two = lax.dynamic_update_slice_in_dim(
            gradient, opened_blocks(other_message), (1 - core) * middle, axis=1
        )
    else:
        even, odd = act[: padded.shape[0]], act[padded.shape[0] :]
        zeros = jnp.zeros((rows, channels), padded.dtype)
        shifted = jnp.concatenate([zeros, padded[: later * rows]], axis=0)
        pairs = [(even, padded), (odd, padded[: later * rows]), (even, shifted)]
        partial = [
            lax.dot_general(
                left, right, (((0,), (0,)), ((), ())), preferred_element_type=jnp.float32
            )
            for left, right in pairs
        ]
        partial = jnp.concatenate(partial, axis=0)
        partial = lax.psum_scatter(partial, "fsdp", scatter_dimension=0, tiled=True)
        grad_weight_two = lax.psum(partial, "dp")
        small = backward(windows, windows_across, *first, weight, padded, sums)
        small = lax.psum(small, ("dp", "fsdp"))

    logvar = flat_logvar.reshape(later, rows).T
    loss = small[14, 0] / small[15, 0]
    return (logvar, loss, grad_weight_two, small[:10], small[10], small[11], small[12], small[13])


def solution(mesh):
    placed = (
        P(("dp", "fsdp"), None),
        P(("dp", "fsdp")),
        P(("dp", "fsdp")),
        P(("dp", "fsdp"), None),
        P(),
        P(),
        P(),
        P("fsdp", None),
        P(),
        P(),
    )
    return jax.shard_map(
        per_device,
        mesh=mesh,
        in_specs=placed,
        out_specs=(P(("dp", "fsdp"), None), P(), P("fsdp", None), P(), P(), P(), P(), P()),
        check_vma=False,
    )
```

time: 94.2 us -> 85.1 us (0.903)
  other arithmetic: 19.3 us -> 5.85 us
  Pallas kernels: 0 us -> 11.1 us
  waiting for transfers between devices: 26.3 us -> 36.1 us
  starting transfers between devices: 24.1 us -> 16.1 us
  matrix products: 7.94 us -> 1.11 us
  between operations: 5.31 us -> 3.74 us
    pallas_call x0 -> x4, Pallas kernels: none -> 11.1 us  [the longest x1 4.33 us: head(): pl.pallas_call(functools.partial(head_kernel, groups), out_shape=shapes,...]
    ppermute x18 -> x14, starting transfers between devices: 18.1 us -> 10.2 us  [swap(): return lax.ppermute(values, axis_name, [(i, i ^ mask) for i in range(size)])]
    dot_general x5 -> x0, matrix products: 6.83 us -> none  [the longest x1 2.47 us: per_device(): second_pre = jnp.dot(patches, weight, preferred_element_type=jnp.float32)]
    ppermute x18 -> x14, waiting for transfers between devices: 24.4 us -> 30.3 us  [swap(): return lax.ppermute(values, axis_name, [(i, i ^ mask) for i in range(size)])]
    reduce_sum x7 -> x0, other arithmetic: 3.95 us -> none  [the longest x2 2.07 us: norm_pull(): jnp.sum(grad_out * unit, axis=0)]
    all_to_all x1, waiting for transfers between devices: 1.88 us -> 5.79 us  [per_device(): got = lax.all_to_all(sent, 'dp', split_axis=0, concat_axis=0, tiled=True)]
    reduce_max x3 -> x4, other arithmetic: 2.85 us -> 0.1 us  [scaled_rows(): bound = jnp.max(jnp.abs(values), axis=0, keepdims=True)]
    add x12 -> x8, other arithmetic: 2.68 us -> 0.19 us  [the longest x2 0.09 us: added_plain(): return (total + message[:rows].astype(jnp.float32), larger)]
  transfers between devices with their start and end apart: 19 -> 15, of which waited for: 17 -> 11; matrix products, arithmetic and copies ran while one was open for 19% -> 10% of each run, Pallas kernels for 0% -> 9%
where the time goes in v3:
time: 85.1 us; the launch traced here: 84.6 us
  waiting for transfers between devices  36.1 us (42%)
  starting transfers between devices  16.1 us (19%)
  Pallas kernels  11.1 us (13%)
  local copies, waits for them, and re-layouts  10.6 us (12%)
  other arithmetic  5.85 us (7%)
  between operations  3.74 us (4%)
  matrix products  1.11 us (1%)
    ppermute x14, waiting for transfers between devices, swap(): return lax.ppermute(values, axis_name, [(i, i ^ mask) for i in range(size)])  30.3 us
    ppermute x14, starting transfers between devices, swap(): return lax.ppermute(values, axis_name, [(i, i ^ mask) for i in range(size)])  10.2 us
    all_to_all x1, starting transfers between devices, per_device(): got = lax.all_to_all(sent, 'dp', split_axis=0, concat_axis=0, tiled=True)  5.91 us
    all_to_all x1, waiting for transfers between devices, per_device(): got = lax.all_to_all(sent, 'dp', split_axis=0, concat_axis=0, tiled=True)  5.79 us
    unnamed x27, local copies, waits for them, and re-layouts  4.57 us
    pallas_call x1, Pallas kernels, head(): pl.pallas_call(functools.partial(head_kernel, groups), out_shape=shapes,...  4.33 us
    pallas_call x1, Pallas kernels, backward(): pl.pallas_call(back_kernel, out_shape=jax.ShapeDtypeStruct((windows.shape...  3.13 us
    pallas_call x1, Pallas kernels, split(): pl.pallas_call(functools.partial(split_kernel, groups), out_shape=shapes,...  2.04 us
  transfers between devices with their start and end apart: 15, of which 11 were waited for; matrix products, arithmetic and copies ran while one was open for 10% of the time, Pallas kernels for 9%

profile of v3, /device:TPU:0, one launch (start us, length us, event | category | flops | bytes accessed | tf_op | source)
XLA Modules:
  0.0 84.6 jit_solution(16876057420130353930)
XLA Ops:
  0.7 1.0 %constant_dynamic-slice_fusion = bf16[384,512]{1,0:T(8,128)(2,1)S(1)} fusion(bf16[768,512]{1,0:T(8,128)(2,1)} %refs_0_.1, s32[]{:T(128)S(6)} %select_n.81), kind=kLoop, calls=%fused_computation.130 | loop fusion | bytes 786436 | tf_op jit(solution)/shard_map/dynamic_slice | solution.py:29
  1.7 3.1 %collective-permute-start = (bf16[384,512]{1,0:T(8,128)(2,1)S(1)}, bf16[384,512]{1,0:T(8,128)(2,1)S(1)}, u32[]{:S(2)}, u32[]{:S(2)}) collective-permute-start(bf16[384,512]{1,0:T(8,128)(2,1)S(1)} %constant_dynamic-slice_fusion), channel_id=1, source_target_pairs={{0,1},{1,0},{2,3},{3,2},{4,5},{5,4},{6,7},{7,6},{8,9},{9,8},{10,11... | collective-permute-start | bytes 1179656 | tf_op jit(solution)/shard_map/ppermute | solution.py:24
  4.7 0.7 convert_bitcast_fusion.1
  5.5 0.9 %select_reduce_fusion = s32[8]{0:T(128)S(1)} fusion(s32[8]{0:T(128)} %param.12, s32[8]{0:T(128)S(1)} %iota_add_fusion), kind=kLoop, calls=%fused_computation.119 | loop fusion | flops 312 | bytes 96 | tf_op jit(solution)/shard_map/reduce_sum | solution.py:433
  6.4 0.7 add.174
  7.1 1.0 %convolution_bitcast_fusion = f32[16,1,401]{2,0,1:T(8,128)S(1)} fusion(f32[8,1]{1,0:T(8,128)S(1)} %copy.91, f32[8,400]{1,0:T(8,128)} %param.10, s32[8]{0:T(128)S(1)} %add.174), kind=kOutput, calls=%fused_computation | convolution fusion | flops 619272 | bytes 38528 | tf_op jit(solution)/shard_map/dot_general | solution.py:435
  8.0 0.7 copy.92
  8.7 5.9 %all-to-all-start = ((f32[16,1,401]{2,1,0:T(1,128)}), f32[16,1,401]{2,1,0:T(1,128)S(1)}, u32[]{:S(2)}, u32[]{:S(2)}) async-start(f32[16,1,401]{2,1,0:T(1,128)} %copy.92), calls=%async_computation | async-start | bytes 65536 | tf_op jit(solution)/shard_map/all_to_all | solution.py:442
  14.6 0.8 stack.45.vectors.refs_5_
  15.5 5.8 %all-to-all-done = f32[16,1,401]{2,1,0:T(1,128)S(1)} async-done(((f32[16,1,401]{2,1,0:T(1,128)}), f32[16,1,401]{2,1,0:T(1,128)S(1)}, u32[]{:S(2)}, u32[]{:S(2)}) %all-to-all-start) | async-done | bytes 25696 | tf_op jit(solution)/shard_map/all_to_all | solution.py:442
  24.6 1.6 %shard_map.161.act.own_act = bf16[632,512]{1,0:T(8,128)(2,1)S(1)} custom-call(f32[632,10]{1,0:T(8,128)S(1)} %copy.98.windows, f32[10,512]{1,0:T(8,128)S(1)} %copy-done.5, f32[8,512]{1,0:T(8,128)S(1)} %stack.45.vectors.refs_5_), custom_call_target="tpu_custom_call" | custom-call | tf_op jit(solution)/shard_map/pallas_call | solution.py:133
  27.2 1.8 %collective-permute-done.1.refs_2_ = bf16[384,512]{1,0:T(8,128)(2,1)S(1)} collective-permute-done((bf16[384,512]{1,0:T(8,128)(2,1)S(1)}, bf16[384,512]{1,0:T(8,128)(2,1)S(1)}, u32[]{:S(2)}, u32[]{:S(2)}) %collective-permute-start.1) | collective-permute-done | bytes 393248 | tf_op jit(solution)/shard_map/ppermute | solution.py:24
  28.9 0.7 copy-done.9
  29.7 4.3 %shard_map.162 = (bf16[1536,512]{1,0:T(8,128)(2,1)}, bf16[320,512]{1,0:T(8,128)(2,1)S(1)}, f32[312,1]{1,0:T(8,128)}, f32[16,512]{1,0:T(8,128)S(1)}, bf16[328,256]{1,0:T(8,128)(2,1)}) custom-call(s32[2]{0:T(128)S(1)} %pad_add_fusion.place, bf16[632,512]{1,0:T(8,128)(2,1)S(1)} %shard_map.161.act.own_act, bf16[768,512]{1,0:T(8,128)(2,1)} %refs_0_.1, ...), custom_call_target="tpu_custom_call" | custom-call | tf_op jit(solution)/shard_map/pallas_call | solution.py:299
  34.8 1.5 %collective-permute-done.3.received = bf16[328,256]{1,0:T(8,128)(2,1)} collective-permute-done((bf16[328,256]{1,0:T(8,128)(2,1)}, bf16[328,256]{1,0:T(8,128)(2,1)}, u32[]{:S(2)}, u32[]{:S(2)}) %collective-permute-start.3) | collective-permute-done | bytes 167968 | tf_op jit(solution)/shard_map/ppermute | solution.py:24
  36.4 0.8 copy-done.4
  37.1 2.0 %shard_map.163 = (bf16[776,128]{1,0:T(8,128)(2,1)S(1)}, f32[768,128]{1,0:T(8,128)S(1)}, bf16[776,128]{1,0:T(8,128)(2,1)S(1)}, f32[768,128]{1,0:T(8,128)S(1)}, f32[8,256]{1,0:T(8,128)S(1)}) custom-call(s32[3]{0:T(128)S(1)} %pad_add_fusion.1.place, bf16[632,512]{1,0:T(8,128)(2,1)S(1)} %shard_map.161.act.own_act, ...), custom_call_target="tpu_custom_call" | custom-call | tf_op jit(solution)/shard_map/pallas_call | solution.py:385
  40.1 3.1 %shard_map.164 = f32[16,512]{1,0:T(8,128)S(1)} custom-call(f32[632,10]{1,0:T(8,128)S(1)} %copy.98.windows, f32[10,632]{1,0:T(8,128)S(1)} %bitcast.63, f32[10,512]{1,0:T(8,128)S(1)} %copy-done.6, f32[8,512]{1,0:T(8,128)S(1)} %stack.45.vectors.refs_5_, bf16[1536,512]{1,0:T(8,128)(2,1)S(1)} %copy-done, bf16[320,512]{1,0:T(8,128)(2,1)S(1)} %get-tuple-element.49.own_grad.padded, ...), custom_call_target="tpu_custom_call" | custom-call | tf_op jit(solution)/shard_map/pallas_call | solution.py:185
  43.3 2.9 %collective-permute-done.5 = bf16[776,128]{1,0:T(8,128)(2,1)S(1)} collective-permute-done((bf16[776,128]{1,0:T(8,128)(2,1)S(1)}, bf16[776,128]{1,0:T(8,128)(2,1)S(1)}, u32[]{:S(2)}, u32[]{:S(2)}) %collective-permute-start.5) | collective-permute-done | bytes 198688 | tf_op jit(solution)/shard_map/ppermute | solution.py:24
  47.3 1.7 %collective-permute-start.7 = (f16[392,128]{1,0:T(8,128)(2,1)S(1)}, f16[392,128]{1,0:T(8,128)(2,1)S(1)}, u32[]{:S(2)}, u32[]{:S(2)}) collective-permute-start(f16[392,128]{1,0:T(8,128)(2,1)S(1)} %pad_maximum_fusion.5), channel_id=1, source_target_pairs={{0,4},{2,6},{4,0},{6,2},{8,12},{10,14},{12,8},{14,10},{16,20},{18,... | collective-permute-start | bytes 301064 | tf_op jit(solution)/shard_map/ppermute | solution.py:24
  49.0 3.0 %collective-permute-done.7 = f16[392,128]{1,0:T(8,128)(2,1)S(1)} collective-permute-done((f16[392,128]{1,0:T(8,128)(2,1)S(1)}, f16[392,128]{1,0:T(8,128)(2,1)S(1)}, u32[]{:S(2)}, u32[]{:S(2)}) %collective-permute-start.7) | collective-permute-done | bytes 100384 | tf_op jit(solution)/shard_map/ppermute | solution.py:24
  52.4 0.6 collective-permute-start.8
  53.1 4.4 %collective-permute-done.8 = f16[264,256]{1,0:T(8,128)(2,1)S(1)} collective-permute-done((f16[264,256]{1,0:T(8,128)(2,1)S(1)}, f16[264,256]{1,0:T(8,128)(2,1)S(1)}, u32[]{:S(2)}, u32[]{:S(2)}) %collective-permute-start.8) | collective-permute-done | bytes 135200 | tf_op jit(solution)/shard_map/ppermute | solution.py:24
  57.8 0.7 collective-permute-start.9
  58.5 6.7 %collective-permute-done.9 = f16[264,256]{1,0:T(8,128)(2,1)S(1)} collective-permute-done((f16[264,256]{1,0:T(8,128)(2,1)S(1)}, f16[264,256]{1,0:T(8,128)(2,1)S(1)}, u32[]{:S(2)}, u32[]{:S(2)}) %collective-permute-start.9) | collective-permute-done | bytes 135200 | tf_op jit(solution)/shard_map/ppermute | solution.py:24
  65.6 1.0 %collective-permute-done.10 = f32[32,256]{1,0:T(8,128)S(1)} collective-permute-done((f32[32,256]{1,0:T(8,128)S(1)}, f32[32,256]{1,0:T(8,128)S(1)}, u32[]{:S(2)}, u32[]{:S(2)}) %collective-permute-start.10) | collective-permute-done | bytes 32800 | tf_op jit(solution)/shard_map/ppermute | solution.py:24
  66.7 4.2 %collective-permute-done.11 = f16[200,256]{1,0:T(8,128)(2,1)S(1)} collective-permute-done((f16[200,256]{1,0:T(8,128)(2,1)S(1)}, f16[200,256]{1,0:T(8,128)(2,1)S(1)}, u32[]{:S(2)}, u32[]{:S(2)}) %collective-permute-start.11) | collective-permute-done | bytes 102432 | tf_op jit(solution)/shard_map/ppermute | solution.py:24
  71.0 1.7 %collective-permute-start.12 = (f16[472,256]{1,0:T(8,128)(2,1)S(1)}, f16[472,256]{1,0:T(8,128)(2,1)S(1)}, u32[]{:S(2)}, u32[]{:S(2)}) collective-permute-start(f16[472,256]{1,0:T(8,128)(2,1)S(1)} %pad_maximum_fusion), channel_id=1, source_target_pairs={{0,4},{2,6},{4,0},{6,2},{8,12},{10,14},{12,8},{14,10},{16,20},{18,... | collective-permute-start | bytes 725000 | tf_op jit(solution)/shard_map/ppermute | solution.py:24
  73.0 0.7 copy.104
  73.7 4.7 %collective-permute-done.12 = f16[472,256]{1,0:T(8,128)(2,1)S(1)} collective-permute-done((f16[472,256]{1,0:T(8,128)(2,1)S(1)}, f16[472,256]{1,0:T(8,128)(2,1)S(1)}, u32[]{:S(2)}, u32[]{:S(2)}) %collective-permute-start.12) | collective-permute-done | bytes 241696 | tf_op jit(solution)/shard_map/ppermute | solution.py:24
  79.2 0.6 pad_maximum_fusion.8
  82.4 1.1 %copy-done.7 = f32[768,512]{1,0:T(8,128)} copy-done((f32[768,512]{1,0:T(8,128)}, f32[768,512]{1,0:T(8,128)S(1)}, u32[]{:S(2)}) %copy-start.7) | copy-done | bytes 1572888
  (144 shorter events, 10.4 us)
Async XLA Ops:
  1.7 19.6 %collective-permute-start = (bf16[384,512]{1,0:T(8,128)(2,1)S(1)}, bf16[384,512]{1,0:T(8,128)(2,1)S(1)}, u32[]{:S(2)}, u32[]{:S(2)}) collective-permute-start(bf16[384,512]{1,0:T(8,128)(2,1)S(1)} %constant_dynamic-slice_fusion), channel_id=1, source_target_pairs={{0,1},{1,0},{2,3},{3,2},{4,5},{5,4},{6,7},{7,6},{8,9},{9,8},{10,11... | collective-permute-start | bytes 1179656 | tf_op jit(solution)/shard_map/ppermute | solution.py:24
  8.7 12.6 %all-to-all-start = ((f32[16,1,401]{2,1,0:T(1,128)}), f32[16,1,401]{2,1,0:T(1,128)S(1)}, u32[]{:S(2)}, u32[]{:S(2)}) async-start(f32[16,1,401]{2,1,0:T(1,128)} %copy.92), calls=%async_computation | async-start | bytes 65536 | tf_op jit(solution)/shard_map/all_to_all | solution.py:442
  21.3 5.0 %copy-start.8 = (bf16[384,512]{1,0:T(8,128)(2,1)}, bf16[384,512]{1,0:T(8,128)(2,1)S(1)}, u32[]{:S(2)}) copy-start(bf16[384,512]{1,0:T(8,128)(2,1)S(1)} %collective-permute-done.refs_1_) | copy-start | bytes 1179652
  22.2 2.4 %copy-start.5 = (f32[10,512]{1,0:T(8,128)S(1)}, f32[10,512]{1,0:T(8,128)}, u32[]{:S(2)}) copy-start(f32[10,512]{1,0:T(8,128)} %first_weight.1) | copy-start | bytes 61444
  22.7 4.1 %copy-start.11 = (f32[8,39]{1,0:T(8,128)S(1)}, f32[8,39]{1,0:T(8,128)}, u32[]{:S(2)}) copy-start(f32[8,39]{1,0:T(8,128)} %param.13) | copy-start | bytes 3748
  23.9 0.6 copy-start.1
  26.2 10.2 %collective-permute-start.2 = (bf16[632,512]{1,0:T(8,128)(2,1)S(1)}, bf16[632,512]{1,0:T(8,128)(2,1)S(1)}, u32[]{:S(2)}, u32[]{:S(2)}) collective-permute-start(bf16[632,512]{1,0:T(8,128)(2,1)S(1)} %shard_map.161.act.own_act), channel_id=1, source_target_pairs={{0,2},{2,0},{4,6},{6,4},{8,10},{10,8},{12,14},{14,12},{16,18},{18,... | collective-permute-start | bytes 1941512 | tf_op jit(solution)/shard_map/ppermute | solution.py:24
  26.3 2.6 %collective-permute-start.1 = (bf16[384,512]{1,0:T(8,128)(2,1)S(1)}, bf16[384,512]{1,0:T(8,128)(2,1)S(1)}, u32[]{:S(2)}, u32[]{:S(2)}) collective-permute-start(bf16[384,512]{1,0:T(8,128)(2,1)S(1)} %collective-permute-done.refs_1_), channel_id=1, source_target_pairs={{0,2},{2,0},{4,6},{6,4},{8,10},{10,8},{12,14},{14,12},{16,18},{18,... | collective-permute-start | bytes 1179656 | tf_op jit(solution)/shard_map/ppermute | solution.py:24
  28.9 0.7 copy-start.9
  34.0 0.6 copy-start.3
  34.6 5.5 %copy-start = (bf16[1536,512]{1,0:T(8,128)(2,1)S(1)}, bf16[1536,512]{1,0:T(8,128)(2,1)}, u32[]{:S(2)}) copy-start(bf16[1536,512]{1,0:T(8,128)(2,1)} %get-tuple-element.48.weight) | copy-start | bytes 4718596
  34.6 1.7 %collective-permute-start.3 = (bf16[328,256]{1,0:T(8,128)(2,1)}, bf16[328,256]{1,0:T(8,128)(2,1)}, u32[]{:S(2)}, u32[]{:S(2)}) collective-permute-start(bf16[328,256]{1,0:T(8,128)(2,1)} %get-tuple-element.39), channel_id=1, source_target_pairs={{0,2},{2,0},{4,6},{6,4},{8,10},{10,8},{12,14},{14,12},{16,18},{18,... | collective-permute-start | bytes 503816 | tf_op jit(solution)/shard_map/ppermute | solution.py:24
  34.8 5.3 %copy-start.2 = (f32[632,10]{0,1:T(8,128)S(1)}, f32[632,10]{0,1:T(8,128)}, u32[]{:S(2)}) copy-start(f32[632,10]{0,1:T(8,128)} %copy-done.1) | copy-start | bytes 75844
  36.4 0.8 copy-start.4
  37.1 3.0 %copy-start.6 = (f32[10,512]{1,0:T(8,128)S(1)}, f32[10,512]{1,0:T(8,128)}, u32[]{:S(2)}) copy-start(f32[10,512]{1,0:T(8,128)} %first_weight.1) | copy-start | bytes 61444
  39.2 7.1 %collective-permute-start.5 = (bf16[776,128]{1,0:T(8,128)(2,1)S(1)}, bf16[776,128]{1,0:T(8,128)(2,1)S(1)}, u32[]{:S(2)}, u32[]{:S(2)}) collective-permute-start(bf16[776,128]{1,0:T(8,128)(2,1)S(1)} %get-tuple-element.47), channel_id=1, source_target_pairs={{0,4},{2,6},{4,0},{6,2},{8,12},{10,14},{12,8},{14,10},{16,20},{18,... | collective-permute-start | bytes 595976 | tf_op jit(solution)/shard_map/ppermute | solution.py:24
  39.6 6.7 %collective-permute-start.4 = (bf16[776,128]{1,0:T(8,128)(2,1)S(1)}, bf16[776,128]{1,0:T(8,128)(2,1)S(1)}, u32[]{:S(2)}, u32[]{:S(2)}) collective-permute-start(bf16[776,128]{1,0:T(8,128)(2,1)S(1)} %get-tuple-element.44), channel_id=1, source_target_pairs={{0,1},{1,0},{2,3},{3,2},{4,5},{5,4},{6,7},{7,6},{8,9},{9,8},{10,11... | collective-permute-start | bytes 595976 | tf_op jit(solution)/shard_map/ppermute | solution.py:24
  46.7 5.3 %collective-permute-start.6 = (f16[520,128]{1,0:T(8,128)(2,1)S(1)}, f16[520,128]{1,0:T(8,128)(2,1)S(1)}, u32[]{:S(2)}, u32[]{:S(2)}) collective-permute-start(f16[520,128]{1,0:T(8,128)(2,1)S(1)} %pad_maximum_fusion.3), channel_id=1, source_target_pairs={{0,1},{1,0},{2,3},{3,2},{4,5},{5,4},{6,7},{7,6},{8,9},{9,8},{10,11... | collective-permute-start | bytes 399368 | tf_op jit(solution)/shard_map/ppermute | solution.py:24
  47.3 4.6 %collective-permute-start.7 = (f16[392,128]{1,0:T(8,128)(2,1)S(1)}, f16[392,128]{1,0:T(8,128)(2,1)S(1)}, u32[]{:S(2)}, u32[]{:S(2)}) collective-permute-start(f16[392,128]{1,0:T(8,128)(2,1)S(1)} %pad_maximum_fusion.5), channel_id=1, source_target_pairs={{0,4},{2,6},{4,0},{6,2},{8,12},{10,14},{12,8},{14,10},{16,20},{18,... | collective-permute-start | bytes 301064 | tf_op jit(solution)/shard_map/ppermute | solution.py:24
  52.4 5.1 %collective-permute-start.8 = (f16[264,256]{1,0:T(8,128)(2,1)S(1)}, f16[264,256]{1,0:T(8,128)(2,1)S(1)}, u32[]{:S(2)}, u32[]{:S(2)}) collective-permute-start(f16[264,256]{1,0:T(8,128)(2,1)S(1)} %pad_maximum_fusion.1), channel_id=1, source_target_pairs={{0,8},{2,10},{4,12},{6,14},{8,0},{10,2},{12,4},{14,6},{16,24},{18,... | collective-permute-start | bytes 405512 | tf_op jit(solution)/shard_map/ppermute | solution.py:24
  57.5 15.2 %copy-start.10 = (f32[312,1]{1,0:T(8,128)S(1)}, f32[312,1]{1,0:T(8,128)}, u32[]{:S(2)}) copy-start(f32[312,1]{1,0:T(8,128)} %get-tuple-element.37) | copy-start | bytes 3748
  57.8 7.4 %collective-permute-start.9 = (f16[264,256]{1,0:T(8,128)(2,1)S(1)}, f16[264,256]{1,0:T(8,128)(2,1)S(1)}, u32[]{:S(2)}, u32[]{:S(2)}) collective-permute-start(f16[264,256]{1,0:T(8,128)(2,1)S(1)} %pad_maximum_fusion.2), channel_id=1, source_target_pairs={{0,16},{2,18},{4,20},{6,22},{8,24},{10,26},{12,28},{14,30},{16,0},... | collective-permute-start | bytes 405512 | tf_op jit(solution)/shard_map/ppermute | solution.py:24
  65.3 1.3 %collective-permute-start.10 = (f32[32,256]{1,0:T(8,128)S(1)}, f32[32,256]{1,0:T(8,128)S(1)}, u32[]{:S(2)}, u32[]{:S(2)}) collective-permute-start(f32[32,256]{1,0:T(8,128)S(1)} %fusion.22), channel_id=1, source_target_pairs={{0,2},{2,0},{4,6},{6,4},{8,10},{10,8},{12,14},{14,12},{16,18},{18,... | collective-permute-start | bytes 98312 | tf_op jit(solution)/shard_map/ppermute | solution.py:24
  65.5 5.3 %collective-permute-start.11 = (f16[200,256]{1,0:T(8,128)(2,1)S(1)}, f16[200,256]{1,0:T(8,128)(2,1)S(1)}, u32[]{:S(2)}, u32[]{:S(2)}) collective-permute-start(f16[200,256]{1,0:T(8,128)(2,1)S(1)} %get-tuple-element.130), channel_id=1, source_target_pairs={{0,8},{2,10},{4,12},{6,14},{8,0},{10,2},{12,4},{14,6},{16,24},{18,... | collective-permute-start | bytes 307208 | tf_op jit(solution)/shard_map/ppermute | solution.py:24
  71.0 7.5 %collective-permute-start.12 = (f16[472,256]{1,0:T(8,128)(2,1)S(1)}, f16[472,256]{1,0:T(8,128)(2,1)S(1)}, u32[]{:S(2)}, u32[]{:S(2)}) collective-permute-start(f16[472,256]{1,0:T(8,128)(2,1)S(1)} %pad_maximum_fusion), channel_id=1, source_target_pairs={{0,4},{2,6},{4,0},{6,2},{8,12},{10,14},{12,8},{14,10},{16,20},{18,... | collective-permute-start | bytes 725000 | tf_op jit(solution)/shard_map/ppermute | solution.py:24
  79.1 3.0 %collective-permute-start.13 = (f16[800,256]{1,0:T(8,128)(2,1)S(1)}, f16[800,256]{1,0:T(8,128)(2,1)S(1)}, u32[]{:S(2)}, u32[]{:S(2)}) collective-permute-start(f16[800,256]{1,0:T(8,128)(2,1)S(1)} %slice_dynamic-update-slice_fusion), channel_id=1, source_target_pairs={{0,2},{2,0},{4,6},{6,4},{8,10},{10,8},{12,14},{14,12},{16,18},{18,... | collective-permute-start | bytes 1228808 | tf_op jit(solution)/shard_map/ppermute | solution.py:24
  82.3 1.2 %copy-start.7 = (f32[768,512]{1,0:T(8,128)}, f32[768,512]{1,0:T(8,128)S(1)}, u32[]{:S(2)}) copy-start(f32[768,512]{1,0:T(8,128)S(1)} %constant_dynamic-update-slice_fusion.2) | copy-start | bytes 4718596

commit v4 on v3

--- a/solution.py
+++ b/solution.py
@@ -6,6 +6,7 @@
 from jax.experimental import pallas as pl
 from jax.experimental.pallas import tpu as pltpu
 from jax.sharding import PartitionSpec as P
+
 
 epsilon = 1e-05
 HIGHEST = lax.Precision.HIGHEST
@@ -95,6 +96,62 @@
 
 def row_mean(values):
     return jnp.sum(values, axis=-1, keepdims=True) * (1.0 / values.shape[-1])
+
+
+def placing_kernel(per_owner, owners_in, lengths_in, waveform_in, weight, out, *refs):
+    *pieces, owners, lengths, waveform, semaphores = refs
+    copies = [
+        pltpu.make_async_copy(owners_in, owners, semaphores.at[0]),
+        pltpu.make_async_copy(lengths_in, lengths, semaphores.at[1]),
+        pltpu.make_async_copy(waveform_in, waveform, semaphores.at[2]),
+    ]
+    for piece in pieces:
+        size = piece.shape[0]
+        start = pl.multiple_of(lax.rem(lax.axis_index("dp"), 2) * size, size)
+        copies.append(
+            pltpu.make_async_copy(weight.at[pl.ds(start, size), :], piece, semaphores.at[3])
+        )
+    for copy in copies:
+        copy.start()
+    samples, width = waveform.shape[1], out.shape[2]
+    out[...] = jnp.zeros_like(out)
+    for copy in copies[:3]:
+        copy.wait()
+    for row in range(waveform.shape[0]):
+        slot = owners[row] * per_owner
+        for earlier in range(row if per_owner > 1 else 0):
+            slot += jnp.where(owners[earlier] == owners[row], 1, 0)
+        out[slot, :, :samples] = waveform[row : row + 1, :]
+        length = lengths[row].astype(jnp.float32)
+        out[slot, :, width - 128 :] = jnp.full((1, 128), length, jnp.float32)
+    for copy in copies[3:]:
+        copy.wait()
+
+
+def placed_rows(owners, lengths, waveform, weight, peers, halved):
+    rows, samples = waveform.shape
+    per_owner = max(1, 2 * rows // peers)
+    width = -(-samples // 128) * 128 + 128
+    shapes = [jax.ShapeDtypeStruct((peers * per_owner, 1, width), jnp.float32)]
+    if halved:
+        shapes.append(jax.ShapeDtypeStruct((weight.shape[0] // 2, weight.shape[1]), weight.dtype))
+    arrays = [
+        pltpu.with_memory_space_constraint(array, pltpu.HBM)
+        for array in (owners, lengths, waveform, weight)
+    ]
+    return pl.pallas_call(
+        functools.partial(placing_kernel, per_owner),
+        out_shape=shapes,
+        in_specs=[pl.BlockSpec(memory_space=pl.ANY)] * 4,
+        out_specs=[pl.BlockSpec(memory_space=pltpu.VMEM)] * len(shapes),
+        scratch_shapes=[
+            pltpu.SMEM((rows,), jnp.int32),
+            pltpu.SMEM((rows,), jnp.int32),
+            pltpu.VMEM((rows, samples), jnp.float32),
+            pltpu.SemaphoreType.DMA((4,)),
+        ],
+        compiler_params=pltpu.CompilerParams(vmem_limit_bytes=3 << 20),
+    )(*arrays)
 
 
 def first_raw(windows, weight):
@@ -393,6 +450,43 @@
     )(place, own_act, other_act, own_grad, received, note)
 
 
+def storing_kernel(last, flips, *refs):
+    own, other, out, semaphores = refs[-4:]
+    me = lax.axis_index("dp")
+    core, side, bit = lax.rem(me, 2), lax.rem(me // 2, 2), lax.rem(me // last, 2)
+    size, middle = out.shape[0] // 4, own.shape[1]
+    copies = []
+    for index, (side_flip, bit_flip) in enumerate(flips):
+        block = (side + side_flip - 2 * side * side_flip) * 2 + (bit + bit_flip - 2 * bit * bit_flip)
+        rows = pl.ds(pl.multiple_of(block * size, 8), size)
+        for number, (source, column) in enumerate(((own, core), (other, 1 - core))):
+            columns = pl.ds(pl.multiple_of(column * middle, middle), middle)
+            copies.append(
+                pltpu.make_async_copy(
+                    source.at[index * size : (index + 1) * size, :],
+                    out.at[rows, columns],
+                    semaphores.at[2 * index + number],
+                )
+            )
+    for copy in copies:
+        copy.start()
+    for copy in copies:
+        copy.wait()
+
+
+def stored(last, flips, shape, before, own, other):
+    blocks = [pl.BlockSpec(memory_space=pltpu.VMEM)] * 2
+    return pl.pallas_call(
+        functools.partial(storing_kernel, last, flips),
+        out_shape=pltpu.HBM(shape, jnp.float32),
+        in_specs=[pl.BlockSpec(memory_space=pl.ANY)] * len(before) + blocks,
+        out_specs=pl.BlockSpec(memory_space=pl.ANY),
+        scratch_shapes=[pltpu.SemaphoreType.DMA((2 * len(flips),))],
+        input_output_aliases={0: 0} if before else {},
+        compiler_params=pltpu.CompilerParams(vmem_limit_bytes=3 << 20),
+    )(*before, own, other)
+
+
 def added_plain(total, exponent, message):
     rows = total.shape[0]
     received = message[rows : rows + 8].astype(jnp.float32)[:1]
@@ -417,41 +511,34 @@
     later = targets.shape[1]
     frames = samples // 5 - 1
     channels = first_weight.shape[1]
-    staged = power_of_two(peers) and power_of_two(groups) and peers >= 4 and groups > 1
+    staged = power_of_two(peers) and power_of_two(groups) and peers >= 16 and groups > 1
     core, side = lax.axis_index("dp") % 2, lax.axis_index("dp") // 2 % 2
 
     vectors = jnp.stack([first_gain, first_shift, second_gain, second_shift] * 2)
 
     fetched = None
     if staged and groups == 2:
-        fetched = swap(part_of(second_weight, core, 2), "fsdp", 1)
-
-    width = samples + 1
-    noted = jnp.concatenate([waveform, lengths.astype(jnp.float32)[:, None]], axis=1)
-    per_owner = max(1, 2 * rows // peers)
-    matches = (owner_of[:, None] == owner_of[None, :]).astype(jnp.int32)
-    slots = owner_of * per_owner + jnp.sum(jnp.tril(matches, -1), axis=1)
-    placing = slots[:, None] == jnp.arange(peers * per_owner, dtype=jnp.int32)[None, :]
-    sent = lax.dot_general(
-        placing.astype(jnp.float32),
-        noted,
-        (((0,), (0,)), ((), ())),
-        precision=HIGHEST,
-        preferred_element_type=jnp.float32,
-    )
+        sent, fetched = placed_rows(owner_of, lengths, waveform, second_weight, peers, True)
+        fetched = swap(fetched, "fsdp", 1)
+    else:
+        (sent,) = placed_rows(owner_of, lengths, waveform, second_weight, peers, False)
     got = lax.all_to_all(sent, "dp", split_axis=0, concat_axis=0, tiled=True)
+    got = got.reshape(sent.shape[0], sent.shape[2])
     if fetched is not None:
         got, fetched, vectors = tie(got, fetched, vectors)
         fetched_others = swap(fetched, "dp", 1)
-    present = got[:, samples] > 0.5
+    present = got[:, -1] > 0.5
     arrival = jnp.cumsum(present.astype(jnp.int32)) - 1
     picking = present[None, :] & (
         arrival[None, :] == jnp.arange(rows, dtype=jnp.int32)[:, None]
     )
-    owned = jnp.dot(
-        picking.astype(jnp.float32), got, precision=HIGHEST, preferred_element_type=jnp.float32
-    )
-    waveform, lengths = owned[:, :samples], owned[:, samples].astype(jnp.int32)
+    waveform = jnp.dot(
+        picking.astype(jnp.float32),
+        got[:, :samples],
+        precision=HIGHEST,
+        preferred_element_type=jnp.float32,
+    )
+    lengths = jnp.sum(jnp.where(picking, got[:, -1][None, :], 0.0), axis=1).astype(jnp.int32)
 
     blocks = waveform.reshape(rows, later + 1, 2, 5).transpose(1, 2, 0, 3)
     earlier_block, later_block = blocks[:, 0], blocks[:, 1]
@@ -537,19 +624,32 @@
             total, exponent = opened(message, piece)
             total, exponent = added(total, exponent, received)
         message = packed(total, exponent)
-        small = small + swap(small, "dp", 1)
-        for mask in strides[-2::-1]:
+        for mask in strides[-2:0:-1]:
             message = gather_pair(message, swap(message, "dp", mask), "dp", mask)
 
+        last = strides[0]
         rows_sent = message.shape[0]
-        extra, small_exponent = scaled_rows(small)
-        small_exponent = jnp.broadcast_to(small_exponent, (8, middle))
-        extra = jnp.concatenate([small_exponent, extra], axis=0)
-        sent = jnp.concatenate([message, extra.astype(jnp.float16)], axis=0)
+
+        def extended(message, small):
+            extra, exponent = scaled_rows(small)
+            exponent = jnp.broadcast_to(exponent, (8, middle))
+            extra = jnp.concatenate([exponent, extra], axis=0).astype(jnp.float16)
+            return jnp.concatenate([message, extra], axis=0)
+
+        sent = extended(message, small)
         received = swap(sent, "dp", 2)
+        beside = swap(message, "dp", last)
         small = exchanged_small(sent, received, rows_sent)
-        message = gather_pair(message, received[:rows_sent], "dp", 2)
-        other_message = swap(message, "dp", 1)
+        across = received[:rows_sent]
+        cut = rows_sent // 16 * 8
+        upper = swap(beside[:cut], "dp", 2)
+        lower = swap(across[cut:], "dp", last)
+        early = jnp.concatenate([message, beside, across], axis=0)
+        sent = extended(early, small)
+        received = swap(sent, "dp", 1)
+        small = exchanged_small(sent, received, early.shape[0])
+        early_other = received[: early.shape[0]]
+        corner = jnp.concatenate([upper, lower], axis=0)
         count = small.shape[0] // 2
         small = jnp.concatenate(
             [
@@ -563,14 +663,15 @@
         def opened_blocks(blocks):
             blocks = blocks.reshape(-1, piece + 8, middle)
             (scale,) = tie(jnp.exp2(blocks[:, piece:, :].astype(jnp.float32)[:, :1] - 14.0))
-            return (blocks[:, :piece].astype(jnp.float32) * scale).reshape(group_rows, middle)
-
-        gradient = jnp.zeros((group_rows, channels), jnp.float32)
-        gradient = lax.dynamic_update_slice_in_dim(
-            gradient, opened_blocks(message), core * middle, axis=1
-        )
-        grad_weight_two = lax.dynamic_update_slice_in_dim(
-            gradient, opened_blocks(other_message), (1 - core) * middle, axis=1
+            return (blocks[:, :piece].astype(jnp.float32) * scale).reshape(-1, middle)
+
+        shape = (group_rows, channels)
+        flips = ((0, 0), (0, 1), (1, 0))
+        gradient = stored(last, flips, shape, (), opened_blocks(early), opened_blocks(early_other))
+        corner, gradient = tie(corner, gradient)
+        corner_other = swap(corner, "dp", 1)
+        grad_weight_two = stored(
+            last, ((1, 1),), shape, (gradient,), opened_blocks(corner), opened_blocks(corner_other)
         )
     else:
         even, odd = act[: padded.shape[0]], act[padded.shape[0] :]
@@ -590,7 +691,8 @@
         small = lax.psum(small, ("dp", "fsdp"))
 
     logvar = flat_logvar.reshape(later, rows).T
-    loss = small[14, 0] / small[15, 0]
+    (loss,) = tie(small[14:15] / small[15:16])
+    loss = loss[0, 0]
     return (logvar, loss, grad_weight_two, small[:10], small[10], small[11], small[12], small[13])
 
 
@@ -607,6 +709,7 @@
         P(),
         P(),
     )
+
     return jax.shard_map(
         per_device,
         mesh=mesh,

time: 85.1 us -> 76.8 us (0.902)
  waiting for transfers between devices: 36.1 us -> 30.9 us
  Pallas kernels: 11.1 us -> 14.7 us
  local copies, waits for them, and re-layouts: 10.6 us -> 8.07 us
  between operations: 3.74 us -> 1.38 us
  other arithmetic: 5.85 us -> 3.79 us
  starting transfers between devices: 16.1 us -> 17.5 us
  matrix products: 1.11 us -> 0.13 us
    ppermute x14 -> x16, waiting for transfers between devices: 30.3 us -> 26 us  [swap(): return lax.ppermute(values, axis_name, [(i, i ^ mask) for i in range(size)])]
    pallas_call x0 -> x3, Pallas kernels: none -> 3.53 us  [the longest x2 1.87 us: stored(): pl.pallas_call(functools.partial(storing_kernel, last, flips), out_shape=...]
    ppermute x14 -> x16, starting transfers between devices: 10.2 us -> 11.6 us  [swap(): return lax.ppermute(values, axis_name, [(i, i ^ mask) for i in range(size)])]
    unnamed x27 -> x30, local copies, waits for them, and re-layouts: 4.57 us -> 3.2 us
    dynamic_slice x1 -> x0, local copies, waits for them, and re-layouts: 1.03 us -> none  [part_of(): return lax.dynamic_slice_in_dim(values, index * size, size, axis=0)]
    dot_general x2 -> x1, matrix products: 1.11 us -> 0.13 us  [per_device(): jnp.dot(picking.astype(jnp.float32), got[:, :samples], precision=HIGHEST,...]
    all_to_all x1, waiting for transfers between devices: 5.79 us -> 4.88 us  [per_device(): got = lax.all_to_all(sent, 'dp', split_axis=0, concat_axis=0, tiled=True)]
  transfers between devices with their start and end apart: 15 -> 17, of which waited for: 11 -> 11; matrix products, arithmetic and copies ran while one was open for 10% -> 6% of each run, Pallas kernels for 9% -> 12%
where the time goes in v4:
time: 76.8 us; the launch traced here: 76.4 us
  waiting for transfers between devices  30.9 us (40%)
  starting transfers between devices  17.5 us (23%)
  Pallas kernels  14.7 us (19%)
  local copies, waits for them, and re-layouts  8.07 us (11%)
  other arithmetic  3.79 us (5%)
  between operations  1.38 us (2%)
    ppermute x16, waiting for transfers between devices, swap(): return lax.ppermute(values, axis_name, [(i, i ^ mask) for i in range(size)])  26 us
    ppermute x16, starting transfers between devices, swap(): return lax.ppermute(values, axis_name, [(i, i ^ mask) for i in range(size)])  11.6 us
    all_to_all x1, starting transfers between devices, per_device(): got = lax.all_to_all(sent, 'dp', split_axis=0, concat_axis=0, tiled=True)  5.91 us
    all_to_all x1, waiting for transfers between devices, per_device(): got = lax.all_to_all(sent, 'dp', split_axis=0, concat_axis=0, tiled=True)  4.88 us
    pallas_call x1, Pallas kernels, head(): pl.pallas_call(functools.partial(head_kernel, groups), out_shape=shapes,...  4.33 us
    unnamed x30, local copies, waits for them, and re-layouts  3.2 us
    pallas_call x1, Pallas kernels, backward(): pl.pallas_call(back_kernel, out_shape=jax.ShapeDtypeStruct((windows.shape...  3.12 us
    pallas_call x1, Pallas kernels, split(): pl.pallas_call(functools.partial(split_kernel, groups), out_shape=shapes,...  2.05 us
  transfers between devices with their start and end apart: 17, of which 11 were waited for; matrix products, arithmetic and copies ran while one was open for 6% of the time, Pallas kernels for 12%

profile of v4, /device:TPU:0, one launch (start us, length us, event | category | flops | bytes accessed | tf_op | source)
XLA Modules:
  0.0 76.4 jit_solution(18121559502169962099)
XLA Ops:
  0.6 1.7 %shard_map.161 = (f32[16,1,640]{2,1,0:T(1,128)}, bf16[384,512]{1,0:T(8,128)(2,1)S(1)}) custom-call(s32[8]{0:T(128)} %owners_in.1, s32[8]{0:T(128)} %lengths_in.1, f32[8,400]{1,0:T(8,128)} %waveform_in.1, bf16[768,512]{1,0:T(8,128)(2,1)} %refs_0_.1), custom_call_target="tpu_custom_call" | custom-call | tf_op jit(solution)/shard_map/pallas_call | solution.py:142
  2.3 3.1 %collective-permute-start = (bf16[384,512]{1,0:T(8,128)(2,1)S(1)}, bf16[384,512]{1,0:T(8,128)(2,1)S(1)}, u32[]{:S(2)}, u32[]{:S(2)}) collective-permute-start(bf16[384,512]{1,0:T(8,128)(2,1)S(1)} %get-tuple-element.39), channel_id=1, source_target_pairs={{0,1},{1,0},{2,3},{3,2},{4,5},{5,4},{6,7},{7,6},{8,9},{9,8},{10,11... | collective-permute-start | bytes 1179656 | tf_op jit(solution)/shard_map/ppermute | solution.py:25
  5.4 5.9 %all-to-all-start = ((f32[16,1,640]{2,1,0:T(1,128)}), f32[16,1,640]{2,1,0:T(1,128)S(1)}, u32[]{:S(2)}, u32[]{:S(2)}) async-start(f32[16,1,640]{2,1,0:T(1,128)} %get-tuple-element.38), calls=%async_computation | async-start | bytes 81920 | tf_op jit(solution)/shard_map/all_to_all | solution.py:525
  11.3 0.8 %copy.83 = f32[39,8]{1,0:T(8,128)S(1)} copy(f32[39,8]{0,1:T(8,128)} %bitcast.122) | data formatting | bytes 2496 | tf_op jit(solution)/shard_map/transpose | solution.py:569
  12.2 0.8 %stack.45.vectors.refs_5_ = f32[8,512]{1,0:T(8,128)S(1)} concatenate(f32[1,512]{1,0:T(1,128)} %bitcast.100, f32[1,512]{1,0:T(1,128)} %bitcast.102, f32[1,512]{1,0:T(1,128)} %bitcast.104, f32[1,512]{1,0:T(1,128)} %bitcast.106, f32[1,512]{1,0:T(1,128)} %bitcast.101, f32[1,512]{1,0:T(1,128)} %bitcast.103, f32[1,512]{1,0:T(1,128)} %bitcast.105, f32[1,512]{1,0:T(1,128)} %bitcast.107), dimensions={0} | concatenate | bytes 32768 | tf_op jit(solution)/shard_map/stack | solution.py:517
  13.1 4.9 %all-to-all-done = f32[16,1,640]{2,1,0:T(1,128)S(1)} async-done(((f32[16,1,640]{2,1,0:T(1,128)}), f32[16,1,640]{2,1,0:T(1,128)S(1)}, u32[]{:S(2)}, u32[]{:S(2)}) %all-to-all-start) | async-done | bytes 40992 | tf_op jit(solution)/shard_map/all_to_all | solution.py:525
  21.4 1.6 %shard_map.162.act.own_act = bf16[632,512]{1,0:T(8,128)(2,1)S(1)} custom-call(f32[632,10]{1,0:T(8,128)S(1)} %copy.82.windows, f32[10,512]{1,0:T(8,128)S(1)} %copy-done.5, f32[8,512]{1,0:T(8,128)S(1)} %stack.45.vectors.refs_5_), custom_call_target="tpu_custom_call" | custom-call | tf_op jit(solution)/shard_map/pallas_call | solution.py:190
  23.4 0.7 copy-done.8
  24.2 4.3 %shard_map.163 = (bf16[1536,512]{1,0:T(8,128)(2,1)}, bf16[320,512]{1,0:T(8,128)(2,1)S(1)}, f32[312,1]{1,0:T(8,128)}, f32[16,512]{1,0:T(8,128)S(1)}, bf16[328,256]{1,0:T(8,128)(2,1)}) custom-call(s32[2]{0:T(128)S(1)} %pad_add_fusion.place, bf16[632,512]{1,0:T(8,128)(2,1)S(1)} %shard_map.162.act.own_act, bf16[768,512]{1,0:T(8,128)(2,1)} %refs_0_.1, ...), custom_call_target="tpu_custom_call" | custom-call | tf_op jit(solution)/shard_map/pallas_call | solution.py:356
  28.5 0.6 copy-done.3
  29.5 1.3 %collective-permute-done.3.received = bf16[328,256]{1,0:T(8,128)(2,1)} collective-permute-done((bf16[328,256]{1,0:T(8,128)(2,1)}, bf16[328,256]{1,0:T(8,128)(2,1)}, u32[]{:S(2)}, u32[]{:S(2)}) %collective-permute-start.3) | collective-permute-done | bytes 167968 | tf_op jit(solution)/shard_map/ppermute | solution.py:25
  30.9 0.8 copy-done.4
  31.6 2.0 %shard_map.164 = (bf16[776,128]{1,0:T(8,128)(2,1)S(1)}, f32[768,128]{1,0:T(8,128)S(1)}, bf16[776,128]{1,0:T(8,128)(2,1)S(1)}, f32[768,128]{1,0:T(8,128)S(1)}, f32[8,256]{1,0:T(8,128)S(1)}) custom-call(s32[3]{0:T(128)S(1)} %pad_add_fusion.1.place, bf16[632,512]{1,0:T(8,128)(2,1)S(1)} %shard_map.162.act.own_act, ...), custom_call_target="tpu_custom_call" | custom-call | tf_op jit(solution)/shard_map/pallas_call | solution.py:442
  34.5 3.1 %shard_map.165 = f32[16,512]{1,0:T(8,128)S(1)} custom-call(f32[632,10]{1,0:T(8,128)S(1)} %copy.82.windows, f32[10,632]{1,0:T(8,128)S(1)} %bitcast.76, f32[10,512]{1,0:T(8,128)S(1)} %copy-done.6, f32[8,512]{1,0:T(8,128)S(1)} %stack.45.vectors.refs_5_, bf16[1536,512]{1,0:T(8,128)(2,1)S(1)} %copy-done, bf16[320,512]{1,0:T(8,128)(2,1)S(1)} %get-tuple-element.55.own_grad.padded, ...), custom_call_target="tpu_custom_call" | custom-call | tf_op jit(solution)/shard_map/pallas_call | solution.py:242
  37.8 3.2 %collective-permute-done.5 = bf16[776,128]{1,0:T(8,128)(2,1)S(1)} collective-permute-done((bf16[776,128]{1,0:T(8,128)(2,1)S(1)}, bf16[776,128]{1,0:T(8,128)(2,1)S(1)}, u32[]{:S(2)}, u32[]{:S(2)}) %collective-permute-start.5) | collective-permute-done | bytes 198688 | tf_op jit(solution)/shard_map/ppermute | solution.py:25
  41.4 0.6 collective-permute-start.6
  42.0 1.7 %collective-permute-start.7 = (f16[392,128]{1,0:T(8,128)(2,1)S(1)}, f16[392,128]{1,0:T(8,128)(2,1)S(1)}, u32[]{:S(2)}, u32[]{:S(2)}) collective-permute-start(f16[392,128]{1,0:T(8,128)(2,1)S(1)} %pad_maximum_fusion.6), channel_id=1, source_target_pairs={{0,4},{2,6},{4,0},{6,2},{8,12},{10,14},{12,8},{14,10},{16,20},{18,... | collective-permute-start | bytes 301064 | tf_op jit(solution)/shard_map/ppermute | solution.py:25
  43.6 3.0 %collective-permute-done.7 = f16[392,128]{1,0:T(8,128)(2,1)S(1)} collective-permute-done((f16[392,128]{1,0:T(8,128)(2,1)S(1)}, f16[392,128]{1,0:T(8,128)(2,1)S(1)}, u32[]{:S(2)}, u32[]{:S(2)}) %collective-permute-start.7) | collective-permute-done | bytes 100384 | tf_op jit(solution)/shard_map/ppermute | solution.py:25
  47.1 0.6 collective-permute-start.8
  47.7 4.4 %collective-permute-done.8 = f16[264,256]{1,0:T(8,128)(2,1)S(1)} collective-permute-done((f16[264,256]{1,0:T(8,128)(2,1)S(1)}, f16[264,256]{1,0:T(8,128)(2,1)S(1)}, u32[]{:S(2)}, u32[]{:S(2)}) %collective-permute-start.8) | collective-permute-done | bytes 135200 | tf_op jit(solution)/shard_map/ppermute | solution.py:25
  52.5 1.8 %collective-permute-start.9 = (f16[264,256]{1,0:T(8,128)(2,1)S(1)}, f16[264,256]{1,0:T(8,128)(2,1)S(1)}, u32[]{:S(2)}, u32[]{:S(2)}) collective-permute-start(f16[264,256]{1,0:T(8,128)(2,1)S(1)} %pad_maximum_fusion.2), channel_id=1, source_target_pairs={{0,16},{2,18},{4,20},{6,22},{8,24},{10,26},{12,28},{14,30},{16,0},... | collective-permute-start | bytes 405512 | tf_op jit(solution)/shard_map/ppermute | solution.py:25
  54.5 0.7 copy.89
  55.2 4.7 %collective-permute-done.9 = f16[264,256]{1,0:T(8,128)(2,1)S(1)} collective-permute-done((f16[264,256]{1,0:T(8,128)(2,1)S(1)}, f16[264,256]{1,0:T(8,128)(2,1)S(1)}, u32[]{:S(2)}, u32[]{:S(2)}) %collective-permute-start.9) | collective-permute-done | bytes 135200 | tf_op jit(solution)/shard_map/ppermute | solution.py:25
  60.2 1.8 %collective-permute-start.10 = (f16[272,256]{1,0:T(8,128)(2,1)S(1)}, f16[272,256]{1,0:T(8,128)(2,1)S(1)}, u32[]{:S(2)}, u32[]{:S(2)}) collective-permute-start(f16[272,256]{1,0:T(8,128)(2,1)S(1)} %get-tuple-element.118), channel_id=1, source_target_pairs={{0,4},{2,6},{4,0},{6,2},{8,12},{10,14},{12,8},{14,10},{16,20},{18,... | collective-permute-start | bytes 417800 | tf_op jit(solution)/shard_map/ppermute | solution.py:25
  62.1 4.6 %collective-permute-done.11 = f16[200,256]{1,0:T(8,128)(2,1)S(1)} collective-permute-done((f16[200,256]{1,0:T(8,128)(2,1)S(1)}, f16[200,256]{1,0:T(8,128)(2,1)S(1)}, u32[]{:S(2)}, u32[]{:S(2)}) %collective-permute-start.11) | collective-permute-done | bytes 102432 | tf_op jit(solution)/shard_map/ppermute | solution.py:25
  67.8 3.2 %collective-permute-done.13 = f16[96,256]{1,0:T(8,128)(2,1)S(1)} collective-permute-done((f16[96,256]{1,0:T(8,128)(2,1)S(1)}, f16[96,256]{1,0:T(8,128)(2,1)S(1)}, u32[]{:S(2)}, u32[]{:S(2)}) %collective-permute-start.13) | collective-permute-done | bytes 49184 | tf_op jit(solution)/shard_map/ppermute | solution.py:25
  70.9 0.8 %collective-permute-done.14 = f16[104,256]{1,0:T(8,128)(2,1)S(1)} collective-permute-done((f16[104,256]{1,0:T(8,128)(2,1)S(1)}, f16[104,256]{1,0:T(8,128)(2,1)S(1)}, u32[]{:S(2)}, u32[]{:S(2)}) %collective-permute-start.14) | collective-permute-done | bytes 53280 | tf_op jit(solution)/shard_map/ppermute | solution.py:25
  71.9 0.6 pad_maximum_fusion.9
  73.2 1.1 %shard_map.166.refs_0_ = f32[768,512]{1,0:T(8,128)} custom-call(f32[576,256]{1,0:T(8,128)S(1)} %bitcast.74, f32[576,256]{1,0:T(8,128)S(1)} %bitcast.75), custom_call_target="tpu_custom_call" | custom-call | tf_op jit(solution)/shard_map/pallas_call | solution.py:479
  74.4 0.6 pad_maximum_fusion.10
  75.0 0.7 collective-permute-done.15
  75.7 0.8 %shard_map.167 = f32[768,512]{1,0:T(8,128)} custom-call(f32[768,512]{1,0:T(8,128)} %shard_map.166.refs_0_, f32[192,256]{1,0:T(8,128)S(1)} %multiply_bitcast_fusion.1.refs_1_, f32[192,256]{1,0:T(8,128)S(1)} %multiply_bitcast_fusion.refs_2_), custom_call_target="tpu_custom_call", output_to_operand_aliasing={{}: (0, {})} | custom-call | tf_op jit(solution)/shard_map/pallas_call | solution.py:479
  (158 shorter events, 8.6 us)
Async XLA Ops:
  2.3 15.7 %collective-permute-start = (bf16[384,512]{1,0:T(8,128)(2,1)S(1)}, bf16[384,512]{1,0:T(8,128)(2,1)S(1)}, u32[]{:S(2)}, u32[]{:S(2)}) collective-permute-start(bf16[384,512]{1,0:T(8,128)(2,1)S(1)} %get-tuple-element.39), channel_id=1, source_target_pairs={{0,1},{1,0},{2,3},{3,2},{4,5},{5,4},{6,7},{7,6},{8,9},{9,8},{10,11... | collective-permute-start | bytes 1179656 | tf_op jit(solution)/shard_map/ppermute | solution.py:25
  5.4 12.6 %all-to-all-start = ((f32[16,1,640]{2,1,0:T(1,128)}), f32[16,1,640]{2,1,0:T(1,128)S(1)}, u32[]{:S(2)}, u32[]{:S(2)}) async-start(f32[16,1,640]{2,1,0:T(1,128)} %get-tuple-element.38), calls=%async_computation | async-start | bytes 81920 | tf_op jit(solution)/shard_map/all_to_all | solution.py:525
  18.0 2.9 %copy-start.7 = (bf16[384,512]{1,0:T(8,128)(2,1)}, bf16[384,512]{1,0:T(8,128)(2,1)S(1)}, u32[]{:S(2)}) copy-start(bf16[384,512]{1,0:T(8,128)(2,1)S(1)} %collective-permute-done.refs_1_) | copy-start | bytes 1179652
  19.0 2.4 %copy-start.5 = (f32[10,512]{1,0:T(8,128)S(1)}, f32[10,512]{1,0:T(8,128)}, u32[]{:S(2)}) copy-start(f32[10,512]{1,0:T(8,128)} %first_weight.1) | copy-start | bytes 61444
  20.7 0.6 copy-start.1
  20.9 2.5 %collective-permute-start.1 = (bf16[384,512]{1,0:T(8,128)(2,1)S(1)}, bf16[384,512]{1,0:T(8,128)(2,1)S(1)}, u32[]{:S(2)}, u32[]{:S(2)}) collective-permute-start(bf16[384,512]{1,0:T(8,128)(2,1)S(1)} %collective-permute-done.refs_1_), channel_id=1, source_target_pairs={{0,2},{2,0},{4,6},{6,4},{8,10},{10,8},{12,14},{14,12},{16,18},{18,... | collective-permute-start | bytes 1179656 | tf_op jit(solution)/shard_map/ppermute | solution.py:25
  23.0 7.8 %collective-permute-start.2 = (bf16[632,512]{1,0:T(8,128)(2,1)S(1)}, bf16[632,512]{1,0:T(8,128)(2,1)S(1)}, u32[]{:S(2)}, u32[]{:S(2)}) collective-permute-start(bf16[632,512]{1,0:T(8,128)(2,1)S(1)} %shard_map.162.act.own_act), channel_id=1, source_target_pairs={{0,2},{2,0},{4,6},{6,4},{8,10},{10,8},{12,14},{14,12},{16,18},{18,... | collective-permute-start | bytes 1941512 | tf_op jit(solution)/shard_map/ppermute | solution.py:25
  23.4 0.8 copy-start.8
  28.5 0.6 copy-start.3
  29.1 5.4 %copy-start = (bf16[1536,512]{1,0:T(8,128)(2,1)S(1)}, bf16[1536,512]{1,0:T(8,128)(2,1)}, u32[]{:S(2)}) copy-start(bf16[1536,512]{1,0:T(8,128)(2,1)} %get-tuple-element.54.weight) | copy-start | bytes 4718596
  29.1 1.7 %collective-permute-start.3 = (bf16[328,256]{1,0:T(8,128)(2,1)}, bf16[328,256]{1,0:T(8,128)(2,1)}, u32[]{:S(2)}, u32[]{:S(2)}) collective-permute-start(bf16[328,256]{1,0:T(8,128)(2,1)} %get-tuple-element.45), channel_id=1, source_target_pairs={{0,2},{2,0},{4,6},{6,4},{8,10},{10,8},{12,14},{14,12},{16,18},{18,... | collective-permute-start | bytes 503816 | tf_op jit(solution)/shard_map/ppermute | solution.py:25
  29.4 5.1 %copy-start.2 = (f32[632,10]{0,1:T(8,128)S(1)}, f32[632,10]{0,1:T(8,128)}, u32[]{:S(2)}) copy-start(f32[632,10]{0,1:T(8,128)} %copy-done.1) | copy-start | bytes 75844
  30.9 0.8 copy-start.4
  31.6 2.9 %copy-start.6 = (f32[10,512]{1,0:T(8,128)S(1)}, f32[10,512]{1,0:T(8,128)}, u32[]{:S(2)}) copy-start(f32[10,512]{1,0:T(8,128)} %first_weight.1) | copy-start | bytes 61444
  33.7 7.2 %collective-permute-start.5 = (bf16[776,128]{1,0:T(8,128)(2,1)S(1)}, bf16[776,128]{1,0:T(8,128)(2,1)S(1)}, u32[]{:S(2)}, u32[]{:S(2)}) collective-permute-start(bf16[776,128]{1,0:T(8,128)(2,1)S(1)} %get-tuple-element.53), channel_id=1, source_target_pairs={{0,4},{2,6},{4,0},{6,2},{8,12},{10,14},{12,8},{14,10},{16,20},{18,... | collective-permute-start | bytes 595976 | tf_op jit(solution)/shard_map/ppermute | solution.py:25
  34.0 7.0 %collective-permute-start.4 = (bf16[776,128]{1,0:T(8,128)(2,1)S(1)}, bf16[776,128]{1,0:T(8,128)(2,1)S(1)}, u32[]{:S(2)}, u32[]{:S(2)}) collective-permute-start(bf16[776,128]{1,0:T(8,128)(2,1)S(1)} %get-tuple-element.50), channel_id=1, source_target_pairs={{0,1},{1,0},{2,3},{3,2},{4,5},{5,4},{6,7},{7,6},{8,9},{9,8},{10,11... | collective-permute-start | bytes 595976 | tf_op jit(solution)/shard_map/ppermute | solution.py:25
  41.4 5.3 %collective-permute-start.6 = (f16[520,128]{1,0:T(8,128)(2,1)S(1)}, f16[520,128]{1,0:T(8,128)(2,1)S(1)}, u32[]{:S(2)}, u32[]{:S(2)}) collective-permute-start(f16[520,128]{1,0:T(8,128)(2,1)S(1)} %pad_maximum_fusion.3), channel_id=1, source_target_pairs={{0,1},{1,0},{2,3},{3,2},{4,5},{5,4},{6,7},{7,6},{8,9},{9,8},{10,11... | collective-permute-start | bytes 399368 | tf_op jit(solution)/shard_map/ppermute | solution.py:25
  42.0 4.6 %collective-permute-start.7 = (f16[392,128]{1,0:T(8,128)(2,1)S(1)}, f16[392,128]{1,0:T(8,128)(2,1)S(1)}, u32[]{:S(2)}, u32[]{:S(2)}) collective-permute-start(f16[392,128]{1,0:T(8,128)(2,1)S(1)} %pad_maximum_fusion.6), channel_id=1, source_target_pairs={{0,4},{2,6},{4,0},{6,2},{8,12},{10,14},{12,8},{14,10},{16,20},{18,... | collective-permute-start | bytes 301064 | tf_op jit(solution)/shard_map/ppermute | solution.py:25
  46.7 7.6 %copy-start.9 = (f32[312,1]{1,0:T(8,128)S(1)}, f32[312,1]{1,0:T(8,128)}, u32[]{:S(2)}) copy-start(f32[312,1]{1,0:T(8,128)} %get-tuple-element.43) | copy-start | bytes 3748
  47.1 5.1 %collective-permute-start.8 = (f16[264,256]{1,0:T(8,128)(2,1)S(1)}, f16[264,256]{1,0:T(8,128)(2,1)S(1)}, u32[]{:S(2)}, u32[]{:S(2)}) collective-permute-start(f16[264,256]{1,0:T(8,128)(2,1)S(1)} %pad_maximum_fusion.1), channel_id=1, source_target_pairs={{0,8},{2,10},{4,12},{6,14},{8,0},{10,2},{12,4},{14,6},{16,24},{18,... | collective-permute-start | bytes 405512 | tf_op jit(solution)/shard_map/ppermute | solution.py:25
  52.5 7.4 %collective-permute-start.9 = (f16[264,256]{1,0:T(8,128)(2,1)S(1)}, f16[264,256]{1,0:T(8,128)(2,1)S(1)}, u32[]{:S(2)}, u32[]{:S(2)}) collective-permute-start(f16[264,256]{1,0:T(8,128)(2,1)S(1)} %pad_maximum_fusion.2), channel_id=1, source_target_pairs={{0,16},{2,18},{4,20},{6,22},{8,24},{10,26},{12,28},{14,30},{16,0},... | collective-permute-start | bytes 405512 | tf_op jit(solution)/shard_map/ppermute | solution.py:25
  60.2 7.0 %collective-permute-start.10 = (f16[272,256]{1,0:T(8,128)(2,1)S(1)}, f16[272,256]{1,0:T(8,128)(2,1)S(1)}, u32[]{:S(2)}, u32[]{:S(2)}) collective-permute-start(f16[272,256]{1,0:T(8,128)(2,1)S(1)} %get-tuple-element.118), channel_id=1, source_target_pairs={{0,4},{2,6},{4,0},{6,2},{8,12},{10,14},{12,8},{14,10},{16,20},{18,... | collective-permute-start | bytes 417800 | tf_op jit(solution)/shard_map/ppermute | solution.py:25
  62.0 4.7 %collective-permute-start.11 = (f16[200,256]{1,0:T(8,128)(2,1)S(1)}, f16[200,256]{1,0:T(8,128)(2,1)S(1)}, u32[]{:S(2)}, u32[]{:S(2)}) collective-permute-start(f16[200,256]{1,0:T(8,128)(2,1)S(1)} %pad_maximum_fusion.4), channel_id=1, source_target_pairs={{0,8},{2,10},{4,12},{6,14},{8,0},{10,2},{12,4},{14,6},{16,24},{18,... | collective-permute-start | bytes 307208 | tf_op jit(solution)/shard_map/ppermute | solution.py:25
  66.8 4.2 %collective-permute-start.13 = (f16[96,256]{1,0:T(8,128)(2,1)S(1)}, f16[96,256]{1,0:T(8,128)(2,1)S(1)}, u32[]{:S(2)}, u32[]{:S(2)}) collective-permute-start(f16[96,256]{1,0:T(8,128)(2,1)S(1)} %slice.534), channel_id=1, source_target_pairs={{0,4},{2,6},{4,0},{6,2},{8,12},{10,14},{12,8},{14,10},{16,20},{18,... | collective-permute-start | bytes 147464 | tf_op jit(solution)/shard_map/ppermute | solution.py:25
  67.4 4.4 %collective-permute-start.12 = (f16[672,256]{1,0:T(8,128)(2,1)S(1)}, f16[672,256]{1,0:T(8,128)(2,1)S(1)}, u32[]{:S(2)}, u32[]{:S(2)}) collective-permute-start(f16[672,256]{1,0:T(8,128)(2,1)S(1)} %get-tuple-element.110), channel_id=1, source_target_pairs={{0,2},{2,0},{4,6},{6,4},{8,10},{10,8},{12,14},{14,12},{16,18},{18,... | collective-permute-start | bytes 1032200 | tf_op jit(solution)/shard_map/ppermute | solution.py:25
  67.5 4.3 %collective-permute-start.14 = (f16[104,256]{1,0:T(8,128)(2,1)S(1)}, f16[104,256]{1,0:T(8,128)(2,1)S(1)}, u32[]{:S(2)}, u32[]{:S(2)}) collective-permute-start(f16[104,256]{1,0:T(8,128)(2,1)S(1)} %slice.535), channel_id=1, source_target_pairs={{0,8},{2,10},{4,12},{6,14},{8,0},{10,2},{12,4},{14,6},{16,24},{18,... | collective-permute-start | bytes 159752 | tf_op jit(solution)/shard_map/ppermute | solution.py:25
  74.2 1.4 %collective-permute-start.15 = (f16[200,256]{1,0:T(8,128)(2,1)S(1)}, f16[200,256]{1,0:T(8,128)(2,1)S(1)}, u32[]{:S(2)}, u32[]{:S(2)}) collective-permute-start(f16[200,256]{1,0:T(8,128)(2,1)S(1)} %pad_maximum_fusion.5), channel_id=1, source_target_pairs={{0,2},{2,0},{4,6},{6,4},{8,10},{10,8},{12,14},{14,12},{16,18},{18,... | collective-permute-start | bytes 307208 | tf_op jit(solution)/shard_map/ppermute | solution.py:25
